TPU v7x, 32 devices: a whole 2x2x4 slice. The times are simulated.
32 devices in a mesh: gx: 4 (over z), gy: 4 (over y, x), gz: 2 (over core).
Axes of the slice: x: 2, y: 2, z: 4, core: 2. Of those that a mesh axis runs over, the one named last changes fastest.
Arguments:
- velocity: float32 [3, 64, 64, 256], P(None, 'gx', 'gy', 'gz'), may hold values from -6 to 6
Outputs:
- stress_residual: float32 [6, 2048], P(None, ('gx', 'gy', 'gz'))
- coefficients: float32 [96, 6], replicated
All inputs are finite; a program needn't handle non-finite values.
Results may differ from a plain program's by a relative error of at most 0.0042.
Values may be sent and summed in bfloat16 or wider, within the bound.
No kernel may reach another device: no remote copies, remote signals or barrier semaphores. Data moves between devices by JAX's collectives and lax.ppermute only.
A program may use at most 64 MiB of HBM per device.

v0:
```python
import jax
import jax.numpy as jnp
import numpy as np
from jax import lax
from jax.sharding import PartitionSpec as P

PRECISE = lax.Precision.HIGHEST
INDEX_PAIRS = ((0, 0), (1, 1), (2, 2), (0, 1), (0, 2), (1, 2))
WIDTHS = (3.0, 6.0, 12.0)


def extended(block, sides, width):
    for axis, dim in sides:
        count = lax.axis_size(axis)
        forward = [(i, i + 1) for i in range(count - 1)]
        forward.append((count - 1, 0))
        backward = [(target, source) for source, target in forward]
        low = lax.ppermute(
            lax.slice_in_dim(block, block.shape[dim] - width, None, axis=dim), axis, forward
        )
        high = lax.ppermute(lax.slice_in_dim(block, 0, width, axis=dim), axis, backward)
        block = jnp.concatenate([low, block, high], axis=dim)
    return block


def window_table(combos):
    weights_table = np.zeros((len(combos), 16), np.float32)
    for row_index in range(len(combos)):
        box_width, offset = combos[row_index]
        low_edge = 7.5 + offset - box_width / 2.0
        high_edge = 7.5 + offset + box_width / 2.0
        for cell_index in range(16):
            cell_share = min(cell_index + 0.5, high_edge) - max(cell_index - 0.5, low_edge)
            weights_table[row_index, cell_index] = max(cell_share, 0.0) / box_width
    return weights_table


def velocity_combos():
    return [(box_width, offset) for box_width in WIDTHS for offset in (-2.0, 0.0, 2.0)]


def product_combos():
    return [(3.0, 0.0), (12.0, 0.0)]


def matrix_product(left_matrix, right_matrix):
    return [
        [
            left_matrix[i][0] * right_matrix[0][j]
            + left_matrix[i][1] * right_matrix[1][j]
            + left_matrix[i][2] * right_matrix[2][j]
            for j in range(3)
        ]
        for i in range(3)
    ]


def pick_pairs(matrix):
    return [matrix[i][j] for i, j in INDEX_PAIRS]


def build_rows(box_means, pair_means):
    feature_rows = []
    centre_values = []
    for width_index in range(3):
        middle = 3 * width_index + 1
        scaled = WIDTHS[width_index] ** 2 * 0.25

        def offset_value(component, direction, step_size):
            position_list = [middle, middle, middle]
            position_list[direction] = middle + step_size
            return box_means[component, position_list[0], position_list[1], position_list[2]]

        centre_values.append([box_means[i, middle, middle, middle] for i in range(3)])
        gradient = [
            [(offset_value(i, j, 1) - offset_value(i, j, -1)) * scaled for j in range(3)]
            for i in range(3)
        ]
        strain = [[(gradient[i][j] + gradient[j][i]) * 0.5 for j in range(3)] for i in range(3)]
        spin_part = [[(gradient[i][j] - gradient[j][i]) * 0.5 for j in range(3)] for i in range(3)]
        square_strain = matrix_product(strain, strain)
        first_order = matrix_product(strain, spin_part)
        second_order = matrix_product(spin_part, strain)
        commutator = [[first_order[i][j] - second_order[i][j] for j in range(3)] for i in range(3)]
        spin_square = matrix_product(spin_part, spin_part)
        magnitude = sum((strain[i][j] * strain[i][j] for i in range(3) for j in range(3)))
        feature_rows += (
            pick_pairs(strain)
            + pick_pairs(square_strain)
            + pick_pairs(commutator)
            + pick_pairs(spin_square)
        )
        feature_rows += [magnitude * entry for entry in pick_pairs(strain)]
    small_box = centre_values[0]
    large_box = centre_values[2]
    feature_rows += [
        pair_means[index, 0] - small_box[i] * small_box[j]
        for index, (i, j) in enumerate(INDEX_PAIRS)
    ]
    target_rows = [
        pair_means[index, 1] - large_box[i] * large_box[j]
        for index, (i, j) in enumerate(INDEX_PAIRS)
    ]
    return (jnp.stack(feature_rows), jnp.stack(target_rows))


def solve_fit(gram_matrix, sample_total):
    scales = jnp.sqrt(jnp.diagonal(gram_matrix) / sample_total + 1e-06)
    feature_scale = scales[:96]
    normal = gram_matrix[:96, :96] / (
        sample_total * feature_scale[:, None] * feature_scale[None, :]
    ) + 0.1 * jnp.eye(96, dtype=jnp.float32)
    target_side = gram_matrix[:96, 96:] / (sample_total * feature_scale[:, None])
    factor = jnp.linalg.cholesky(normal)
    solved = jax.scipy.linalg.cho_solve((factor, True), target_side)
    return (solved / feature_scale[:, None], scales[96:])


def axis_weights(length, weights_table):
    sample_count = length // 8
    combo_count = weights_table.shape[0]
    full_table = np.zeros((sample_count * combo_count, length + 8), np.float32)
    for sample_index in range(sample_count):
        full_table[
            sample_index * combo_count : (sample_index + 1) * combo_count,
            8 * sample_index : 8 * sample_index + 16,
        ] = weights_table
    return jnp.asarray(full_table)


def windowed(wide_field, weights_table):
    along_z = jnp.einsum(
        "cxyz,kz->cxyk",
        wide_field,
        axis_weights(wide_field.shape[3] - 8, weights_table),
        precision=PRECISE,
    )
    along_y = jnp.einsum(
        "cxyk,jy->cxjk",
        along_z,
        axis_weights(wide_field.shape[2] - 8, weights_table),
        precision=PRECISE,
    )
    return jnp.einsum(
        "cxjk,ix->cijk",
        along_y,
        axis_weights(wide_field.shape[1] - 8, weights_table),
        precision=PRECISE,
    )


def shards(velocity):
    rounded = velocity.astype(jnp.bfloat16)
    padded = extended(rounded, (("gx", 1), ("gy", 2), ("gz", 3)), 4)
    wide_field = padded.astype(jnp.float32)
    count_x = velocity.shape[1] // 8
    count_y = velocity.shape[2] // 8
    count_z = velocity.shape[3] // 8
    samples = count_x * count_y * count_z
    box_means = windowed(wide_field, window_table(velocity_combos()))
    box_means = box_means.reshape(3, count_x, 9, count_y, 9, count_z, 9)
    box_means = jnp.transpose(box_means, (0, 2, 4, 6, 1, 3, 5)).reshape(3, 9, 9, 9, samples)
    pair_field = jnp.stack([wide_field[i] * wide_field[j] for i, j in INDEX_PAIRS])
    pair_means = windowed(pair_field, window_table(product_combos())).reshape(
        6, count_x, 2, count_y, 2, count_z, 2
    )
    pair_means = jnp.stack(
        [pair_means[:, :, 0, :, 0, :, 0], pair_means[:, :, 1, :, 1, :, 1]], axis=1
    )
    pair_means = pair_means.reshape(6, 2, samples)
    features, targets = build_rows(box_means, pair_means)
    stacked = jnp.concatenate([features, targets], axis=0)
    local_gram = jnp.dot(stacked, stacked.T, precision=PRECISE, preferred_element_type=jnp.float32)
    gram_matrix = lax.psum(local_gram, ("gx", "gy", "gz"))
    sample_total = float(samples * lax.axis_size("gx") * lax.axis_size("gy") * lax.axis_size("gz"))
    coefficients, target_scale = solve_fit(gram_matrix, sample_total)
    predicted = jnp.dot(
        coefficients.T, features, precision=PRECISE, preferred_element_type=jnp.float32
    )
    residual = (targets - predicted) / target_scale[:, None]
    return (residual, coefficients)


def solution(mesh):
    in_specs = (P(None, "gx", "gy", "gz"),)
    out_specs = (P(None, ("gx", "gy", "gz")), P())
    return jax.shard_map(shards, mesh=mesh, in_specs=in_specs, out_specs=out_specs, check_vma=False)
```

profile of v0, /device:TPU:1, one launch (start us, length us, event | category | flops | bytes accessed | tf_op | source)
XLA Modules:
  0.0 116.9 jit_solution(10109509089073360371)
XLA Ops:
  0.6 1.0 convert_element_type.7
  1.7 2.2 %collective-permute-start = (bf16[3,4,16,128]{3,2,1,0:T(8,128)(2,1)S(1)}, bf16[3,4,16,128]{3,2,1,0:T(8,128)(2,1)S(1)}, u32[]{:S(2)}, u32[]{:S(2)}) collective-permute-start(bf16[3,4,16,128]{3,2,1,0:T(8,128)(2,1)S(1)} %get-tuple-element.102), channel_id=1, source_target_pairs={{0,8},{8,16},{16,24},{24,0},{1,9},{9,17},{17,25},{25,1},{2,10},{10... | collective-permute-start | bytes 147464 | tf_op jit(solution)/shard_map/ppermute | solution.py:18
  3.9 2.1 %collective-permute-start.1 = (bf16[3,4,16,128]{3,2,1,0:T(8,128)(2,1)S(1)}, bf16[3,4,16,128]{3,2,1,0:T(8,128)(2,1)S(1)}, u32[]{:S(2)}, u32[]{:S(2)}) collective-permute-start(bf16[3,4,16,128]{3,2,1,0:T(8,128)(2,1)S(1)} %get-tuple-element.103), channel_id=1, source_target_pairs={{8,0},{16,8},{24,16},{0,24},{9,1},{17,9},{25,17},{1,25},{10,2},{18... | collective-permute-start | bytes 147464 | tf_op jit(solution)/shard_map/ppermute | solution.py:21
  5.9 1.4 %collective-permute-done = bf16[3,4,16,128]{3,2,1,0:T(8,128)(2,1)S(1)} collective-permute-done((bf16[3,4,16,128]{3,2,1,0:T(8,128)(2,1)S(1)}, bf16[3,4,16,128]{3,2,1,0:T(8,128)(2,1)S(1)}, u32[]{:S(2)}, u32[]{:S(2)}) %collective-permute-start) | collective-permute-done | bytes 49184 | tf_op jit(solution)/shard_map/ppermute | solution.py:18
  7.4 1.3 %collective-permute-start.2 = (bf16[3,24,4,128]{3,2,1,0:T(4,128)(2,1)S(1)}, bf16[3,24,4,128]{3,2,1,0:T(4,128)(2,1)S(1)}, u32[]{:S(2)}, u32[]{:S(2)}) collective-permute-start(bf16[3,24,4,128]{3,2,1,0:T(4,128)(2,1)S(1)} %get-tuple-element.100), channel_id=1, source_target_pairs={{0,2},{2,4},{4,6},{6,0},{1,3},{3,5},{5,7},{7,1},{8,10},{10,12},{12... | collective-permute-start | bytes 221192 | tf_op jit(solution)/shard_map/ppermute | solution.py:18
  8.7 1.2 collective-permute-start.3
  9.9 1.7 %collective-permute-done.2 = bf16[3,24,4,128]{3,2,1,0:T(4,128)(2,1)S(1)} collective-permute-done((bf16[3,24,4,128]{3,2,1,0:T(4,128)(2,1)S(1)}, bf16[3,24,4,128]{3,2,1,0:T(4,128)(2,1)S(1)}, u32[]{:S(2)}, u32[]{:S(2)}) %collective-permute-start.2) | collective-permute-done | bytes 73760 | tf_op jit(solution)/shard_map/ppermute | solution.py:18
  11.6 0.8 collective-permute-done.3
  12.9 3.3 %collective-permute-start.4 = (bf16[3,24,24,4]{3,2,1,0:T(8,128)(2,1)S(1)}, bf16[3,24,24,4]{3,2,1,0:T(8,128)(2,1)S(1)}, u32[]{:S(2)}, u32[]{:S(2)}) collective-permute-start(bf16[3,24,24,4]{3,2,1,0:T(8,128)(2,1)S(1)} %get-tuple-element.98), channel_id=1, source_target_pairs={{0,1},{1,0},{2,3},{3,2},{4,5},{5,4},{6,7},{7,6},{8,9},{9,8},{10,11... | collective-permute-start | bytes 41480 | tf_op jit(solution)/shard_map/ppermute | solution.py:18
  16.2 1.3 %collective-permute-done.4 = bf16[3,24,24,4]{3,2,1,0:T(8,128)(2,1)S(1)} collective-permute-done((bf16[3,24,24,4]{3,2,1,0:T(8,128)(2,1)S(1)}, bf16[3,24,24,4]{3,2,1,0:T(8,128)(2,1)S(1)}, u32[]{:S(2)}, u32[]{:S(2)}) %collective-permute-start.4) | collective-permute-done | bytes 13856 | tf_op jit(solution)/shard_map/ppermute | solution.py:18
  17.6 0.6 collective-permute-done.5
  18.2 1.3 %fusion.124 = f32[3,24,24,144]{3,2,1,0:T(8,128)S(1)} fusion(f32[144,136,1,1]{0,1,3,2:T(8,128)S(1)} %copy-done.8, bf16[3,24,24,4]{3,2,1,0:T(8,128)(2,1)S(1)} %collective-permute-done.5, bf16[3,24,4,128]{3,2,1,0:T(4,128)(2,1)S(1)} %collective-permute-done.3, bf16[3,4,16,128]{3,2,1,0:T(8,128)(2,1)S(1)} %collective-permute-done.1, ...), kind=kOutput, calls=%fused_computation.402 | convolution fusion | flops 409383936 | bytes 1543680 | tf_op jit(solution)/shard_map/cxyz,kz->cxyk/dot_general | solution.py:132
  19.6 1.6 %convolution_bitcast_fusion = f32[3,24,18,144]{3,2,1,0:T(8,128)S(1)} fusion(f32[3,24,24,144]{3,2,1,0:T(8,128)S(1)} %fusion.124, f32[18,24,1,1]{1,0,3,2:T(8,128)S(1)} %copy-done.4), kind=kOutput, calls=%fused_computation.1 | convolution fusion | flops 53747712 | bytes 1743552 | tf_op jit(solution)/shard_map/cxyk,jy->cxjk/dot_general | solution.py:138
  21.2 1.6 %convolution_bitcast_fusion.1 = f32[3,18,18,144]{3,1,2,0:T(8,128)S(1)} fusion(f32[18,24,1,1]{1,0,3,2:T(8,128)S(1)} %copy-done.4, f32[3,24,18,144]{3,2,1,0:T(8,128)S(1)} %convolution_bitcast_fusion), kind=kOutput, calls=%fused_computation.2 | convolution fusion | flops 40310784 | bytes 1308096 | tf_op jit(solution)/shard_map/cxjk,ix->cijk/dot_general | solution.py:144
  22.8 0.3 copy.30
  23.1 6.3 %reshape.6592 = f32[3,2,9,2,9,16,9]{6,5,4,3,2,1,0:T(8,128)} reshape(f32[3,18,18,144]{3,2,1,0:T(8,128)S(1)} %copy.30) | data formatting | bytes 1119744 | tf_op jit(solution)/shard_map/reshape | solution.py:161
  29.5 11.0 %copy.31 = f32[3,9,9,9,2,2,16]{6,5,4,0,3,2,1:T(2,128)} copy(f32[3,9,9,9,2,2,16]{3,6,2,5,1,4,0:T(8,128)} %bitcast.897) | data formatting | bytes 1119744 | tf_op jit(solution)/shard_map/transpose | solution.py:162
  40.4 5.8 %reshape.6593 = f32[3,9,9,9,64]{4,0,3,2,1:T(4,128)S(1)} reshape(f32[3,9,9,9,2,2,16]{6,5,4,0,3,2,1:T(2,128)} %copy.31) | data formatting | bytes 1119744 | tf_op jit(solution)/shard_map/reshape | solution.py:162
  46.3 0.8 fusion.125
  47.6 0.6 copy-done.5
  48.1 2.9 %fusion.158 = f32[6,24,24,32]{3,2,1,0:T(8,128)S(1)} fusion(f32[6,24,24,136]{3,2,1,0:T(8,128)S(1)} %multiply_dynamic-update-slice_fusion, f32[32,136,1,1]{1,0,3,2:T(8,128)S(1)} %copy-done.5), kind=kOutput, calls=%fused_computation.409 | convolution fusion | flops 180486144 | bytes 2339840 | tf_op jit(solution)/shard_map/cxyz,kz->cxyk/dot_general | solution.py:132
  51.1 1.0 convolution_bitcast_fusion.2
  52.1 0.3 convolution_bitcast_fusion.3
  52.6 2.0 %slice_reduce_fusion = (f32[2,2,16]{2,1,0:T(2,128)S(1)}, f32[2,2,16]{2,1,0:T(2,128)S(1)}, f32[2,2,16]{2,1,0:T(2,128)S(1)}, f32[2,2,16]{2,1,0:T(2,128)S(1)}, f32[...) fusion(f32[6,2,2,2,2,16,2]{0,6,5,4,3,2,1:T(2,128)S(1)} %bitcast.898), kind=kLoop, calls=%fused_computation.34 | loop fusion | bytes 6144 | tf_op jit(solution)/shard_map/slice | solution.py:97
  56.4 0.3 concatenate.21
  56.9 39.2 %psum.7 = f32[102,102]{1,0:T(8,128)S(1)} all-reduce(f32[102,102]{1,0:T(8,128)S(1)} %fusion.159), channel_id=1, replica_groups=mesh['gx'=4,'gy'=4,'gz'=2] {'gx','gy','gz'}, use_global_device_ids=true, to_apply=%region_0.0 | all-reduce | flops 10404 | bytes 83232 | tf_op jit(solution)/shard_map/psum | solution.py:174
  96.1 1.7 %gather_fusion = f32[102]{0:T(128)S(1)} fusion(f32[102,102]{1,0:T(8,128)S(1)} %psum.7, s32[102]{0:T(128)S(1)} %or_bitcast_fusion), kind=kCustom, calls=%fused_computation | custom fusion | bytes 1632 | tf_op jit(solution)/shard_map/jit(diagonal)/cond/branch_0_fun/gather | solution.py:108
  98.2 8.8 %cholesky.16 = f32[96,96]{1,0:T(8,128)S(1)} custom-call(f32[96,96]{1,0:T(8,128)S(1)} %fusion.8), custom_call_target="Cholesky" | custom-call | tf_op jit(solution)/shard_map/jit(cholesky)/cholesky | solution.py:114
  107.0 0.6 compare_reduce_fusion
  107.6 0.7 fusion.3
  108.3 7.4 %custom-call.10 = f32[1,96,96]{1,2,0:T(8,128)S(1)} custom-call(f32[1,96,96]{2,1,0:T(8,128)S(1)} %fusion.3), custom_call_target="InvertDiagBlocksLowerTriangular" | custom-call | tf_op jit(solution)/shard_map/jit(_cho_solve)/triangular_solve | solution.py:115
  116.1 0.8 fusion.1
  (78 shorter events, 3.9 us)
Async XLA Ops:
  1.7 16.6 %copy-start.8 = (f32[144,136,1,1]{0,1,3,2:T(8,128)S(1)}, f32[144,136,1,1]{0,1,3,2:T(8,128)}, u32[]{:S(2)}) copy-start(f32[144,136,1,1]{0,1,3,2:T(8,128)} %constant.98) | copy-start | bytes 235012
  1.7 5.7 %collective-permute-start = (bf16[3,4,16,128]{3,2,1,0:T(8,128)(2,1)S(1)}, bf16[3,4,16,128]{3,2,1,0:T(8,128)(2,1)S(1)}, u32[]{:S(2)}, u32[]{:S(2)}) collective-permute-start(bf16[3,4,16,128]{3,2,1,0:T(8,128)(2,1)S(1)} %get-tuple-element.102), channel_id=1, source_target_pairs={{0,8},{8,16},{16,24},{24,0},{1,9},{9,17},{17,25},{25,1},{2,10},{10... | collective-permute-start | bytes 147464 | tf_op jit(solution)/shard_map/ppermute | solution.py:18
  3.9 3.5 %collective-permute-start.1 = (bf16[3,4,16,128]{3,2,1,0:T(8,128)(2,1)S(1)}, bf16[3,4,16,128]{3,2,1,0:T(8,128)(2,1)S(1)}, u32[]{:S(2)}, u32[]{:S(2)}) collective-permute-start(bf16[3,4,16,128]{3,2,1,0:T(8,128)(2,1)S(1)} %get-tuple-element.103), channel_id=1, source_target_pairs={{8,0},{16,8},{24,16},{0,24},{9,1},{17,9},{25,17},{1,25},{10,2},{18... | collective-permute-start | bytes 147464 | tf_op jit(solution)/shard_map/ppermute | solution.py:21
  7.4 12.2 %copy-start.2 = (bf16[3,4,16,128]{3,2,1,0:T(8,128)(2,1)}, bf16[3,4,16,128]{3,2,1,0:T(8,128)(2,1)S(1)}, u32[]{:S(2)}) copy-start(bf16[3,4,16,128]{3,2,1,0:T(8,128)(2,1)S(1)} %collective-permute-done.1) | copy-start | bytes 147460
  7.4 4.2 %collective-permute-start.2 = (bf16[3,24,4,128]{3,2,1,0:T(4,128)(2,1)S(1)}, bf16[3,24,4,128]{3,2,1,0:T(4,128)(2,1)S(1)}, u32[]{:S(2)}, u32[]{:S(2)}) collective-permute-start(bf16[3,24,4,128]{3,2,1,0:T(4,128)(2,1)S(1)} %get-tuple-element.100), channel_id=1, source_target_pairs={{0,2},{2,4},{4,6},{6,0},{1,3},{3,5},{5,7},{7,1},{8,10},{10,12},{12... | collective-permute-start | bytes 221192 | tf_op jit(solution)/shard_map/ppermute | solution.py:18
  8.7 3.7 %collective-permute-start.3 = (bf16[3,24,4,128]{3,2,1,0:T(4,128)(2,1)S(1)}, bf16[3,24,4,128]{3,2,1,0:T(4,128)(2,1)S(1)}, u32[]{:S(2)}, u32[]{:S(2)}) collective-permute-start(bf16[3,24,4,128]{3,2,1,0:T(4,128)(2,1)S(1)} %get-tuple-element.101), channel_id=1, source_target_pairs={{2,0},{4,2},{6,4},{0,6},{3,1},{5,3},{7,5},{1,7},{10,8},{12,10},{14... | collective-permute-start | bytes 221192 | tf_op jit(solution)/shard_map/ppermute | solution.py:21
  12.9 4.7 %collective-permute-start.4 = (bf16[3,24,24,4]{3,2,1,0:T(8,128)(2,1)S(1)}, bf16[3,24,24,4]{3,2,1,0:T(8,128)(2,1)S(1)}, u32[]{:S(2)}, u32[]{:S(2)}) collective-permute-start(bf16[3,24,24,4]{3,2,1,0:T(8,128)(2,1)S(1)} %get-tuple-element.98), channel_id=1, source_target_pairs={{0,1},{1,0},{2,3},{3,2},{4,5},{5,4},{6,7},{7,6},{8,9},{9,8},{10,11... | collective-permute-start | bytes 41480 | tf_op jit(solution)/shard_map/ppermute | solution.py:18
  16.2 2.1 %collective-permute-start.5 = (bf16[3,24,24,4]{3,2,1,0:T(8,128)(2,1)S(1)}, bf16[3,24,24,4]{3,2,1,0:T(8,128)(2,1)S(1)}, u32[]{:S(2)}, u32[]{:S(2)}) collective-permute-start(bf16[3,24,24,4]{3,2,1,0:T(8,128)(2,1)S(1)} %get-tuple-element.99), channel_id=1, source_target_pairs={{1,0},{0,1},{3,2},{2,3},{5,4},{4,5},{7,6},{6,7},{9,8},{8,9},{11,10... | collective-permute-start | bytes 41480 | tf_op jit(solution)/shard_map/ppermute | solution.py:21
  16.2 3.3 %copy-start.4 = (f32[18,24,1,1]{1,0,3,2:T(8,128)S(1)}, f32[18,24,1,1]{1,0,3,2:T(8,128)}, u32[]{:S(2)}) copy-start(f32[18,24,1,1]{1,0,3,2:T(8,128)} %constant.99) | copy-start | bytes 5188
  18.2 1.3 %copy-start = (bf16[3,24,24,4]{3,2,1,0:T(8,128)(2,1)}, bf16[3,24,24,4]{3,2,1,0:T(8,128)(2,1)S(1)}, u32[]{:S(2)}) copy-start(bf16[3,24,24,4]{3,2,1,0:T(8,128)(2,1)S(1)} %collective-permute-done.5) | copy-start | bytes 41476
  40.4 5.9 %copy-start.1 = (bf16[3,24,24,4]{3,2,1,0:T(8,128)(2,1)S(1)}, bf16[3,24,24,4]{3,2,1,0:T(8,128)(2,1)}, u32[]{:S(2)}) copy-start(bf16[3,24,24,4]{3,2,1,0:T(8,128)(2,1)} %copy-done) | copy-start | bytes 41476
  40.4 5.9 %copy-start.3 = (bf16[3,4,16,128]{3,2,1,0:T(8,128)(2,1)S(1)}, bf16[3,4,16,128]{3,2,1,0:T(8,128)(2,1)}, u32[]{:S(2)}) copy-start(bf16[3,4,16,128]{3,2,1,0:T(8,128)(2,1)} %copy-done.2) | copy-start | bytes 147460
  47.4 0.8 copy-start.5
  48.1 3.0 %copy-start.6 = (f32[4,24,1,1]{1,0,3,2:T(4,128)S(1)}, f32[4,24,1,1]{1,0,3,2:T(4,128)}, u32[]{:S(2)}) copy-start(f32[4,24,1,1]{1,0,3,2:T(4,128)} %constant.97) | copy-start | bytes 1156
  116.1 0.8 copy-start.7
where the time goes:
time: 119 us; the launch traced here: 117 us
  blocking collectives  39.2 us (33%)
  local copies, waits for them, and re-layouts  29.8 us (25%)
  other arithmetic  20.6 us (17%)
  matrix products  10.3 us (9%)
  starting transfers between devices  10 us (8%)
  waiting for transfers between devices  5.97 us (5%)
    psum x1, blocking collectives, shards(): gram_matrix = lax.psum(local_gram, ('gx', 'gy', 'gz'))  39.2 us
    transpose x1, local copies, waits for them, and re-layouts, shards(): jnp.transpose(box_means, (0, 2, 4, 6, 1, 3, 5)).reshape(3, 9, 9, 9, samples)  11 us
    another operation x3, other arithmetic, solve_fit(): factor = jnp.linalg.cholesky(normal)  9.45 us
    another operation x2, other arithmetic, solve_fit(): solved = jax.scipy.linalg.cho_solve((factor, True), target_side)  8.01 us
    ppermute x3, starting transfers between devices, extended(): lax.ppermute(lax.slice_in_dim(block, block.shape[dim] - width, None, axis...  6.7 us
    reshape x1, local copies, waits for them, and re-layouts, shards(): box_means = box_means.reshape(3, count_x, 9, count_y, 9, count_z, 9)  6.35 us
    reshape x1, local copies, waits for them, and re-layouts, shards(): jnp.transpose(box_means, (0, 2, 4, 6, 1, 3, 5)).reshape(3, 9, 9, 9, samples)  5.76 us
    ppermute x3, waiting for transfers between devices, extended(): lax.ppermute(lax.slice_in_dim(block, block.shape[dim] - width, None, axis...  4.49 us
  transfers between devices with their start and end apart: 6, of which 5 were waited for; matrix products, arithmetic and copies ran while one was open for 0% of the time, Pallas kernels for 0%

commit v1 on v0

--- a/solution.py
+++ b/solution.py
@@ -1,7 +1,11 @@
+import functools
+
 import jax
 import jax.numpy as jnp
 import numpy as np
 from jax import lax
+from jax.experimental import pallas as pl
+from jax.experimental.pallas import tpu as pltpu
 from jax.sharding import PartitionSpec as P
 
 PRECISE = lax.Precision.HIGHEST
@@ -181,7 +185,351 @@
     return (residual, coefficients)
 
 
+WAYS = (0.0, 2.0, -2.0, 0.0, 0.0, 0.0, 0.0)
+YWAYS = (0.0, 0.0, 0.0, 2.0, -2.0, 0.0, 0.0)
+OWN = ((0, 0), (0, 1), (1, 0), (1, 1))
+FACE_LOW = ((-1, -1), (-1, 2), (-1, 0), (-1, 1))
+FACE_HIGH = ((2, 0), (2, 1), (2, -1), (2, 2))
+FACE_Y = ((1, -1), (1, 2), (0, -1), (0, 2))
+
+
+def share(centre, width, cell):
+    part = min(cell + 0.5, centre + width / 2) - max(cell - 0.5, centre - width / 2)
+    return max(part, 0.0)
+
+
+def plane_row(bx, by, width, place, shift):
+    along_x = [share(8 * place[0] + 3.5 + shift[0], width, n) for n in range(bx)]
+    along_y = [share(8 * place[1] + 3.5 + shift[1], width, n) for n in range(by)]
+    return np.outer(along_x, along_y).reshape(-1)
+
+
+def velocity_plane_table(bx, by):
+    rows = []
+
+    def add(place, entries):
+        for entry in entries:
+            if entry is None:
+                rows.append(np.zeros(bx * by))
+            else:
+                rows.append(plane_row(bx, by, entry[0], place, (entry[1], entry[2])))
+
+    centre = (12.0, 0.0, 0.0)
+    for width in WIDTHS:
+        for place in OWN:
+            add(place, [(width, WAYS[q], YWAYS[q]) for q in range(7)] + [None])
+    for places in (FACE_LOW, FACE_HIGH):
+        for place in places:
+            low = places is FACE_LOW
+            first = (12.0 if low else 6.0, 2.0 if low else -2.0, 0.0)
+            second = (6.0 if low else 12.0, 2.0 if low else -2.0, 0.0)
+            if place[1] in (0, 1):
+                third, fourth = (12.0, 0.0, 2.0), (12.0, 0.0, -2.0)
+            else:
+                third, fourth = (12.0, 0.0, 2.0 if place[1] < 0 else -2.0), None
+            add(place, [centre, first, second, third, fourth, centre, centre, None])
+    for place in FACE_Y:
+        step = 2.0 if place[1] < 0 else -2.0
+        add(
+            place,
+            [centre, (12.0, 2.0, 0.0), (12.0, -2.0, 0.0), (12.0, 0.0, step), (6.0, 0.0, step)]
+            + [centre, centre, None],
+        )
+    return np.stack(rows)
+
+
+def pair_plane_table(bx, by):
+    rows = []
+    for width, places in ((3.0, OWN), (12.0, OWN + FACE_LOW + FACE_HIGH + FACE_Y)):
+        for place in places:
+            rows.append(plane_row(bx, by, width, place, (0.0, 0.0)))
+    while len(rows) % 16:
+        rows.append(np.zeros(bx * by))
+    return np.stack(rows)
+
+
+def line_table(length, width, extra):
+    samples = length // 8
+    table = np.zeros((length, 4 * samples))
+    blocks = [(width, 0.0), (width, 2.0), (width, -2.0)] + ([(extra, 0.0)] if extra else [])
+    for block, (box, shift) in enumerate(blocks):
+        for sample in range(samples):
+            for cell in range(length):
+                for turn in (-1, 0, 1):
+                    table[cell, block * samples + sample] += share(
+                        8 * sample + 3.5 + shift, box, cell + turn * length
+                    )
+    return table
+
+
+def three_parts(value):
+    high = value.astype(jnp.bfloat16)
+    rest = value - high.astype(jnp.float32)
+    middle = rest.astype(jnp.bfloat16)
+    low = (rest - middle.astype(jnp.float32)).astype(jnp.bfloat16)
+    return high, middle, low
+
+
+def mxu(left, right):
+    return jnp.dot(left, right, preferred_element_type=jnp.float32)
+
+
+def sums_kernel(x_ref, wv_ref, wp_ref, l3_ref, l6_ref, l12_ref, out_ref, pair_ref):
+    core = lax.axis_index("gz")
+    cells = x_ref.shape[1] * x_ref.shape[2]
+    length = x_ref.shape[3]
+    begin = pl.multiple_of(core * length, length)
+    lines = [ref[pl.ds(begin, length), :] for ref in (l3_ref, l6_ref, l12_ref)]
+    doubled = [jnp.concatenate([line, line], axis=0) for line in lines]
+
+    def along_line(value, which):
+        high, middle, low = three_parts(value)
+        return mxu(jnp.concatenate([high, middle], axis=1), doubled[which]) + mxu(low, lines[which])
+
+    rows = lax.broadcasted_iota(jnp.int32, (8, 128), 0)
+    lanes = lax.broadcasted_iota(jnp.int32, (8, 128), 1) // 32
+
+    def gathered(groups, row_block):
+        total = jnp.zeros((8, 128), jnp.float32)
+        for place in range(4):
+            merged = groups[8 * place : 8 * place + 8]
+            base = merged
+            for row, block in row_block.items():
+                merged = jnp.where(rows == row, pltpu.roll(base, (128 - 32 * block) % 128, 1), merged)
+            if place:
+                merged = pltpu.roll(merged, 32 * place, 1)
+            total = jnp.where(lanes == place, merged, total)
+        return total
+
+    fields = [x_ref[c].reshape(cells, length).astype(jnp.bfloat16) for c in range(3)]
+    ends = {5: 1, 6: 2}
+    faces = ({5: 1, 6: 2, 2: 3}, {5: 1, 6: 2, 1: 3}, {5: 1, 6: 2, 4: 3})
+    for c in range(3):
+        plane = mxu(wv_ref[...], fields[c])
+        for which in range(3):
+            line = along_line(plane[32 * which : 32 * which + 32], which)
+            out_ref[pl.ds((which * 3 + c) * 8, 8), :] = gathered(line, ends)
+        line = along_line(plane[96:192], 2)
+        for face in range(3):
+            out_ref[pl.ds(88 + 32 * face + 8 * c, 8), :] = gathered(
+                line[32 * face : 32 * face + 32], faces[face]
+            )
+    wide = [field.astype(jnp.float32) for field in fields]
+    pair_ref[...] = jnp.zeros(pair_ref.shape, jnp.float32)
+    count = wp_ref.shape[0]
+    weights = jnp.concatenate([wp_ref[...], wp_ref[...]], axis=1)
+    for pair, (i, j) in enumerate(INDEX_PAIRS):
+        product = wide[i] * wide[j]
+        high = product.astype(jnp.bfloat16)
+        low = (product - high.astype(jnp.float32)).astype(jnp.bfloat16)
+        pair_ref[pl.ds(pair, count, stride=8), :] = mxu(
+            weights, jnp.concatenate([high, low], axis=0)
+        )
+    out_ref[pl.ds(72, 8), :] = gathered(along_line(pair_ref[pl.ds(0, 32), :], 0), {})
+    line = along_line(pair_ref[pl.ds(32, 128), :], 2)
+    out_ref[pl.ds(80, 8), :] = gathered(line[0:32], {})
+    for face in range(3):
+        out_ref[pl.ds(112 + 32 * face, 8), :] = gathered(line[32 * face + 32 : 32 * face + 64], {})
+
+
+def features_kernel(f_ref, low_ref, high_ref, next_ref, prev_ref, z_ref, gram_ref, s_ref):
+    rows = lax.broadcasted_iota(jnp.int32, (8, 128), 0)
+    lane = lax.broadcasted_iota(jnp.int32, (8, 128), 1)
+    right = lane >= 64
+    upper = (lane // 32) % 2 == 1
+    keep = jnp.logical_not(((rows == 1) & (lane < 64)) | ((rows == 2) & right))
+    zero = jnp.zeros((8, 128), jnp.float32)
+
+    def along_x(at):
+        return jnp.where(right, low_ref[pl.ds(at, 8), :], high_ref[pl.ds(at, 8), :])
+
+    def along_y(at):
+        after = pltpu.roll(next_ref[pl.ds(at, 8), :], 96, 1)
+        before = pltpu.roll(prev_ref[pl.ds(at, 8), :], 32, 1)
+        return jnp.where(upper, after, before)
+
+    for c in range(3):
+        s_ref[pl.ds(8 * c, 8), :] = f_ref[pl.ds(8 * c, 8), :]
+        ex = along_x(8 * c)
+        ey = along_y(8 * c)
+        six = f_ref[pl.ds(24 + 8 * c, 8), :]
+        six += jnp.where((rows == 1) & right, pltpu.roll(ex, 7, 0), zero)
+        six += jnp.where((rows == 2) & (lane < 64), pltpu.roll(ex, 1, 0), zero)
+        six += jnp.where((rows == 3) & upper, pltpu.roll(ey, 7, 0), zero)
+        six += jnp.where((rows == 4) & jnp.logical_not(upper), ey, zero)
+        s_ref[pl.ds(24 + 8 * c, 8), :] = six
+        twelve = f_ref[pl.ds(48 + 8 * c, 8), :] + jnp.where(keep, ex, zero)
+        twelve += jnp.where((rows < 3) | (rows > 4) | ((rows == 3) & upper), ey, zero)
+        twelve += jnp.where((rows == 4) & jnp.logical_not(upper), pltpu.roll(ey, 1, 0), zero)
+        s_ref[pl.ds(48 + 8 * c, 8), :] = twelve
+    small_pairs = f_ref[pl.ds(72, 8), :] * (1.0 / 27.0)
+    large_pairs = (f_ref[pl.ds(80, 8), :] + along_x(24) + along_y(24)) * (1.0 / 1728.0)
+
+    def mean(c, q):
+        return s_ref[pl.ds(8 * c + q, 3, stride=24), :]
+
+    which = lax.broadcasted_iota(jnp.int32, (3, 128), 0)
+    factor = jnp.where(which == 0, 1.0 / 12.0, jnp.where(which == 1, 1.0 / 24.0, 1.0 / 48.0))
+    grad = [[(mean(i, 1 + 2 * j) - mean(i, 2 + 2 * j)) * factor for j in range(3)] for i in range(3)]
+    strain = [[None] * 3 for _ in range(3)]
+    spin = [[None] * 3 for _ in range(3)]
+    for i in range(3):
+        for j in range(i, 3):
+            strain[i][j] = strain[j][i] = (grad[i][j] + grad[j][i]) * 0.5
+            if i != j:
+                spin[i][j] = (grad[i][j] - grad[j][i]) * 0.5
+                spin[j][i] = (grad[j][i] - grad[i][j]) * 0.5
+
+    def entry(left, right, i, j):
+        terms = [
+            left[i][k] * right[k][j]
+            for k in range(3)
+            if left[i][k] is not None and right[k][j] is not None
+        ]
+        return sum(terms[1:], terms[0])
+
+    magnitude = sum(
+        (strain[i][j] * strain[i][j] for i in range(3) for j in range(3)),
+        jnp.zeros((3, 128), jnp.float32),
+    )
+    columns = [strain[i][j] for i, j in INDEX_PAIRS]
+    columns += [entry(strain, strain, i, j) for i, j in INDEX_PAIRS]
+    columns += [entry(strain, spin, i, j) - entry(spin, strain, i, j) for i, j in INDEX_PAIRS]
+    columns += [entry(spin, spin, i, j) for i, j in INDEX_PAIRS]
+    columns += [magnitude * strain[i][j] for i, j in INDEX_PAIRS]
+    for index, column in enumerate(columns):
+        z_ref[pl.ds(index, 3, stride=30), :] = column
+    z_ref[pl.ds(96, 32), :] = jnp.zeros((32, 128), jnp.float32)
+    for pair, (i, j) in enumerate(INDEX_PAIRS):
+        for base, box, values, width in ((90, 0, small_pairs, 3.0), (96, 48, large_pairs, 12.0)):
+            first = s_ref[pl.ds(box + 8 * i, 1), :] * (1.0 / width**3)
+            second = s_ref[pl.ds(box + 8 * j, 1), :] * (1.0 / width**3)
+            z_ref[pl.ds(base + pair, 1), :] = values[pair : pair + 1] - first * second
+    stacked = z_ref[...]
+    gram_ref[...] = lax.dot_general(
+        stacked[:104],
+        stacked,
+        (((1,), (1,)), ((), ())),
+        precision=PRECISE,
+        preferred_element_type=jnp.float32,
+    )
+
+
+def solve_kernel(total, gram_ref, z_ref, res_ref, coef_ref, p_ref):
+    core = lax.axis_index("gz")
+    count = 12
+    rows = lax.broadcasted_iota(jnp.int32, (8, 128), 0)
+    lane = lax.broadcasted_iota(jnp.int32, (8, 128), 1)
+    block = []
+    for i in range(count):
+        value = gram_ref[pl.ds(8 * i, 8), :]
+        block.append(
+            jnp.where(lane == rows + 8 * i, value + 0.1 * (value + total * 1e-06), value)
+        )
+    for k in range(8 * count):
+        at, row = k // 8, k % 8
+        column = [jnp.broadcast_to(block[i][:, k : k + 1], (8, 128)) for i in range(count)]
+        pivot = jnp.broadcast_to(column[at][row : row + 1, :], (8, 128))
+        line = jnp.broadcast_to(block[at][row : row + 1, :], (8, 128)) / pivot
+        column[at] = column[at] - (rows == row).astype(jnp.float32)
+        for i in range(count):
+            block[i] = block[i] - column[i] * line
+    for i in range(count):
+        coef_ref[pl.ds(8 * i, 8), :] = block[i][:, 96:102]
+    tail = gram_ref[pl.ds(96, 8), :]
+    diag = jnp.sum(jnp.where(lane == rows + 96, tail, 0.0), axis=1, keepdims=True)
+    scale = jnp.sqrt(diag / total + 1e-06)
+    for k in range(6):
+        acc = jnp.zeros((8, 128), jnp.float32)
+        for i in range(count):
+            acc += jnp.broadcast_to(block[i][:, 96 + k : 97 + k], (8, 128)) * z_ref[pl.ds(8 * i, 8), :]
+        p_ref[pl.ds(k, 1), :] = jnp.sum(acc, axis=0, keepdims=True)
+    p_ref[pl.ds(6, 2), :] = jnp.zeros((2, 128), jnp.float32)
+    residual = (z_ref[pl.ds(96, 8), :] - p_ref[...]) / jnp.broadcast_to(scale, (8, 128))
+    picked = jnp.zeros((8, 128), jnp.float32)
+    for place in range(4):
+        even = pltpu.roll(residual, (128 - 16 * place) % 128, 1) if place else residual
+        odd = pltpu.roll(residual, 112 - 16 * place, 1)
+        picked = jnp.where(lane // 16 == place, jnp.where(core == 0, even, odd), picked)
+    res_ref[...] = picked[:6, :64]
+
+
+def moved(value, axis, step):
+    size = lax.axis_size(axis)
+    return lax.ppermute(value, axis, [(i, (i + step) % size) for i in range(size)])
+
+
+def added_up(value, axis):
+    size = lax.axis_size(axis)
+    if size & (size - 1):
+        return lax.psum(value, axis)
+    bit = 1
+    while bit < size:
+        value = value + lax.ppermute(value, axis, [(i, i ^ bit) for i in range(size)])
+        bit *= 2
+    return value
+
+
+def call(kernel, outs, scratch):
+    vmem = pl.BlockSpec(memory_space=pltpu.VMEM)
+
+    def run(*args):
+        return pl.pallas_call(
+            kernel,
+            out_shape=[jax.ShapeDtypeStruct(shape, jnp.float32) for shape in outs],
+            in_specs=[vmem] * len(args),
+            out_specs=[vmem] * len(outs),
+            scratch_shapes=[pltpu.VMEM(shape, jnp.float32) for shape in scratch],
+        )(*args)
+
+    return run
+
+
+def chip_shards(velocity):
+    bx, by, bz = velocity.shape[1:]
+    length = bz * lax.axis_size("gz")
+    low_type = jnp.bfloat16
+    tables = [
+        jnp.asarray(velocity_plane_table(bx, by), low_type),
+        jnp.asarray(pair_plane_table(bx, by), low_type),
+        jnp.asarray(line_table(length, 3.0, None), low_type),
+        jnp.asarray(line_table(length, 6.0, None), low_type),
+        jnp.asarray(line_table(length, 12.0, 6.0), low_type),
+    ]
+    (part,) = call(sums_kernel, [(184, 128)], [(256, 128)])(velocity, *tables)
+    part = part + moved(part, "gz", 1)
+    own, low, high, side = part[:88], part[88:120], part[120:152], part[152:]
+    low = moved(low, "gx", -1)
+    high = moved(high, "gx", 1)
+    left = jnp.arange(128, dtype=jnp.int32)[None, :] < 64
+    side = side + jnp.where(left, low, high)
+    after = moved(side, "gy", -1)
+    before = moved(side, "gy", 1)
+    stacked, gram = call(features_kernel, [(128, 128), (104, 128)], [(72, 128)])(
+        own, low, high, after, before
+    )
+    gram = added_up(added_up(gram, "gy"), "gx")
+    samples = (bx // 8) * (by // 8) * (length // 8)
+    total = float(samples * lax.axis_size("gx") * lax.axis_size("gy"))
+    residual, coefficients = call(
+        functools.partial(solve_kernel, total), [(6, 64), (96, 6)], [(8, 128)]
+    )(gram, stacked)
+    return (residual, coefficients)
+
+
+def chip_form(mesh, velocity):
+    bricks = (velocity.shape[1] // mesh.shape["gx"], velocity.shape[2] // mesh.shape["gy"])
+    return mesh.shape["gz"] == 2 and bricks == (16, 16) and velocity.shape[3] == 256
+
+
 def solution(mesh):
     in_specs = (P(None, "gx", "gy", "gz"),)
     out_specs = (P(None, ("gx", "gy", "gz")), P())
-    return jax.shard_map(shards, mesh=mesh, in_specs=in_specs, out_specs=out_specs, check_vma=False)
+
+    def run(velocity):
+        body = chip_shards if chip_form(mesh, velocity) else shards
+        return jax.shard_map(
+            body, mesh=mesh, in_specs=in_specs, out_specs=out_specs, check_vma=False
+        )(velocity)
+
+    return run

time: 119 us -> 57.4 us (0.48)
  the two profiles are of different devices: /device:TPU:1 before, /device:TPU:0 now
where the time goes in v1:
time: 57.4 us; the launch traced here: 57 us
  Pallas kernels  19.3 us (34%)
  starting transfers between devices  15.8 us (28%)
  waiting for transfers between devices  15.5 us (27%)
  local copies, waits for them, and re-layouts  3.28 us (6%)
  other arithmetic  2.39 us (4%)
  between operations  0.66 us (1%)
    pallas_call x3, Pallas kernels, run(): pl.pallas_call(kernel, out_shape=[jax.ShapeDtypeStruct(shape, jnp.float32...  19.3 us
    ppermute x4, waiting for transfers between devices, added_up(): lax.ppermute(value, axis, [(i, i ^ bit) for i in range(size)])  10.8 us
    ppermute x5, starting transfers between devices, moved(): lax.ppermute(value, axis, [(i, (i + step) % size) for i in range(size)])  8.48 us
    ppermute x4, starting transfers between devices, added_up(): lax.ppermute(value, axis, [(i, i ^ bit) for i in range(size)])  7.37 us
    ppermute x5, waiting for transfers between devices, moved(): lax.ppermute(value, axis, [(i, (i + step) % size) for i in range(size)])  4.71 us
    add x4, other arithmetic, added_up(): value + lax.ppermute(value, axis, [(i, i ^ bit) for i in range(size)])  1.47 us
    pallas_call x1, local copies, waits for them, and re-layouts, run(): pl.pallas_call(kernel, out_shape=[jax.ShapeDtypeStruct(shape, jnp.float32...  1.46 us
    unnamed x8, local copies, waits for them, and re-layouts  1.19 us
  transfers between devices with their start and end apart: 9, of which 9 were waited for; matrix products, arithmetic and copies ran while one was open for 1% of the time, Pallas kernels for 0%

profile of v1, /device:TPU:0, one launch (start us, length us, event | category | flops | bytes accessed | tf_op | source)
XLA Modules:
  0.0 57.0 jit_solution(9034172136074003316)
XLA Ops:
  0.6 2.8 %shard_map.77 = f32[184,128]{1,0:T(8,128)} custom-call(f32[3,16,16,128]{3,2,1,0:T(8,128)} %x_ref.1, bf16[192,256]{1,0:T(8,128)(2,1)} %constant.12.clone.wv_ref, bf16[32,256]{1,0:T(8,128)(2,1)} %constant.13.clone.wp_ref, bf16[256,128]{1,0:T(8,128)(2,1)} %constant.14.clone.l3_ref, bf16[256,128]{1,0:T(8,128)(2,1)} %constant.15.clone.l6_ref, ...), custom_call_target="tpu_custom_call" | custom-call | tf_op jit(solution)/shard_map/pallas_call | solution.py:477
  3.5 0.5 collective-permute-start
  4.0 1.1 %collective-permute-done = f32[184,128]{1,0:T(8,128)S(1)} collective-permute-done((f32[184,128]{1,0:T(8,128)}, f32[184,128]{1,0:T(8,128)S(1)}, u32[]{:S(2)}, u32[]{:S(2)}) %collective-permute-start) | collective-permute-done | bytes 94240 | tf_op jit(solution)/shard_map/ppermute | solution.py:459
  5.1 0.9 %add.18 = f32[184,128]{1,0:T(8,128)S(1)} add(f32[184,128]{1,0:T(8,128)} %shard_map.77, f32[184,128]{1,0:T(8,128)S(1)} %collective-permute-done) | non-fusion elementwise | flops 23552 | bytes 282624 | tf_op jit(solution)/shard_map/add | solution.py:500
  6.0 3.0 %collective-permute-start.2 = (f32[32,128]{1,0:T(8,128)S(1)}, f32[32,128]{1,0:T(8,128)S(1)}, u32[]{:S(2)}, u32[]{:S(2)}) collective-permute-start(f32[32,128]{1,0:T(8,128)S(1)} %get-tuple-element.8), channel_id=1, source_target_pairs={{0,8},{8,16},{16,24},{24,0},{1,9},{9,17},{17,25},{25,1},{2,10},{10... | collective-permute-start | bytes 49160 | tf_op jit(solution)/shard_map/ppermute | solution.py:459
  9.0 2.1 %collective-permute-start.1 = (f32[32,128]{1,0:T(8,128)S(1)}, f32[32,128]{1,0:T(8,128)S(1)}, u32[]{:S(2)}, u32[]{:S(2)}) collective-permute-start(f32[32,128]{1,0:T(8,128)S(1)} %get-tuple-element.9), channel_id=1, source_target_pairs={{0,24},{8,0},{16,8},{24,16},{1,25},{9,1},{17,9},{25,17},{2,26},{10... | collective-permute-start | bytes 49160 | tf_op jit(solution)/shard_map/ppermute | solution.py:459
  11.1 1.8 %collective-permute-done.2.high_ref = f32[32,128]{1,0:T(8,128)S(1)} collective-permute-done((f32[32,128]{1,0:T(8,128)S(1)}, f32[32,128]{1,0:T(8,128)S(1)}, u32[]{:S(2)}, u32[]{:S(2)}) %collective-permute-start.2) | collective-permute-done | bytes 16416 | tf_op jit(solution)/shard_map/ppermute | solution.py:459
  12.8 0.0 copy-start
  12.8 0.1 collective-permute-done.1.low_ref
  12.9 0.0 copy-start.1
  12.9 0.5 copy-done
  13.4 0.1 copy-done.1
  13.5 1.6 %collective-permute-start.4 = (f32[32,128]{1,0:T(8,128)S(1)}, f32[32,128]{1,0:T(8,128)S(1)}, u32[]{:S(2)}, u32[]{:S(2)}) collective-permute-start(f32[32,128]{1,0:T(8,128)S(1)} %slice_add_fusion), channel_id=1, source_target_pairs={{0,2},{2,4},{4,6},{6,0},{1,3},{3,5},{5,7},{7,1},{8,10},{10,12},{12... | collective-permute-start | bytes 49160 | tf_op jit(solution)/shard_map/ppermute | solution.py:459
  15.1 1.4 %collective-permute-start.3 = (f32[32,128]{1,0:T(8,128)S(1)}, f32[32,128]{1,0:T(8,128)S(1)}, u32[]{:S(2)}, u32[]{:S(2)}) collective-permute-start(f32[32,128]{1,0:T(8,128)S(1)} %slice_add_fusion), channel_id=1, source_target_pairs={{0,6},{2,0},{4,2},{6,4},{1,7},{3,1},{5,3},{7,5},{8,14},{10,8},{12,... | collective-permute-start | bytes 49160 | tf_op jit(solution)/shard_map/ppermute | solution.py:459
  16.4 0.6 %slice.16.f_ref = f32[88,128]{1,0:T(8,128)} slice(f32[184,128]{1,0:T(8,128)S(1)} %add.18), slice={[0:88], [0:128]} | slice | bytes 90112 | tf_op jit(solution)/shard_map/slice | solution.py:501
  17.1 1.1 %collective-permute-done.4.prev_ref = f32[32,128]{1,0:T(8,128)S(1)} collective-permute-done((f32[32,128]{1,0:T(8,128)S(1)}, f32[32,128]{1,0:T(8,128)S(1)}, u32[]{:S(2)}, u32[]{:S(2)}) %collective-permute-start.4) | collective-permute-done | bytes 16416 | tf_op jit(solution)/shard_map/ppermute | solution.py:459
  18.1 0.7 %collective-permute-done.3.next_ref = f32[32,128]{1,0:T(8,128)S(1)} collective-permute-done((f32[32,128]{1,0:T(8,128)S(1)}, f32[32,128]{1,0:T(8,128)S(1)}, u32[]{:S(2)}, u32[]{:S(2)}) %collective-permute-start.3) | collective-permute-done | bytes 16416 | tf_op jit(solution)/shard_map/ppermute | solution.py:459
  18.8 0.0 copy-done.2
  18.8 0.6 %copy-done.3 = f32[32,128]{1,0:T(8,128)} copy-done((f32[32,128]{1,0:T(8,128)}, f32[32,128]{1,0:T(8,128)S(1)}, u32[]{:S(2)}) %copy-start.3) | copy-done | bytes 16408
  19.4 1.8 %shard_map.78 = (f32[128,128]{1,0:T(8,128)}, f32[104,128]{1,0:T(8,128)}) custom-call(f32[88,128]{1,0:T(8,128)} %slice.16.f_ref, f32[32,128]{1,0:T(8,128)} %copy-done.1, f32[32,128]{1,0:T(8,128)} %copy-done, f32[32,128]{1,0:T(8,128)} %copy-done.3, f32[32,128]{1,0:T(8,128)} %copy-done.2), custom_call_target="tpu_custom_call" | custom-call | tf_op jit(solution)/shard_map/pallas_call | solution.py:477
  21.2 2.4 %collective-permute-start.5 = (f32[104,128]{1,0:T(8,128)}, f32[104,128]{1,0:T(8,128)S(1)}, u32[]{:S(2)}, u32[]{:S(2)}) collective-permute-start(f32[104,128]{1,0:T(8,128)} %get-tuple-element.4), channel_id=1, source_target_pairs={{0,2},{2,0},{4,6},{6,4},{1,3},{3,1},{5,7},{7,5},{8,10},{10,8},{12,... | collective-permute-start | bytes 159752 | tf_op jit(solution)/shard_map/ppermute | solution.py:468
  23.6 2.3 %collective-permute-done.5 = f32[104,128]{1,0:T(8,128)S(1)} collective-permute-done((f32[104,128]{1,0:T(8,128)}, f32[104,128]{1,0:T(8,128)S(1)}, u32[]{:S(2)}, u32[]{:S(2)}) %collective-permute-start.5) | collective-permute-done | bytes 53280 | tf_op jit(solution)/shard_map/ppermute | solution.py:468
  25.9 0.8 %add.20 = f32[104,128]{1,0:T(8,128)S(1)} add(f32[104,128]{1,0:T(8,128)} %get-tuple-element.4, f32[104,128]{1,0:T(8,128)S(1)} %collective-permute-done.5) | non-fusion elementwise | flops 13312 | bytes 159744 | tf_op jit(solution)/shard_map/add | solution.py:468
  26.7 1.2 %collective-permute-start.6 = (f32[104,128]{1,0:T(8,128)S(1)}, f32[104,128]{1,0:T(8,128)S(1)}, u32[]{:S(2)}, u32[]{:S(2)}) collective-permute-start(f32[104,128]{1,0:T(8,128)S(1)} %add.20), channel_id=1, source_target_pairs={{0,4},{2,6},{4,0},{6,2},{1,5},{3,7},{5,1},{7,3},{8,12},{10,14},{12... | collective-permute-start | bytes 159752 | tf_op jit(solution)/shard_map/ppermute | solution.py:468
  27.9 3.0 %collective-permute-done.6 = f32[104,128]{1,0:T(8,128)S(1)} collective-permute-done((f32[104,128]{1,0:T(8,128)S(1)}, f32[104,128]{1,0:T(8,128)S(1)}, u32[]{:S(2)}, u32[]{:S(2)}) %collective-permute-start.6) | collective-permute-done | bytes 53280 | tf_op jit(solution)/shard_map/ppermute | solution.py:468
  30.9 1.4 %collective-permute-start.7 = (f32[104,128]{1,0:T(8,128)S(1)}, f32[104,128]{1,0:T(8,128)S(1)}, u32[]{:S(2)}, u32[]{:S(2)}) collective-permute-start(f32[104,128]{1,0:T(8,128)S(1)} %add.21), channel_id=1, source_target_pairs={{0,8},{8,0},{16,24},{24,16},{1,9},{9,1},{17,25},{25,17},{2,10},{10... | collective-permute-start | bytes 159752 | tf_op jit(solution)/shard_map/ppermute | solution.py:468
  32.3 2.8 %collective-permute-done.7 = f32[104,128]{1,0:T(8,128)S(1)} collective-permute-done((f32[104,128]{1,0:T(8,128)S(1)}, f32[104,128]{1,0:T(8,128)S(1)}, u32[]{:S(2)}, u32[]{:S(2)}) %collective-permute-start.7) | collective-permute-done | bytes 53280 | tf_op jit(solution)/shard_map/ppermute | solution.py:468
  35.1 2.4 %collective-permute-start.8 = (f32[104,128]{1,0:T(8,128)S(1)}, f32[104,128]{1,0:T(8,128)S(1)}, u32[]{:S(2)}, u32[]{:S(2)}) collective-permute-start(f32[104,128]{1,0:T(8,128)S(1)} %add.22), channel_id=1, source_target_pairs={{0,16},{8,24},{16,0},{24,8},{1,17},{9,25},{17,1},{25,9},{2,18},{10... | collective-permute-start | bytes 159752 | tf_op jit(solution)/shard_map/ppermute | solution.py:468
  37.5 2.7 %collective-permute-done.8 = f32[104,128]{1,0:T(8,128)S(1)} collective-permute-done((f32[104,128]{1,0:T(8,128)S(1)}, f32[104,128]{1,0:T(8,128)S(1)}, u32[]{:S(2)}, u32[]{:S(2)}) %collective-permute-start.8) | collective-permute-done | bytes 53280 | tf_op jit(solution)/shard_map/ppermute | solution.py:468
  40.2 0.6 %add.23.gram_ref = f32[104,128]{1,0:T(8,128)} add(f32[104,128]{1,0:T(8,128)S(1)} %add.22, f32[104,128]{1,0:T(8,128)S(1)} %collective-permute-done.8) | non-fusion elementwise | flops 13312 | bytes 159744 | tf_op jit(solution)/shard_map/add | solution.py:468
  40.8 14.7 %shard_map.79 = (f32[6,64]{1,0:T(8,128)}, f32[96,6]{1,0:T(8,128)}) custom-call(f32[104,128]{1,0:T(8,128)} %add.23.gram_ref, f32[128,128]{1,0:T(8,128)} %get-tuple-element.5.z_ref), custom_call_target="tpu_custom_call" | custom-call | tf_op jit(solution)/shard_map/pallas_call | solution.py:477
  55.5 1.5 %copy.8 = f32[96,6]{0,1:T(8,128)} copy(f32[96,6]{1,0:T(8,128)} %get-tuple-element.7) | data formatting | bytes 4608 | tf_op jit(solution)/shard_map/pallas_call | solution.py:477
  (7 shorter events, 0.0 us)
Async XLA Ops:
  3.5 1.6 %collective-permute-start = (f32[184,128]{1,0:T(8,128)}, f32[184,128]{1,0:T(8,128)S(1)}, u32[]{:S(2)}, u32[]{:S(2)}) collective-permute-start(f32[184,128]{1,0:T(8,128)} %shard_map.77), channel_id=1, source_target_pairs={{0,1},{1,0},{2,3},{3,2},{4,5},{5,4},{6,7},{7,6},{8,9},{9,8},{10,11... | collective-permute-start | bytes 282632 | tf_op jit(solution)/shard_map/ppermute | solution.py:459
  6.0 6.8 %collective-permute-start.2 = (f32[32,128]{1,0:T(8,128)S(1)}, f32[32,128]{1,0:T(8,128)S(1)}, u32[]{:S(2)}, u32[]{:S(2)}) collective-permute-start(f32[32,128]{1,0:T(8,128)S(1)} %get-tuple-element.8), channel_id=1, source_target_pairs={{0,8},{8,16},{16,24},{24,0},{1,9},{9,17},{17,25},{25,1},{2,10},{10... | collective-permute-start | bytes 49160 | tf_op jit(solution)/shard_map/ppermute | solution.py:459
  9.0 3.9 %collective-permute-start.1 = (f32[32,128]{1,0:T(8,128)S(1)}, f32[32,128]{1,0:T(8,128)S(1)}, u32[]{:S(2)}, u32[]{:S(2)}) collective-permute-start(f32[32,128]{1,0:T(8,128)S(1)} %get-tuple-element.9), channel_id=1, source_target_pairs={{0,24},{8,0},{16,8},{24,16},{1,25},{9,1},{17,9},{25,17},{2,26},{10... | collective-permute-start | bytes 49160 | tf_op jit(solution)/shard_map/ppermute | solution.py:459
  12.8 0.6 %copy-start = (f32[32,128]{1,0:T(8,128)}, f32[32,128]{1,0:T(8,128)S(1)}, u32[]{:S(2)}) copy-start(f32[32,128]{1,0:T(8,128)S(1)} %collective-permute-done.2.high_ref) | copy-start | bytes 49156
  12.9 0.6 %copy-start.1 = (f32[32,128]{1,0:T(8,128)}, f32[32,128]{1,0:T(8,128)S(1)}, u32[]{:S(2)}) copy-start(f32[32,128]{1,0:T(8,128)S(1)} %collective-permute-done.1.low_ref) | copy-start | bytes 49156
  13.5 4.6 %collective-permute-start.4 = (f32[32,128]{1,0:T(8,128)S(1)}, f32[32,128]{1,0:T(8,128)S(1)}, u32[]{:S(2)}, u32[]{:S(2)}) collective-permute-start(f32[32,128]{1,0:T(8,128)S(1)} %slice_add_fusion), channel_id=1, source_target_pairs={{0,2},{2,4},{4,6},{6,0},{1,3},{3,5},{5,7},{7,1},{8,10},{10,12},{12... | collective-permute-start | bytes 49160 | tf_op jit(solution)/shard_map/ppermute | solution.py:459
  15.1 3.7 %collective-permute-start.3 = (f32[32,128]{1,0:T(8,128)S(1)}, f32[32,128]{1,0:T(8,128)S(1)}, u32[]{:S(2)}, u32[]{:S(2)}) collective-permute-start(f32[32,128]{1,0:T(8,128)S(1)} %slice_add_fusion), channel_id=1, source_target_pairs={{0,6},{2,0},{4,2},{6,4},{1,7},{3,1},{5,3},{7,5},{8,14},{10,8},{12,... | collective-permute-start | bytes 49160 | tf_op jit(solution)/shard_map/ppermute | solution.py:459
  18.1 0.7 %copy-start.2 = (f32[32,128]{1,0:T(8,128)}, f32[32,128]{1,0:T(8,128)S(1)}, u32[]{:S(2)}) copy-start(f32[32,128]{1,0:T(8,128)S(1)} %collective-permute-done.4.prev_ref) | copy-start | bytes 49156
  18.8 0.6 %copy-start.3 = (f32[32,128]{1,0:T(8,128)}, f32[32,128]{1,0:T(8,128)S(1)}, u32[]{:S(2)}) copy-start(f32[32,128]{1,0:T(8,128)S(1)} %collective-permute-done.3.next_ref) | copy-start | bytes 49156
  21.2 4.7 %collective-permute-start.5 = (f32[104,128]{1,0:T(8,128)}, f32[104,128]{1,0:T(8,128)S(1)}, u32[]{:S(2)}, u32[]{:S(2)}) collective-permute-start(f32[104,128]{1,0:T(8,128)} %get-tuple-element.4), channel_id=1, source_target_pairs={{0,2},{2,0},{4,6},{6,4},{1,3},{3,1},{5,7},{7,5},{8,10},{10,8},{12,... | collective-permute-start | bytes 159752 | tf_op jit(solution)/shard_map/ppermute | solution.py:468
  26.7 4.1 %collective-permute-start.6 = (f32[104,128]{1,0:T(8,128)S(1)}, f32[104,128]{1,0:T(8,128)S(1)}, u32[]{:S(2)}, u32[]{:S(2)}) collective-permute-start(f32[104,128]{1,0:T(8,128)S(1)} %add.20), channel_id=1, source_target_pairs={{0,4},{2,6},{4,0},{6,2},{1,5},{3,7},{5,1},{7,3},{8,12},{10,14},{12... | collective-permute-start | bytes 159752 | tf_op jit(solution)/shard_map/ppermute | solution.py:468
  30.9 4.2 %collective-permute-start.7 = (f32[104,128]{1,0:T(8,128)S(1)}, f32[104,128]{1,0:T(8,128)S(1)}, u32[]{:S(2)}, u32[]{:S(2)}) collective-permute-start(f32[104,128]{1,0:T(8,128)S(1)} %add.21), channel_id=1, source_target_pairs={{0,8},{8,0},{16,24},{24,16},{1,9},{9,1},{17,25},{25,17},{2,10},{10... | collective-permute-start | bytes 159752 | tf_op jit(solution)/shard_map/ppermute | solution.py:468
  35.1 5.1 %collective-permute-start.8 = (f32[104,128]{1,0:T(8,128)S(1)}, f32[104,128]{1,0:T(8,128)S(1)}, u32[]{:S(2)}, u32[]{:S(2)}) collective-permute-start(f32[104,128]{1,0:T(8,128)S(1)} %add.22), channel_id=1, source_target_pairs={{0,16},{8,24},{16,0},{24,8},{1,17},{9,25},{17,1},{25,9},{2,18},{10... | collective-permute-start | bytes 159752 | tf_op jit(solution)/shard_map/ppermute | solution.py:468

commit v2 on v0

--- a/solution.py
+++ b/solution.py
@@ -1,7 +1,11 @@
+import functools
+
 import jax
 import jax.numpy as jnp
 import numpy as np
 from jax import lax
+from jax.experimental import pallas as pl
+from jax.experimental.pallas import tpu as pltpu
 from jax.sharding import PartitionSpec as P
 
 PRECISE = lax.Precision.HIGHEST
@@ -181,7 +185,413 @@
     return (residual, coefficients)
 
 
+OWN = ((0, 0), (0, 1), (1, 0), (1, 1))
+FACE_LOW = ((-1, -1), (-1, 2), (-1, 0), (-1, 1))
+FACE_HIGH = ((2, 0), (2, 1), (2, -1), (2, 2))
+FACE_Y = ((1, -1), (1, 2), (0, -1), (0, 2))
+ROWS, FACE = 48, 24
+
+
+def share(centre, width, cell):
+    part = min(cell + 0.5, centre + width / 2) - max(cell - 0.5, centre - width / 2)
+    return max(part, 0.0)
+
+
+def window(length, width, sample, difference, turns=(0,)):
+    total = np.zeros(length)
+    for shift, sign in ((2.0, 1.0), (-2.0, -1.0)) if difference else ((0.0, 1.0),):
+        for cell in range(length):
+            for turn in turns:
+                total[cell] += sign * share(
+                    8 * sample + 3.5 + shift, width, cell + turn * length
+                )
+    return total
+
+
+def plane_row(bx, by, place, width, direction):
+    return np.outer(
+        window(bx, width, place[0], direction == 0), window(by, width, place[1], direction == 1)
+    ).reshape(-1)
+
+
+def velocity_plane_table(bx, by):
+    none = np.zeros(bx * by)
+    rows = []
+    for place in OWN:
+        three = [plane_row(bx, by, place, 3.0, k) for k in (0, 1, 2)]
+        six = [plane_row(bx, by, place, 6.0, k) for k in (0, 1, 2)]
+        rows += three + [three[2]] + six + [none]
+    for places in (OWN, FACE_LOW, FACE_HIGH, FACE_Y):
+        for place in places:
+            twelve = [plane_row(bx, by, place, 12.0, k) for k in (0, 1, 2)]
+            along = {FACE_LOW: 0, FACE_HIGH: 0, FACE_Y: 1}.get(places)
+            last = none if along is None else plane_row(bx, by, place, 6.0, along)
+            rows += twelve + [twelve[2], last, none, none, none]
+    return np.stack(rows)
+
+
+def pair_plane_table(bx, by):
+    rows = [plane_row(bx, by, place, 3.0, 2) for place in OWN]
+    for places in (OWN, FACE_LOW, FACE_HIGH, FACE_Y):
+        rows += [plane_row(bx, by, place, 12.0, 2) for place in places]
+    while len(rows) % 16:
+        rows.append(np.zeros(bx * by))
+    return np.stack(rows)
+
+
+def line_table(length, blocks):
+    columns = []
+    for width, difference in blocks:
+        for sample in range(length // 8):
+            if width:
+                columns.append(window(length, width, sample, difference, (-1, 0, 1)))
+            else:
+                columns.append(np.zeros(length))
+    return np.stack(columns, axis=1)
+
+
+def three_parts(value):
+    high = value.astype(jnp.bfloat16)
+    rest = value - high.astype(jnp.float32)
+    middle = rest.astype(jnp.bfloat16)
+    low = (rest - middle.astype(jnp.float32)).astype(jnp.bfloat16)
+    return high, middle, low
+
+
+def mxu(left, right):
+    return jnp.dot(left, right, preferred_element_type=jnp.float32)
+
+
+def sums_kernel(x_hbm, wv_hbm, wp_hbm, la_hbm, lb_hbm, out_ref, x_ref, wv, wp, la, lb, pair_ref, sems):
+    core = lax.axis_index("gz")
+    cells = x_ref.shape[1] * x_ref.shape[2]
+    length = x_ref.shape[3]
+    begin = pl.multiple_of(core * length, length)
+    copies = [pltpu.make_async_copy(wv_hbm, wv, sems.at[0])]
+    copies += [pltpu.make_async_copy(x_hbm.at[c], x_ref.at[c], sems.at[1 + c]) for c in range(3)]
+    copies += [pltpu.make_async_copy(wp_hbm, wp, sems.at[4])]
+    copies += [pltpu.make_async_copy(la_hbm.at[pl.ds(begin, length)], la, sems.at[5])]
+    copies += [pltpu.make_async_copy(lb_hbm.at[pl.ds(begin, length)], lb, sems.at[6])]
+    for copy in copies:
+        copy.start()
+    rows = lax.broadcasted_iota(jnp.int32, (8, 128), 0)
+    lanes = lax.broadcasted_iota(jnp.int32, (8, 128), 1) // 32
+    pair_ref[...] = jnp.zeros(pair_ref.shape, jnp.float32)
+
+    def gathered(groups, blocks):
+        total = jnp.zeros((8, 128), jnp.float32)
+        for place in range(4):
+            base = merged = groups[8 * place : 8 * place + 8]
+            for block, chosen in blocks:
+                hit = rows == chosen[0]
+                for row in chosen[1:]:
+                    hit = hit | (rows == row)
+                merged = jnp.where(hit, pltpu.roll(base, 128 - 32 * block, 1), merged)
+            if place:
+                merged = pltpu.roll(merged, 32 * place, 1)
+            total = jnp.where(lanes == place, merged, total)
+        return total
+
+    for copy in copies:
+        copy.wait()
+    fields = [x_ref[c].reshape(cells, length).astype(jnp.bfloat16) for c in range(3)]
+    planes = [mxu(wv[...], field) for field in fields]
+    wide = [field.astype(jnp.float32) for field in fields]
+    count = wp.shape[0]
+    weights = jnp.concatenate([wp[...], wp[...]], axis=1)
+    for pair, (i, j) in enumerate(INDEX_PAIRS):
+        product = wide[i] * wide[j]
+        high = product.astype(jnp.bfloat16)
+        low = (product - high.astype(jnp.float32)).astype(jnp.bfloat16)
+        pair_ref[pl.ds(pair, count, stride=8), :] = mxu(
+            weights, jnp.concatenate([high, low], axis=0)
+        )
+
+    def along_line(value, line):
+        high, middle, low = three_parts(value)
+        return mxu(
+            jnp.concatenate([high, middle], axis=1), jnp.concatenate([line, line], axis=0)
+        ) + mxu(low, line)
+
+    narrow = along_line(
+        jnp.concatenate([plane[:32] for plane in planes] + [pair_ref[pl.ds(0, 32), :]], axis=0),
+        la[...],
+    )
+    broad = along_line(
+        jnp.concatenate([plane[32:] for plane in planes] + [pair_ref[pl.ds(32, 128), :]], axis=0),
+        lb[...],
+    )
+    for c in range(3):
+        value = gathered(narrow[32 * c : 32 * c + 32], ((1, (2,)), (2, (4, 5)), (3, (6,))))
+        out_ref[pl.ds(27 + 3 * c, 3), :] = value[0:3]
+        out_ref[pl.ds(36 + c, 1), :] = value[3:4]
+        out_ref[pl.ds(12 + c, 1), :] = value[4:5]
+        out_ref[pl.ds(21 + c, 1), :] = value[5:6]
+        out_ref[pl.ds(24 + c, 1), :] = value[6:7]
+        for part in range(4):
+            at = 128 * c + 32 * part
+            base = (0, ROWS + FACE, ROWS + 2 * FACE, ROWS)[part]
+            blocks = ((1, (2,)), (2, (4,))) if part else ((1, (2,)),)
+            value = gathered(broad[at : at + 32], blocks)
+            out_ref[pl.ds(base + 3 * c, 3), :] = value[0:3]
+            out_ref[pl.ds(base + 9 + c, 1), :] = value[3:4]
+            if part:
+                live, still = (12, 21) if part < 3 else (21, 12)
+                out_ref[pl.ds(base + live + c, 1), :] = value[4:5]
+                out_ref[pl.ds(base + still + c, 1), :] = jnp.zeros((1, 128), jnp.float32)
+    out_ref[pl.ds(39, 6), :] = gathered(narrow[96:128], ())[:6]
+    out_ref[pl.ds(45, 3), :] = jnp.zeros((3, 128), jnp.float32)
+    for part in range(4):
+        base = (0, ROWS + FACE, ROWS + 2 * FACE, ROWS)[part]
+        out_ref[pl.ds(base + 15, 6), :] = gathered(broad[384 + 32 * part : 416 + 32 * part], ())[:6]
+
+
+def features_kernel(near_ref, far_ref, z_out, gram_ref, b_ref, a_ref, z_ref):
+    core = lax.axis_index("gz")
+    mine = lax.axis_index("gy")
+    chips = b_ref.shape[0]
+    for slot in range(chips):
+        swapped = (slot % 2) * 2 + slot // 2
+        at = jnp.bitwise_xor(mine, jnp.where(core == 0, slot, swapped))
+        b_ref[at] = near_ref[slot] if slot < 2 else far_ref[slot - 2]
+    lane = lax.broadcasted_iota(jnp.int32, (FACE, 128), 1)
+    upper = (lane // 32) % 2 == 1
+    z_ref[:, 96:, :] = jnp.zeros((chips, 32, 128), jnp.float32)
+    for chip in range(chips):
+        after = pltpu.roll(b_ref[(chip + 1) % chips, ROWS:, :], 96, 1)
+        before = pltpu.roll(b_ref[(chip - 1) % chips, ROWS:, :], 32, 1)
+        sums = b_ref[chip, :FACE, :] + jnp.where(upper, after, before)
+        base = 27 * chip
+        a_ref[pl.ds(base, 9), :] = b_ref[chip, 27:36, :]
+        a_ref[pl.ds(base + 9, 3, stride=3), :] = sums[12:15]
+        a_ref[pl.ds(base + 10, 3, stride=3), :] = sums[21:24]
+        a_ref[pl.ds(base + 11, 3, stride=3), :] = b_ref[chip, 24:27, :]
+        a_ref[pl.ds(base + 18, 9), :] = sums[0:9]
+        for at, centres, products, width in (
+            (90, b_ref[chip, 36:39, :], b_ref[chip, 39:45, :], 3.0),
+            (96, sums[9:12], sums[15:21], 12.0),
+        ):
+            means = [centres[c : c + 1] * (1.0 / width**3) for c in range(3)]
+            for pair, (i, j) in enumerate(INDEX_PAIRS):
+                z_ref[chip, pl.ds(at + pair, 1), :] = (
+                    products[pair : pair + 1] * (1.0 / width**3) - means[i] * means[j]
+                )
+    total = 3 * chips
+    width = lax.broadcasted_iota(jnp.int32, (total, 128), 0) % 3
+    factor = jnp.where(width == 0, 1.0 / 12.0, jnp.where(width == 1, 1.0 / 24.0, 1.0 / 48.0))
+    grad = [
+        [a_ref[pl.ds(3 * i + j, total, stride=9), :] * factor for j in range(3)] for i in range(3)
+    ]
+    strain = [[None] * 3 for _ in range(3)]
+    spin = [[None] * 3 for _ in range(3)]
+    for i in range(3):
+        for j in range(i, 3):
+            strain[i][j] = strain[j][i] = (grad[i][j] + grad[j][i]) * 0.5
+            if i != j:
+                spin[i][j] = (grad[i][j] - grad[j][i]) * 0.5
+                spin[j][i] = (grad[j][i] - grad[i][j]) * 0.5
+
+    def entry(left, right, i, j):
+        terms = [
+            left[i][k] * right[k][j]
+            for k in range(3)
+            if left[i][k] is not None and right[k][j] is not None
+        ]
+        return sum(terms[1:], terms[0])
+
+    squares = [strain[i][j] * strain[i][j] for i in range(3) for j in range(3)]
+    magnitude = sum(squares[1:], squares[0])
+    columns = [strain[i][j] for i, j in INDEX_PAIRS]
+    columns += [entry(strain, strain, i, j) for i, j in INDEX_PAIRS]
+    columns += [entry(strain, spin, i, j) - entry(spin, strain, i, j) for i, j in INDEX_PAIRS]
+    columns += [entry(spin, spin, i, j) for i, j in INDEX_PAIRS]
+    columns += [magnitude * strain[i][j] for i, j in INDEX_PAIRS]
+    for index, column in enumerate(columns):
+        for chip in range(chips):
+            z_ref[chip, pl.ds(index, 3, stride=30), :] = column[3 * chip : 3 * chip + 3]
+    z_out[...] = z_ref[mine]
+    stacked = jnp.concatenate([z_ref[chip] for chip in range(chips)], axis=1)
+    gram_ref[...] = lax.dot_general(
+        stacked[:104],
+        stacked,
+        (((1,), (1,)), ((), ())),
+        precision=PRECISE,
+        preferred_element_type=jnp.float32,
+    )
+
+
+def solve_kernel(total, gram_ref, z_ref, res_ref, coef_ref):
+    core = lax.axis_index("gz")
+    one = jnp.where(core >= 0, 1.0, 2.0)
+    count, group = 12, 2
+    rows = lax.broadcasted_iota(jnp.int32, (8, 128), 0)
+    lane = lax.broadcasted_iota(jnp.int32, (8, 128), 1)
+    block = []
+    for i in range(count + 1):
+        value = gram_ref[pl.ds(8 * i, 8), :]
+        if i < count:
+            ridge = value + 0.1 * (value + total * 1e-06)
+            value = jnp.where(lane == rows + 8 * i, ridge, value)
+        block.append(value)
+    diag = jnp.sum(jnp.where(lane == rows + 96, block[count], 0.0), axis=1, keepdims=True)
+    scale = jnp.broadcast_to(jnp.sqrt(diag / total + 1e-06), (8, 128))
+
+    def spread(value, column):
+        return jnp.broadcast_to(value[:, column : column + 1], (8, 128))
+
+    def row_of(parts, row):
+        return jnp.broadcast_to(parts[row // 8][row % 8 : row % 8 + 1, :], (8, 128))
+
+    for start in range(0, count, group):
+        size = 8 * group
+        first = 8 * start
+        square = [
+            [spread(block[start + p], first + m) * one for p in range(group)] for m in range(size)
+        ]
+        below = {
+            i: [spread(block[i], first + m) for m in range(size)]
+            for i in range(start + group, count + 1)
+        }
+        panel = []
+        for p in range(group):
+            unit = (lane == rows + first + 8 * p).astype(jnp.float32)
+            inside = (lane >= first) & (lane < first + size)
+            panel.append(jnp.where(inside, -unit, block[start + p]))
+        inverses = []
+        for m in range(size):
+            inverses.append(1.0 / row_of(square[m], m))
+            factor = [
+                jnp.where(rows == m - 8 * p, 0.0, square[m][p]) if m // 8 == p else square[m][p]
+                for p in range(group)
+            ]
+            for k in range(m + 1, size):
+                line = row_of(square[k], m) * inverses[m]
+                square[k] = [square[k][p] - factor[p] * line for p in range(group)]
+            line = row_of(panel, m) * inverses[m]
+            panel = [panel[p] - factor[p] * line for p in range(group)]
+        lines = [row_of(panel, m) * inverses[m] for m in range(size)]
+        for i in below:
+            terms = [below[i][m] * lines[m] for m in range(size)]
+            while len(terms) > 1:
+                terms = [terms[t] + terms[t + 1] for t in range(0, len(terms), 2)]
+            outside = (lane < first) | (lane >= first + size)
+            block[i] = jnp.where(outside, block[i], 0.0) - terms[0]
+    answer = jnp.where(lane < 96, block[count], 0.0)
+    coef_ref[...] = answer[:6, :96]
+    predicted = jnp.dot(answer, z_ref[...], precision=PRECISE, preferred_element_type=jnp.float32)
+    residual = (z_ref[pl.ds(96, 8), :] - predicted) / scale
+    picked = jnp.zeros((8, 128), jnp.float32)
+    for place in range(4):
+        even = pltpu.roll(residual, (128 - 16 * place) % 128, 1) if place else residual
+        odd = pltpu.roll(residual, 112 - 16 * place, 1)
+        picked = jnp.where(lane // 16 == place, jnp.where(core == 0, even, odd), picked)
+    res_ref[...] = picked[:6, :64]
+
+
+def moved(value, axis, step):
+    size = lax.axis_size(axis)
+    return lax.ppermute(value, axis, [(i, (i + step) % size) for i in range(size)])
+
+
+def added_up(value, axis):
+    size = lax.axis_size(axis)
+    bit = 1
+    while bit < size:
+        value = value + lax.ppermute(value, axis, [(i, i ^ bit) for i in range(size)])
+        bit *= 2
+    return value
+
+
+def call(kernel, outs, scratch, place=pltpu.VMEM):
+    def run(*args):
+        return pl.pallas_call(
+            kernel,
+            out_shape=[jax.ShapeDtypeStruct(shape, jnp.float32) for shape in outs],
+            in_specs=[pl.BlockSpec(memory_space=place)] * len(args),
+            out_specs=[pl.BlockSpec(memory_space=pltpu.VMEM)] * len(outs),
+            scratch_shapes=scratch,
+            compiler_params=pltpu.CompilerParams(vmem_limit_bytes=8 * 2**20),
+        )(*args)
+
+    return run
+
+
+def chip_shards(velocity):
+    bx, by, bz = velocity.shape[1:]
+    chips = lax.axis_size("gy")
+    length = bz * lax.axis_size("gz")
+    low_type, wide_type = jnp.bfloat16, jnp.float32
+    tables = [
+        velocity_plane_table(bx, by),
+        pair_plane_table(bx, by),
+        line_table(length, ((3.0, False), (3.0, True), (6.0, False), (6.0, True))),
+        line_table(length, ((12.0, False), (12.0, True), (6.0, False), (0.0, False))),
+    ]
+    tables = [jnp.asarray(table, low_type) for table in tables]
+    shapes = [tables[0].shape, tables[1].shape, (bz, 128), (bz, 128)]
+    (part,) = call(
+        sums_kernel,
+        [(ROWS + 3 * FACE, 128)],
+        [pltpu.VMEM(velocity.shape, wide_type)]
+        + [pltpu.VMEM(shape, low_type) for shape in shapes]
+        + [pltpu.VMEM((8 * shapes[1][0], 128), wide_type), pltpu.SemaphoreType.DMA((7,))],
+        pltpu.HBM,
+    )(velocity, *tables)
+    part = part + moved(part, "gz", 1)
+    own = part[: ROWS + FACE]
+    low = moved(part[ROWS + FACE : ROWS + 2 * FACE], "gx", -1)
+    high = moved(part[ROWS + 2 * FACE :], "gx", 1)
+    left = jnp.arange(128, dtype=jnp.int32)[None, :] < 64
+    middle = jnp.zeros((ROWS - FACE, 128), wide_type)
+    own = own + jnp.concatenate(
+        [jnp.where(left, high, low), middle, jnp.where(left, low, high)], axis=0
+    )
+
+    def across(value, bits):
+        pairs = []
+        for chip in range(chips):
+            for core in range(2):
+                pairs.append((2 * chip + core, 2 * (chip ^ bits[core]) + core))
+        return lax.ppermute(value, ("gy", "gz"), pairs)
+
+    near = jnp.stack([own, across(own, (1, 2))])
+    far = across(near, (2, 1))
+    stacked, gram = call(
+        features_kernel,
+        [(128, 128), (104, 128)],
+        [
+            pltpu.VMEM((chips, ROWS + FACE, 128), wide_type),
+            pltpu.VMEM((27 * chips, 128), wide_type),
+            pltpu.VMEM((chips, 128, 128), wide_type),
+        ],
+    )(near, far)
+    gram = added_up(gram, "gx")
+    samples = (bx // 8) * (by // 8) * (length // 8)
+    total = float(samples * lax.axis_size("gx") * chips)
+    residual, coefficients = call(
+        functools.partial(solve_kernel, total), [(6, 64), (6, 96)], []
+    )(gram, stacked)
+    return (residual, coefficients.T)
+
+
+def chip_form(mesh, velocity):
+    shape = mesh.shape
+    brick = (velocity.shape[1] // shape["gx"], velocity.shape[2] // shape["gy"])
+    even = shape["gx"] & (shape["gx"] - 1) == 0
+    return (
+        even and shape["gy"] == 4 and shape["gz"] == 2
+        and brick == (16, 16) and velocity.shape[3] == 256
+    )
+
+
 def solution(mesh):
     in_specs = (P(None, "gx", "gy", "gz"),)
     out_specs = (P(None, ("gx", "gy", "gz")), P())
-    return jax.shard_map(shards, mesh=mesh, in_specs=in_specs, out_specs=out_specs, check_vma=False)
+
+    def run(velocity):
+        body = chip_shards if chip_form(mesh, velocity) else shards
+        return jax.shard_map(
+            body, mesh=mesh, in_specs=in_specs, out_specs=out_specs, check_vma=False
+        )(velocity)
+
+    return run

time: 119 us -> 36.8 us (0.31)
  the two profiles are of different devices: /device:TPU:1 before, /device:TPU:0 now
where the time goes in v2:
time: 36.8 us; the launch traced here: 36.4 us
  waiting for transfers between devices  13.8 us (38%)
  starting transfers between devices  12.5 us (34%)
  Pallas kernels  5.05 us (14%)
  local copies, waits for them, and re-layouts  4.35 us (12%)
  between operations  0.67 us (2%)
    ppermute x2, waiting for transfers between devices, added_up(): lax.ppermute(value, axis, [(i, i ^ bit) for i in range(size)])  6.11 us
    ppermute x3, starting transfers between devices, moved(): lax.ppermute(value, axis, [(i, (i + step) % size) for i in range(size)])  5.62 us
    ppermute x2, waiting for transfers between devices, across(): return lax.ppermute(value, ('gy', 'gz'), pairs)  5.1 us
    pallas_call x3, Pallas kernels, run(): pl.pallas_call(kernel, out_shape=[jax.ShapeDtypeStruct(shape, jnp.float32...  5.05 us
    unnamed x10, local copies, waits for them, and re-layouts  4.27 us
    ppermute x2, starting transfers between devices, added_up(): lax.ppermute(value, axis, [(i, i ^ bit) for i in range(size)])  3.61 us
    ppermute x2, starting transfers between devices, across(): return lax.ppermute(value, ('gy', 'gz'), pairs)  3.23 us
    ppermute x3, waiting for transfers between devices, moved(): lax.ppermute(value, axis, [(i, (i + step) % size) for i in range(size)])  2.55 us
  transfers between devices with their start and end apart: 7, of which 6 were waited for; matrix products, arithmetic and copies ran while one was open for 0% of the time, Pallas kernels for 0%

profile of v2, /device:TPU:0, one launch (start us, length us, event | category | flops | bytes accessed | tf_op | source)
XLA Modules:
  0.0 36.4 jit_solution(8489622370976682931)
XLA Ops:
  0.6 0.0 copy-start
  0.6 1.0 %copy-done = f32[3,16,16,128]{3,2,1,0:T(8,128)S(1)} copy-done((f32[3,16,16,128]{3,2,1,0:T(8,128)S(1)}, f32[3,16,16,128]{3,2,1,0:T(8,128)}, u32[]{:S(2)}) %copy-start) | copy-done | bytes 393240
  1.6 0.0 copy-start.1
  1.6 0.9 %copy-done.1 = bf16[160,256]{1,0:T(8,128)(2,1)S(1)} copy-done((bf16[160,256]{1,0:T(8,128)(2,1)S(1)}, bf16[160,256]{1,0:T(8,128)(2,1)}, u32[]{:S(2)}) %copy-start.1) | copy-done | bytes 81944
  2.5 0.0 copy-start.2
  2.5 0.8 %copy-done.2 = bf16[256,128]{1,0:T(8,128)(2,1)S(1)} copy-done((bf16[256,128]{1,0:T(8,128)(2,1)S(1)}, bf16[256,128]{1,0:T(8,128)(2,1)}, u32[]{:S(2)}) %copy-start.2) | copy-done | bytes 65560
  3.4 0.0 copy-start.3
  3.4 0.8 %copy-done.3 = bf16[256,128]{1,0:T(8,128)(2,1)S(1)} copy-done((bf16[256,128]{1,0:T(8,128)(2,1)S(1)}, bf16[256,128]{1,0:T(8,128)(2,1)}, u32[]{:S(2)}) %copy-start.3) | copy-done | bytes 65560
  4.2 0.0 copy-start.4
  4.2 0.7 %copy-done.4 = bf16[32,256]{1,0:T(8,128)(2,1)S(1)} copy-done((bf16[32,256]{1,0:T(8,128)(2,1)S(1)}, bf16[32,256]{1,0:T(8,128)(2,1)}, u32[]{:S(2)}) %copy-start.4) | copy-done | bytes 16408
  4.9 1.5 %shard_map.68 = f32[120,128]{1,0:T(8,128)S(1)} custom-call(f32[3,16,16,128]{3,2,1,0:T(8,128)S(1)} %copy-done, bf16[160,256]{1,0:T(8,128)(2,1)S(1)} %copy-done.1, bf16[32,256]{1,0:T(8,128)(2,1)S(1)} %copy-done.4, bf16[256,128]{1,0:T(8,128)(2,1)S(1)} %copy-done.3, bf16[256,128]{1,0:T(8,128)(2,1)S(1)} %copy-done.2), custom_call_target="tpu_custom_call" | custom-call | tf_op jit(solution)/shard_map/pallas_call | solution.py:507
  6.4 0.6 %collective-permute-start = (f32[120,128]{1,0:T(8,128)S(1)}, f32[120,128]{1,0:T(8,128)S(1)}, u32[]{:S(2)}, u32[]{:S(2)}) collective-permute-start(f32[120,128]{1,0:T(8,128)S(1)} %shard_map.68), channel_id=1, source_target_pairs={{0,1},{1,0},{2,3},{3,2},{4,5},{5,4},{6,7},{7,6},{8,9},{9,8},{10,11... | collective-permute-start | bytes 184328 | tf_op jit(solution)/shard_map/ppermute | solution.py:493
  7.0 0.9 %collective-permute-done = f32[120,128]{1,0:T(8,128)S(1)} collective-permute-done((f32[120,128]{1,0:T(8,128)S(1)}, f32[120,128]{1,0:T(8,128)S(1)}, u32[]{:S(2)}, u32[]{:S(2)}) %collective-permute-start) | collective-permute-done | bytes 61472 | tf_op jit(solution)/shard_map/ppermute | solution.py:493
  7.9 3.0 %collective-permute-start.1 = (f32[24,128]{1,0:T(8,128)S(1)}, f32[24,128]{1,0:T(8,128)S(1)}, u32[]{:S(2)}, u32[]{:S(2)}) collective-permute-start(f32[24,128]{1,0:T(8,128)S(1)} %get-tuple-element.10), channel_id=1, source_target_pairs={{0,8},{8,16},{16,24},{24,0},{1,9},{9,17},{17,25},{25,1},{2,10},{10... | collective-permute-start | bytes 36872 | tf_op jit(solution)/shard_map/ppermute | solution.py:493
  10.8 2.1 %collective-permute-start.2 = (f32[24,128]{1,0:T(8,128)S(1)}, f32[24,128]{1,0:T(8,128)S(1)}, u32[]{:S(2)}, u32[]{:S(2)}) collective-permute-start(f32[24,128]{1,0:T(8,128)S(1)} %get-tuple-element.11), channel_id=1, source_target_pairs={{0,24},{8,0},{16,8},{24,16},{1,25},{9,1},{17,9},{25,17},{2,26},{10... | collective-permute-start | bytes 36872 | tf_op jit(solution)/shard_map/ppermute | solution.py:493
  12.9 0.1 pad.3.clone
  13.0 1.6 %collective-permute-done.1 = f32[24,128]{1,0:T(8,128)S(1)} collective-permute-done((f32[24,128]{1,0:T(8,128)S(1)}, f32[24,128]{1,0:T(8,128)S(1)}, u32[]{:S(2)}, u32[]{:S(2)}) %collective-permute-start.1) | collective-permute-done | bytes 12320 | tf_op jit(solution)/shard_map/ppermute | solution.py:493
  14.6 0.0 collective-permute-done.2
  14.7 0.1 slice_add_fusion
  14.8 1.6 %collective-permute-start.3 = (f32[72,128]{1,0:T(8,128)S(1)}, f32[72,128]{1,0:T(8,128)S(1)}, u32[]{:S(2)}, u32[]{:S(2)}) collective-permute-start(f32[72,128]{1,0:T(8,128)S(1)} %slice_add_fusion), channel_id=1, source_target_pairs={{0,2},{1,5},{2,0},{3,7},{4,6},{5,1},{6,4},{7,3},{8,10},{9,13},{10,... | collective-permute-start | bytes 110600 | tf_op jit(solution)/shard_map/ppermute | solution.py:555
  16.4 2.4 %collective-permute-done.3 = f32[72,128]{1,0:T(8,128)S(1)} collective-permute-done((f32[72,128]{1,0:T(8,128)S(1)}, f32[72,128]{1,0:T(8,128)S(1)}, u32[]{:S(2)}, u32[]{:S(2)}) %collective-permute-start.3) | collective-permute-done | bytes 36896 | tf_op jit(solution)/shard_map/ppermute | solution.py:555
  18.7 1.6 %collective-permute-start.4 = (f32[2,72,128]{2,1,0:T(8,128)S(1)}, f32[2,72,128]{2,1,0:T(8,128)S(1)}, u32[]{:S(2)}, u32[]{:S(2)}) collective-permute-start(f32[2,72,128]{2,1,0:T(8,128)S(1)} %pad_maximum_fusion.near_ref), channel_id=1, source_target_pairs={{0,4},{1,3},{2,6},{3,1},{4,0},{5,7},{6,2},{7,5},{8,12},{9,11},{10,... | collective-permute-start | bytes 221192 | tf_op jit(solution)/shard_map/ppermute | solution.py:555
  20.4 2.7 %collective-permute-done.4.far_ref = f32[2,72,128]{2,1,0:T(8,128)S(1)} collective-permute-done((f32[2,72,128]{2,1,0:T(8,128)S(1)}, f32[2,72,128]{2,1,0:T(8,128)S(1)}, u32[]{:S(2)}, u32[]{:S(2)}) %collective-permute-start.4) | collective-permute-done | bytes 73760 | tf_op jit(solution)/shard_map/ppermute | solution.py:555
  23.1 0.6 %shard_map.69 = (f32[128,128]{1,0:T(8,128)S(1)}, f32[104,128]{1,0:T(8,128)S(1)}) custom-call(f32[2,72,128]{2,1,0:T(8,128)S(1)} %pad_maximum_fusion.near_ref, f32[2,72,128]{2,1,0:T(8,128)S(1)} %collective-permute-done.4.far_ref), custom_call_target="tpu_custom_call" | custom-call | tf_op jit(solution)/shard_map/pallas_call | solution.py:507
  23.7 1.5 %collective-permute-start.5 = (f32[104,128]{1,0:T(8,128)S(1)}, f32[104,128]{1,0:T(8,128)S(1)}, u32[]{:S(2)}, u32[]{:S(2)}) collective-permute-start(f32[104,128]{1,0:T(8,128)S(1)} %get-tuple-element.6), channel_id=1, source_target_pairs={{0,8},{8,0},{16,24},{24,16},{1,9},{9,1},{17,25},{25,17},{2,10},{10... | collective-permute-start | bytes 159752 | tf_op jit(solution)/shard_map/ppermute | solution.py:500
  25.2 3.1 %collective-permute-done.5 = f32[104,128]{1,0:T(8,128)S(1)} collective-permute-done((f32[104,128]{1,0:T(8,128)S(1)}, f32[104,128]{1,0:T(8,128)S(1)}, u32[]{:S(2)}, u32[]{:S(2)}) %collective-permute-start.5) | collective-permute-done | bytes 53280 | tf_op jit(solution)/shard_map/ppermute | solution.py:500
  28.3 2.1 %collective-permute-start.6 = (f32[104,128]{1,0:T(8,128)S(1)}, f32[104,128]{1,0:T(8,128)S(1)}, u32[]{:S(2)}, u32[]{:S(2)}) collective-permute-start(f32[104,128]{1,0:T(8,128)S(1)} %add.14), channel_id=1, source_target_pairs={{0,16},{8,24},{16,0},{24,8},{1,17},{9,25},{17,1},{25,9},{2,18},{10... | collective-permute-start | bytes 159752 | tf_op jit(solution)/shard_map/ppermute | solution.py:500
  30.4 3.0 %collective-permute-done.6 = f32[104,128]{1,0:T(8,128)S(1)} collective-permute-done((f32[104,128]{1,0:T(8,128)S(1)}, f32[104,128]{1,0:T(8,128)S(1)}, u32[]{:S(2)}, u32[]{:S(2)}) %collective-permute-start.6) | collective-permute-done | bytes 53280 | tf_op jit(solution)/shard_map/ppermute | solution.py:500
  33.4 3.0 %shard_map.70 = (f32[6,64]{1,0:T(8,128)}, f32[6,96]{1,0:T(8,128)}) custom-call(f32[104,128]{1,0:T(8,128)S(1)} %add.15.gram_ref, f32[128,128]{1,0:T(8,128)S(1)} %get-tuple-element.7.z_ref), custom_call_target="tpu_custom_call" | custom-call | tf_op jit(solution)/shard_map/pallas_call | solution.py:507
  (8 shorter events, 0.1 us)
Async XLA Ops:
  0.6 1.0 %copy-start = (f32[3,16,16,128]{3,2,1,0:T(8,128)S(1)}, f32[3,16,16,128]{3,2,1,0:T(8,128)}, u32[]{:S(2)}) copy-start(f32[3,16,16,128]{3,2,1,0:T(8,128)} %x_hbm.1) | copy-start | bytes 1179652
  1.6 0.9 %copy-start.1 = (bf16[160,256]{1,0:T(8,128)(2,1)S(1)}, bf16[160,256]{1,0:T(8,128)(2,1)}, u32[]{:S(2)}) copy-start(bf16[160,256]{1,0:T(8,128)(2,1)} %constant.12.clone.wv_hbm) | copy-start | bytes 245764
  2.5 0.8 %copy-start.2 = (bf16[256,128]{1,0:T(8,128)(2,1)S(1)}, bf16[256,128]{1,0:T(8,128)(2,1)}, u32[]{:S(2)}) copy-start(bf16[256,128]{1,0:T(8,128)(2,1)} %constant.15.clone.lb_hbm) | copy-start | bytes 196612
  3.4 0.8 %copy-start.3 = (bf16[256,128]{1,0:T(8,128)(2,1)S(1)}, bf16[256,128]{1,0:T(8,128)(2,1)}, u32[]{:S(2)}) copy-start(bf16[256,128]{1,0:T(8,128)(2,1)} %constant.14.clone.la_hbm) | copy-start | bytes 196612
  4.2 0.7 %copy-start.4 = (bf16[32,256]{1,0:T(8,128)(2,1)S(1)}, bf16[32,256]{1,0:T(8,128)(2,1)}, u32[]{:S(2)}) copy-start(bf16[32,256]{1,0:T(8,128)(2,1)} %constant.13.clone.wp_hbm) | copy-start | bytes 49156
  6.4 1.5 %collective-permute-start = (f32[120,128]{1,0:T(8,128)S(1)}, f32[120,128]{1,0:T(8,128)S(1)}, u32[]{:S(2)}, u32[]{:S(2)}) collective-permute-start(f32[120,128]{1,0:T(8,128)S(1)} %shard_map.68), channel_id=1, source_target_pairs={{0,1},{1,0},{2,3},{3,2},{4,5},{5,4},{6,7},{7,6},{8,9},{9,8},{10,11... | collective-permute-start | bytes 184328 | tf_op jit(solution)/shard_map/ppermute | solution.py:493
  7.9 6.8 %collective-permute-start.1 = (f32[24,128]{1,0:T(8,128)S(1)}, f32[24,128]{1,0:T(8,128)S(1)}, u32[]{:S(2)}, u32[]{:S(2)}) collective-permute-start(f32[24,128]{1,0:T(8,128)S(1)} %get-tuple-element.10), channel_id=1, source_target_pairs={{0,8},{8,16},{16,24},{24,0},{1,9},{9,17},{17,25},{25,1},{2,10},{10... | collective-permute-start | bytes 36872 | tf_op jit(solution)/shard_map/ppermute | solution.py:493
  10.8 3.8 %collective-permute-start.2 = (f32[24,128]{1,0:T(8,128)S(1)}, f32[24,128]{1,0:T(8,128)S(1)}, u32[]{:S(2)}, u32[]{:S(2)}) collective-permute-start(f32[24,128]{1,0:T(8,128)S(1)} %get-tuple-element.11), channel_id=1, source_target_pairs={{0,24},{8,0},{16,8},{24,16},{1,25},{9,1},{17,9},{25,17},{2,26},{10... | collective-permute-start | bytes 36872 | tf_op jit(solution)/shard_map/ppermute | solution.py:493
  14.8 4.0 %collective-permute-start.3 = (f32[72,128]{1,0:T(8,128)S(1)}, f32[72,128]{1,0:T(8,128)S(1)}, u32[]{:S(2)}, u32[]{:S(2)}) collective-permute-start(f32[72,128]{1,0:T(8,128)S(1)} %slice_add_fusion), channel_id=1, source_target_pairs={{0,2},{1,5},{2,0},{3,7},{4,6},{5,1},{6,4},{7,3},{8,10},{9,13},{10,... | collective-permute-start | bytes 110600 | tf_op jit(solution)/shard_map/ppermute | solution.py:555
  18.7 4.4 %collective-permute-start.4 = (f32[2,72,128]{2,1,0:T(8,128)S(1)}, f32[2,72,128]{2,1,0:T(8,128)S(1)}, u32[]{:S(2)}, u32[]{:S(2)}) collective-permute-start(f32[2,72,128]{2,1,0:T(8,128)S(1)} %pad_maximum_fusion.near_ref), channel_id=1, source_target_pairs={{0,4},{1,3},{2,6},{3,1},{4,0},{5,7},{6,2},{7,5},{8,12},{9,11},{10,... | collective-permute-start | bytes 221192 | tf_op jit(solution)/shard_map/ppermute | solution.py:555
  23.7 4.6 %collective-permute-start.5 = (f32[104,128]{1,0:T(8,128)S(1)}, f32[104,128]{1,0:T(8,128)S(1)}, u32[]{:S(2)}, u32[]{:S(2)}) collective-permute-start(f32[104,128]{1,0:T(8,128)S(1)} %get-tuple-element.6), channel_id=1, source_target_pairs={{0,8},{8,0},{16,24},{24,16},{1,9},{9,1},{17,25},{25,17},{2,10},{10... | collective-permute-start | bytes 159752 | tf_op jit(solution)/shard_map/ppermute | solution.py:500
  28.3 5.1 %collective-permute-start.6 = (f32[104,128]{1,0:T(8,128)S(1)}, f32[104,128]{1,0:T(8,128)S(1)}, u32[]{:S(2)}, u32[]{:S(2)}) collective-permute-start(f32[104,128]{1,0:T(8,128)S(1)} %add.14), channel_id=1, source_target_pairs={{0,16},{8,24},{16,0},{24,8},{1,17},{9,25},{17,1},{25,9},{2,18},{10... | collective-permute-start | bytes 159752 | tf_op jit(solution)/shard_map/ppermute | solution.py:500

commit v3 on v2

--- a/solution.py
+++ b/solution.py
@@ -347,13 +347,10 @@
 
 
 def features_kernel(near_ref, far_ref, z_out, gram_ref, b_ref, a_ref, z_ref):
-    core = lax.axis_index("gz")
     mine = lax.axis_index("gy")
     chips = b_ref.shape[0]
     for slot in range(chips):
-        swapped = (slot % 2) * 2 + slot // 2
-        at = jnp.bitwise_xor(mine, jnp.where(core == 0, slot, swapped))
-        b_ref[at] = near_ref[slot] if slot < 2 else far_ref[slot - 2]
+        b_ref[jnp.bitwise_xor(mine, slot)] = near_ref[slot] if slot < 2 else far_ref[slot - 2]
     lane = lax.broadcasted_iota(jnp.int32, (FACE, 128), 1)
     upper = (lane // 32) % 2 == 1
     z_ref[:, 96:, :] = jnp.zeros((chips, 32, 128), jnp.float32)
@@ -488,16 +485,23 @@
     res_ref[...] = picked[:6, :64]
 
 
+def crosswise(value, axis, target):
+    pairs = []
+    for chip in range(lax.axis_size(axis)):
+        for core in range(2):
+            pairs.append((2 * chip + core, 2 * target(chip) + 1 - core))
+    return lax.ppermute(value, (axis, "gz"), pairs)
+
+
 def moved(value, axis, step):
     size = lax.axis_size(axis)
-    return lax.ppermute(value, axis, [(i, (i + step) % size) for i in range(size)])
+    return crosswise(value, axis, lambda chip: (chip + step) % size)
 
 
 def added_up(value, axis):
-    size = lax.axis_size(axis)
     bit = 1
-    while bit < size:
-        value = value + lax.ppermute(value, axis, [(i, i ^ bit) for i in range(size)])
+    while bit < lax.axis_size(axis):
+        value = value + crosswise(value, axis, lambda chip: chip ^ bit)
         bit *= 2
     return value
 
@@ -536,8 +540,8 @@
         + [pltpu.VMEM(shape, low_type) for shape in shapes]
         + [pltpu.VMEM((8 * shapes[1][0], 128), wide_type), pltpu.SemaphoreType.DMA((7,))],
         pltpu.HBM,
-    )(velocity, *tables)
-    part = part + moved(part, "gz", 1)
+    )(*[pltpu.with_memory_space_constraint(value, pltpu.HBM) for value in (velocity, *tables)])
+    part = part + lax.ppermute(part, "gz", [(0, 1), (1, 0)])
     own = part[: ROWS + FACE]
     low = moved(part[ROWS + FACE : ROWS + 2 * FACE], "gx", -1)
     high = moved(part[ROWS + 2 * FACE :], "gx", 1)
@@ -547,15 +551,8 @@
         [jnp.where(left, high, low), middle, jnp.where(left, low, high)], axis=0
     )
 
-    def across(value, bits):
-        pairs = []
-        for chip in range(chips):
-            for core in range(2):
-                pairs.append((2 * chip + core, 2 * (chip ^ bits[core]) + core))
-        return lax.ppermute(value, ("gy", "gz"), pairs)
-
-    near = jnp.stack([own, across(own, (1, 2))])
-    far = across(near, (2, 1))
+    near = jnp.stack([own, crosswise(own, "gy", lambda chip: chip ^ 1)])
+    far = crosswise(near, "gy", lambda chip: chip ^ 2)
     stacked, gram = call(
         features_kernel,
         [(128, 128), (104, 128)],

time: 36.8 us -> 30.4 us (0.83)
  the two profiles are of different devices: /device:TPU:0 before, /device:TPU:5 now
where the time goes in v3:
time: 30.4 us; the launch traced here: 30.3 us
  waiting for transfers between devices  14.8 us (49%)
  starting transfers between devices  9.15 us (30%)
  Pallas kernels  5.43 us (18%)
  between operations  0.66 us (2%)
    ppermute x6, waiting for transfers between devices, crosswise(): return lax.ppermute(value, (axis, 'gz'), pairs)  14 us
    ppermute x6, starting transfers between devices, crosswise(): return lax.ppermute(value, (axis, 'gz'), pairs)  8.41 us
    pallas_call x3, Pallas kernels, run(): pl.pallas_call(kernel, out_shape=[jax.ShapeDtypeStruct(shape, jnp.float32...  5.43 us
    ppermute x1, waiting for transfers between devices, chip_shards(): part = part + lax.ppermute(part, 'gz', [(0, 1), (1, 0)])  0.9 us
    ppermute x1, starting transfers between devices, chip_shards(): part = part + lax.ppermute(part, 'gz', [(0, 1), (1, 0)])  0.74 us
  transfers between devices with their start and end apart: 7, of which 6 were waited for; matrix products, arithmetic and copies ran while one was open for 0% of the time, Pallas kernels for 0%

profile of v3, /device:TPU:5, one launch (start us, length us, event | category | flops | bytes accessed | tf_op | source)
XLA Modules:
  0.0 30.3 jit_solution(3871286318495079285)
XLA Ops:
  0.6 1.9 %shard_map.68 = f32[120,128]{1,0:T(8,128)S(1)} custom-call(f32[3,16,16,128]{3,2,1,0:T(8,128)} %x_hbm.1, bf16[160,256]{1,0:T(8,128)(2,1)} %constant.12.clone.wv_hbm, bf16[32,256]{1,0:T(8,128)(2,1)} %constant.13.clone.wp_hbm, bf16[256,128]{1,0:T(8,128)(2,1)} %constant.14.clone.la_hbm, bf16[256,128]{1,0:T(8,128)(2,1)} %constant.15.clone.lb_hbm), custom_call_target="tpu_custom_call" | custom-call | tf_op jit(solution)/shard_map/pallas_call | solution.py:511
  2.5 0.7 %collective-permute-start = (f32[120,128]{1,0:T(8,128)S(1)}, f32[120,128]{1,0:T(8,128)S(1)}, u32[]{:S(2)}, u32[]{:S(2)}) collective-permute-start(f32[120,128]{1,0:T(8,128)S(1)} %shard_map.68), channel_id=1, source_target_pairs={{0,1},{1,0},{2,3},{3,2},{4,5},{5,4},{6,7},{7,6},{8,9},{9,8},{10,11... | collective-permute-start | bytes 184328 | tf_op jit(solution)/shard_map/ppermute | solution.py:544
  3.2 0.9 %collective-permute-done = f32[120,128]{1,0:T(8,128)S(1)} collective-permute-done((f32[120,128]{1,0:T(8,128)S(1)}, f32[120,128]{1,0:T(8,128)S(1)}, u32[]{:S(2)}, u32[]{:S(2)}) %collective-permute-start) | collective-permute-done | bytes 61472 | tf_op jit(solution)/shard_map/ppermute | solution.py:544
  4.2 1.6 %collective-permute-start.1 = (f32[24,128]{1,0:T(8,128)S(1)}, f32[24,128]{1,0:T(8,128)S(1)}, u32[]{:S(2)}, u32[]{:S(2)}) collective-permute-start(f32[24,128]{1,0:T(8,128)S(1)} %get-tuple-element.10), channel_id=1, source_target_pairs={{0,9},{1,8},{8,17},{9,16},{16,25},{17,24},{24,1},{25,0},{2,11},{3,... | collective-permute-start | bytes 36872 | tf_op jit(solution)/shard_map/ppermute | solution.py:493
  5.7 2.1 %collective-permute-start.2 = (f32[24,128]{1,0:T(8,128)S(1)}, f32[24,128]{1,0:T(8,128)S(1)}, u32[]{:S(2)}, u32[]{:S(2)}) collective-permute-start(f32[24,128]{1,0:T(8,128)S(1)} %get-tuple-element.11), channel_id=1, source_target_pairs={{0,25},{1,24},{8,1},{9,0},{16,9},{17,8},{24,17},{25,16},{2,27},{3,... | collective-permute-start | bytes 36872 | tf_op jit(solution)/shard_map/ppermute | solution.py:493
  7.8 0.1 pad.3.clone
  7.9 1.2 %collective-permute-done.1 = f32[24,128]{1,0:T(8,128)S(1)} collective-permute-done((f32[24,128]{1,0:T(8,128)S(1)}, f32[24,128]{1,0:T(8,128)S(1)}, u32[]{:S(2)}, u32[]{:S(2)}) %collective-permute-start.1) | collective-permute-done | bytes 12320 | tf_op jit(solution)/shard_map/ppermute | solution.py:493
  9.2 0.0 collective-permute-done.2
  9.2 0.1 slice_add_fusion
  9.2 1.5 %collective-permute-start.3 = (f32[72,128]{1,0:T(8,128)S(1)}, f32[72,128]{1,0:T(8,128)S(1)}, u32[]{:S(2)}, u32[]{:S(2)}) collective-permute-start(f32[72,128]{1,0:T(8,128)S(1)} %slice_add_fusion), channel_id=1, source_target_pairs={{0,3},{1,2},{2,1},{3,0},{4,7},{5,6},{6,5},{7,4},{8,11},{9,10},{10,... | collective-permute-start | bytes 110600 | tf_op jit(solution)/shard_map/ppermute | solution.py:493
  10.7 2.0 %collective-permute-done.3 = f32[72,128]{1,0:T(8,128)S(1)} collective-permute-done((f32[72,128]{1,0:T(8,128)S(1)}, f32[72,128]{1,0:T(8,128)S(1)}, u32[]{:S(2)}, u32[]{:S(2)}) %collective-permute-start.3) | collective-permute-done | bytes 36896 | tf_op jit(solution)/shard_map/ppermute | solution.py:493
  12.7 0.3 collective-permute-start.4
  13.0 3.9 %collective-permute-done.4.far_ref = f32[2,72,128]{2,1,0:T(8,128)S(1)} collective-permute-done((f32[2,72,128]{2,1,0:T(8,128)S(1)}, f32[2,72,128]{2,1,0:T(8,128)S(1)}, u32[]{:S(2)}, u32[]{:S(2)}) %collective-permute-start.4) | collective-permute-done | bytes 73760 | tf_op jit(solution)/shard_map/ppermute | solution.py:493
  16.9 0.6 %shard_map.69 = (f32[128,128]{1,0:T(8,128)S(1)}, f32[104,128]{1,0:T(8,128)S(1)}) custom-call(f32[2,72,128]{2,1,0:T(8,128)S(1)} %pad_maximum_fusion.near_ref, f32[2,72,128]{2,1,0:T(8,128)S(1)} %collective-permute-done.4.far_ref), custom_call_target="tpu_custom_call" | custom-call | tf_op jit(solution)/shard_map/pallas_call | solution.py:511
  17.5 0.8 %collective-permute-start.5 = (f32[104,128]{1,0:T(8,128)S(1)}, f32[104,128]{1,0:T(8,128)S(1)}, u32[]{:S(2)}, u32[]{:S(2)}) collective-permute-start(f32[104,128]{1,0:T(8,128)S(1)} %get-tuple-element.6), channel_id=1, source_target_pairs={{0,9},{1,8},{8,1},{9,0},{16,25},{17,24},{24,17},{25,16},{2,11},{3,... | collective-permute-start | bytes 159752 | tf_op jit(solution)/shard_map/ppermute | solution.py:493
  18.4 3.0 %collective-permute-done.5 = f32[104,128]{1,0:T(8,128)S(1)} collective-permute-done((f32[104,128]{1,0:T(8,128)S(1)}, f32[104,128]{1,0:T(8,128)S(1)}, u32[]{:S(2)}, u32[]{:S(2)}) %collective-permute-start.5) | collective-permute-done | bytes 53280 | tf_op jit(solution)/shard_map/ppermute | solution.py:493
  21.4 2.1 %collective-permute-start.6 = (f32[104,128]{1,0:T(8,128)S(1)}, f32[104,128]{1,0:T(8,128)S(1)}, u32[]{:S(2)}, u32[]{:S(2)}) collective-permute-start(f32[104,128]{1,0:T(8,128)S(1)} %add.14), channel_id=1, source_target_pairs={{0,17},{1,16},{8,25},{9,24},{16,1},{17,0},{24,9},{25,8},{2,19},{3,... | collective-permute-start | bytes 159752 | tf_op jit(solution)/shard_map/ppermute | solution.py:493
  23.5 3.8 %collective-permute-done.6 = f32[104,128]{1,0:T(8,128)S(1)} collective-permute-done((f32[104,128]{1,0:T(8,128)S(1)}, f32[104,128]{1,0:T(8,128)S(1)}, u32[]{:S(2)}, u32[]{:S(2)}) %collective-permute-start.6) | collective-permute-done | bytes 53280 | tf_op jit(solution)/shard_map/ppermute | solution.py:493
  27.3 3.0 %shard_map.70 = (f32[6,64]{1,0:T(8,128)}, f32[6,96]{1,0:T(8,128)}) custom-call(f32[104,128]{1,0:T(8,128)S(1)} %add.15.gram_ref, f32[128,128]{1,0:T(8,128)S(1)} %get-tuple-element.7.z_ref), custom_call_target="tpu_custom_call" | custom-call | tf_op jit(solution)/shard_map/pallas_call | solution.py:511
  (8 shorter events, 0.1 us)
Async XLA Ops:
  2.5 1.6 %collective-permute-start = (f32[120,128]{1,0:T(8,128)S(1)}, f32[120,128]{1,0:T(8,128)S(1)}, u32[]{:S(2)}, u32[]{:S(2)}) collective-permute-start(f32[120,128]{1,0:T(8,128)S(1)} %shard_map.68), channel_id=1, source_target_pairs={{0,1},{1,0},{2,3},{3,2},{4,5},{5,4},{6,7},{7,6},{8,9},{9,8},{10,11... | collective-permute-start | bytes 184328 | tf_op jit(solution)/shard_map/ppermute | solution.py:544
  4.2 5.0 %collective-permute-start.1 = (f32[24,128]{1,0:T(8,128)S(1)}, f32[24,128]{1,0:T(8,128)S(1)}, u32[]{:S(2)}, u32[]{:S(2)}) collective-permute-start(f32[24,128]{1,0:T(8,128)S(1)} %get-tuple-element.10), channel_id=1, source_target_pairs={{0,9},{1,8},{8,17},{9,16},{16,25},{17,24},{24,1},{25,0},{2,11},{3,... | collective-permute-start | bytes 36872 | tf_op jit(solution)/shard_map/ppermute | solution.py:493
  5.7 3.4 %collective-permute-start.2 = (f32[24,128]{1,0:T(8,128)S(1)}, f32[24,128]{1,0:T(8,128)S(1)}, u32[]{:S(2)}, u32[]{:S(2)}) collective-permute-start(f32[24,128]{1,0:T(8,128)S(1)} %get-tuple-element.11), channel_id=1, source_target_pairs={{0,25},{1,24},{8,1},{9,0},{16,9},{17,8},{24,17},{25,16},{2,27},{3,... | collective-permute-start | bytes 36872 | tf_op jit(solution)/shard_map/ppermute | solution.py:493
  9.2 3.5 %collective-permute-start.3 = (f32[72,128]{1,0:T(8,128)S(1)}, f32[72,128]{1,0:T(8,128)S(1)}, u32[]{:S(2)}, u32[]{:S(2)}) collective-permute-start(f32[72,128]{1,0:T(8,128)S(1)} %slice_add_fusion), channel_id=1, source_target_pairs={{0,3},{1,2},{2,1},{3,0},{4,7},{5,6},{6,5},{7,4},{8,11},{9,10},{10,... | collective-permute-start | bytes 110600 | tf_op jit(solution)/shard_map/ppermute | solution.py:493
  12.7 4.2 %collective-permute-start.4 = (f32[2,72,128]{2,1,0:T(8,128)S(1)}, f32[2,72,128]{2,1,0:T(8,128)S(1)}, u32[]{:S(2)}, u32[]{:S(2)}) collective-permute-start(f32[2,72,128]{2,1,0:T(8,128)S(1)} %pad_maximum_fusion.near_ref), channel_id=1, source_target_pairs={{0,5},{1,4},{2,7},{3,6},{4,1},{5,0},{6,3},{7,2},{8,13},{9,12},{10,... | collective-permute-start | bytes 221192 | tf_op jit(solution)/shard_map/ppermute | solution.py:493
  17.5 3.9 %collective-permute-start.5 = (f32[104,128]{1,0:T(8,128)S(1)}, f32[104,128]{1,0:T(8,128)S(1)}, u32[]{:S(2)}, u32[]{:S(2)}) collective-permute-start(f32[104,128]{1,0:T(8,128)S(1)} %get-tuple-element.6), channel_id=1, source_target_pairs={{0,9},{1,8},{8,1},{9,0},{16,25},{17,24},{24,17},{25,16},{2,11},{3,... | collective-permute-start | bytes 159752 | tf_op jit(solution)/shard_map/ppermute | solution.py:493
  21.4 5.9 %collective-permute-start.6 = (f32[104,128]{1,0:T(8,128)S(1)}, f32[104,128]{1,0:T(8,128)S(1)}, u32[]{:S(2)}, u32[]{:S(2)}) collective-permute-start(f32[104,128]{1,0:T(8,128)S(1)} %add.14), channel_id=1, source_target_pairs={{0,17},{1,16},{8,25},{9,24},{16,1},{17,0},{24,9},{25,8},{2,19},{3,... | collective-permute-start | bytes 159752 | tf_op jit(solution)/shard_map/ppermute | solution.py:493

commit v4 on v3

--- a/solution.py
+++ b/solution.py
@@ -408,13 +408,21 @@
             z_ref[chip, pl.ds(index, 3, stride=30), :] = column[3 * chip : 3 * chip + 3]
     z_out[...] = z_ref[mine]
     stacked = jnp.concatenate([z_ref[chip] for chip in range(chips)], axis=1)
-    gram_ref[...] = lax.dot_general(
+    gram = lax.dot_general(
         stacked[:104],
         stacked,
         (((1,), (1,)), ((), ())),
         precision=PRECISE,
         preferred_element_type=jnp.float32,
     )
+    rows = lax.broadcasted_iota(jnp.int32, (8, 128), 0)
+    lane = lax.broadcasted_iota(jnp.int32, (8, 128), 1)
+    gram_ref[pl.ds(0, 8), :] = gram[:8]
+    for p in range(1, 7):
+        lower = pltpu.roll(gram[48 + 8 * p : 56 + 8 * p], 72, 1)
+        gram_ref[pl.ds(8 * p, 8), :] = jnp.where(
+            lane >= rows + 8 * p, gram[8 * p : 8 * p + 8], lower
+        )
 
 
 def solve_kernel(total, gram_ref, z_ref, res_ref, coef_ref):
@@ -423,13 +431,22 @@
     count, group = 12, 2
     rows = lax.broadcasted_iota(jnp.int32, (8, 128), 0)
     lane = lax.broadcasted_iota(jnp.int32, (8, 128), 1)
+    half = []
+    for i in range(count + 1):
+        if i < 7:
+            value = gram_ref[pl.ds(8 * i, 8), :]
+            half.append(jnp.where(lane >= rows + 8 * i, value, 0.0))
+        else:
+            value = pltpu.roll(gram_ref[pl.ds(8 * i - 48, 8), :], 56, 1)
+            half.append(jnp.where((lane >= 56) & (lane <= rows + 8 * i), value, 0.0))
+    blank = [jnp.zeros((8, 128), jnp.float32)]
+    other = jnp.transpose(jnp.concatenate(half + blank * (15 - count), axis=0))
     block = []
     for i in range(count + 1):
-        value = gram_ref[pl.ds(8 * i, 8), :]
-        if i < count:
-            ridge = value + 0.1 * (value + total * 1e-06)
-            value = jnp.where(lane == rows + 8 * i, ridge, value)
-        block.append(value)
+        value = half[i]
+        ridge = value + 0.1 * (value + total * 1e-06) if i < count else value
+        value = value + other[8 * i : 8 * i + 8]
+        block.append(jnp.where(lane == rows + 8 * i, ridge, value))
     diag = jnp.sum(jnp.where(lane == rows + 96, block[count], 0.0), axis=1, keepdims=True)
     scale = jnp.broadcast_to(jnp.sqrt(diag / total + 1e-06), (8, 128))
 
@@ -442,17 +459,14 @@
     for start in range(0, count, group):
         size = 8 * group
         first = 8 * start
-        square = [
-            [spread(block[start + p], first + m) * one for p in range(group)] for m in range(size)
-        ]
-        below = {
-            i: [spread(block[i], first + m) for m in range(size)]
-            for i in range(start + group, count + 1)
-        }
+        near = range(start + group, min(start + 2 * group, count + 1))
+        far = range(start + 2 * group, count + 1)
+        square = [[spread(block[start + p], first + m) * one for p in range(group)] for m in range(size)]
+        below = {i: [spread(block[i], first + m) for m in range(size)] for i in near}
+        inside = (lane >= first) & (lane < first + size)
         panel = []
         for p in range(group):
             unit = (lane == rows + first + 8 * p).astype(jnp.float32)
-            inside = (lane >= first) & (lane < first + size)
             panel.append(jnp.where(inside, -unit, block[start + p]))
         inverses = []
         for m in range(size):
@@ -467,12 +481,24 @@
             line = row_of(panel, m) * inverses[m]
             panel = [panel[p] - factor[p] * line for p in range(group)]
         lines = [row_of(panel, m) * inverses[m] for m in range(size)]
-        for i in below:
+        for i in near:
             terms = [below[i][m] * lines[m] for m in range(size)]
             while len(terms) > 1:
                 terms = [terms[t] + terms[t + 1] for t in range(0, len(terms), 2)]
-            outside = (lane < first) | (lane >= first + size)
-            block[i] = jnp.where(outside, block[i], 0.0) - terms[0]
+            block[i] = jnp.where(inside, 0.0, block[i]) - terms[0]
+        if far:
+            scaled = []
+            for p in range(group):
+                inverse = inverses[8 * p]
+                for row in range(1, 8):
+                    inverse = jnp.where(rows == row, inverses[8 * p + row], inverse)
+                scaled.append(panel[p] * inverse)
+            blank = [jnp.zeros((8, 128), jnp.float32)]
+            right = jnp.concatenate(blank * start + scaled + blank * (16 - group - start), axis=0)
+            left = jnp.concatenate([jnp.where(inside, block[i], 0.0) for i in far], axis=0)
+            change = jnp.dot(left, right, precision=PRECISE, preferred_element_type=jnp.float32)
+            for at, i in enumerate(far):
+                block[i] = jnp.where(inside, 0.0, block[i]) - change[8 * at : 8 * at + 8]
     answer = jnp.where(lane < 96, block[count], 0.0)
     coef_ref[...] = answer[:6, :96]
     predicted = jnp.dot(answer, z_ref[...], precision=PRECISE, preferred_element_type=jnp.float32)
@@ -555,7 +581,7 @@
     far = crosswise(near, "gy", lambda chip: chip ^ 2)
     stacked, gram = call(
         features_kernel,
-        [(128, 128), (104, 128)],
+        [(128, 128), (56, 128)],
         [
             pltpu.VMEM((chips, ROWS + FACE, 128), wide_type),
             pltpu.VMEM((27 * chips, 128), wide_type),

time: 30.4 us -> 28.9 us (0.951)
  the two profiles are of different devices: /device:TPU:5 before, /device:TPU:1 now
where the time goes in v4:
time: 28.9 us; the launch traced here: 28.5 us
  starting transfers between devices  11.3 us (39%)
  waiting for transfers between devices  11.2 us (39%)
  Pallas kernels  5.24 us (18%)
  between operations  0.66 us (2%)
    ppermute x6, starting transfers between devices, crosswise(): return lax.ppermute(value, (axis, 'gz'), pairs)  11.2 us
    ppermute x6, waiting for transfers between devices, crosswise(): return lax.ppermute(value, (axis, 'gz'), pairs)  9.92 us
    pallas_call x3, Pallas kernels, run(): pl.pallas_call(kernel, out_shape=[jax.ShapeDtypeStruct(shape, jnp.float32...  5.24 us
    ppermute x1, waiting for transfers between devices, chip_shards(): part = part + lax.ppermute(part, 'gz', [(0, 1), (1, 0)])  1.23 us
  transfers between devices with their start and end apart: 7, of which 6 were waited for; matrix products, arithmetic and copies ran while one was open for 0% of the time, Pallas kernels for 0%

profile of v4, /device:TPU:1, one launch (start us, length us, event | category | flops | bytes accessed | tf_op | source)
XLA Modules:
  0.0 28.5 jit_solution(8367507933197670206)
XLA Ops:
  0.6 1.9 %shard_map.68 = f32[120,128]{1,0:T(8,128)S(1)} custom-call(f32[3,16,16,128]{3,2,1,0:T(8,128)} %x_hbm.1, bf16[160,256]{1,0:T(8,128)(2,1)} %constant.12.clone.wv_hbm, bf16[32,256]{1,0:T(8,128)(2,1)} %constant.13.clone.wp_hbm, bf16[256,128]{1,0:T(8,128)(2,1)} %constant.14.clone.la_hbm, bf16[256,128]{1,0:T(8,128)(2,1)} %constant.15.clone.lb_hbm), custom_call_target="tpu_custom_call" | custom-call | tf_op jit(solution)/shard_map/pallas_call | solution.py:537
  2.5 0.1 collective-permute-start
  2.6 1.2 %collective-permute-done = f32[120,128]{1,0:T(8,128)S(1)} collective-permute-done((f32[120,128]{1,0:T(8,128)S(1)}, f32[120,128]{1,0:T(8,128)S(1)}, u32[]{:S(2)}, u32[]{:S(2)}) %collective-permute-start) | collective-permute-done | bytes 61472 | tf_op jit(solution)/shard_map/ppermute | solution.py:570
  3.8 2.7 %collective-permute-start.1 = (f32[24,128]{1,0:T(8,128)S(1)}, f32[24,128]{1,0:T(8,128)S(1)}, u32[]{:S(2)}, u32[]{:S(2)}) collective-permute-start(f32[24,128]{1,0:T(8,128)S(1)} %get-tuple-element.10), channel_id=1, source_target_pairs={{0,9},{1,8},{8,17},{9,16},{16,25},{17,24},{24,1},{25,0},{2,11},{3,... | collective-permute-start | bytes 36872 | tf_op jit(solution)/shard_map/ppermute | solution.py:519
  6.6 2.1 %collective-permute-start.2 = (f32[24,128]{1,0:T(8,128)S(1)}, f32[24,128]{1,0:T(8,128)S(1)}, u32[]{:S(2)}, u32[]{:S(2)}) collective-permute-start(f32[24,128]{1,0:T(8,128)S(1)} %get-tuple-element.11), channel_id=1, source_target_pairs={{0,25},{1,24},{8,1},{9,0},{16,9},{17,8},{24,17},{25,16},{2,27},{3,... | collective-permute-start | bytes 36872 | tf_op jit(solution)/shard_map/ppermute | solution.py:519
  8.7 0.1 pad.3.clone
  8.7 1.2 %collective-permute-done.1 = f32[24,128]{1,0:T(8,128)S(1)} collective-permute-done((f32[24,128]{1,0:T(8,128)S(1)}, f32[24,128]{1,0:T(8,128)S(1)}, u32[]{:S(2)}, u32[]{:S(2)}) %collective-permute-start.1) | collective-permute-done | bytes 12320 | tf_op jit(solution)/shard_map/ppermute | solution.py:519
  10.0 0.0 collective-permute-done.2
  10.0 0.1 slice_add_fusion
  10.1 1.5 %collective-permute-start.3 = (f32[72,128]{1,0:T(8,128)S(1)}, f32[72,128]{1,0:T(8,128)S(1)}, u32[]{:S(2)}, u32[]{:S(2)}) collective-permute-start(f32[72,128]{1,0:T(8,128)S(1)} %slice_add_fusion), channel_id=1, source_target_pairs={{0,3},{1,2},{2,1},{3,0},{4,7},{5,6},{6,5},{7,4},{8,11},{9,10},{10,... | collective-permute-start | bytes 110600 | tf_op jit(solution)/shard_map/ppermute | solution.py:519
  11.5 1.9 %collective-permute-done.3 = f32[72,128]{1,0:T(8,128)S(1)} collective-permute-done((f32[72,128]{1,0:T(8,128)S(1)}, f32[72,128]{1,0:T(8,128)S(1)}, u32[]{:S(2)}, u32[]{:S(2)}) %collective-permute-start.3) | collective-permute-done | bytes 36896 | tf_op jit(solution)/shard_map/ppermute | solution.py:519
  13.5 1.5 %collective-permute-start.4 = (f32[2,72,128]{2,1,0:T(8,128)S(1)}, f32[2,72,128]{2,1,0:T(8,128)S(1)}, u32[]{:S(2)}, u32[]{:S(2)}) collective-permute-start(f32[2,72,128]{2,1,0:T(8,128)S(1)} %pad_maximum_fusion.near_ref), channel_id=1, source_target_pairs={{0,5},{1,4},{2,7},{3,6},{4,1},{5,0},{6,3},{7,2},{8,13},{9,12},{10,... | collective-permute-start | bytes 221192 | tf_op jit(solution)/shard_map/ppermute | solution.py:519
  15.0 2.6 %collective-permute-done.4.far_ref = f32[2,72,128]{2,1,0:T(8,128)S(1)} collective-permute-done((f32[2,72,128]{2,1,0:T(8,128)S(1)}, f32[2,72,128]{2,1,0:T(8,128)S(1)}, u32[]{:S(2)}, u32[]{:S(2)}) %collective-permute-start.4) | collective-permute-done | bytes 73760 | tf_op jit(solution)/shard_map/ppermute | solution.py:519
  17.6 0.6 %shard_map.69 = (f32[128,128]{1,0:T(8,128)S(1)}, f32[56,128]{1,0:T(8,128)S(1)}) custom-call(f32[2,72,128]{2,1,0:T(8,128)S(1)} %pad_maximum_fusion.near_ref, f32[2,72,128]{2,1,0:T(8,128)S(1)} %collective-permute-done.4.far_ref), custom_call_target="tpu_custom_call" | custom-call | tf_op jit(solution)/shard_map/pallas_call | solution.py:537
  18.2 1.0 %collective-permute-start.5 = (f32[56,128]{1,0:T(8,128)S(1)}, f32[56,128]{1,0:T(8,128)S(1)}, u32[]{:S(2)}, u32[]{:S(2)}) collective-permute-start(f32[56,128]{1,0:T(8,128)S(1)} %get-tuple-element.6), channel_id=1, source_target_pairs={{0,9},{1,8},{8,1},{9,0},{16,25},{17,24},{24,17},{25,16},{2,11},{3,... | collective-permute-start | bytes 86024 | tf_op jit(solution)/shard_map/ppermute | solution.py:519
  19.3 2.3 %collective-permute-done.5 = f32[56,128]{1,0:T(8,128)S(1)} collective-permute-done((f32[56,128]{1,0:T(8,128)S(1)}, f32[56,128]{1,0:T(8,128)S(1)}, u32[]{:S(2)}, u32[]{:S(2)}) %collective-permute-start.5) | collective-permute-done | bytes 28704 | tf_op jit(solution)/shard_map/ppermute | solution.py:519
  21.6 2.4 %collective-permute-start.6 = (f32[56,128]{1,0:T(8,128)S(1)}, f32[56,128]{1,0:T(8,128)S(1)}, u32[]{:S(2)}, u32[]{:S(2)}) collective-permute-start(f32[56,128]{1,0:T(8,128)S(1)} %add.14), channel_id=1, source_target_pairs={{0,17},{1,16},{8,25},{9,24},{16,1},{17,0},{24,9},{25,8},{2,19},{3,... | collective-permute-start | bytes 86024 | tf_op jit(solution)/shard_map/ppermute | solution.py:519
  24.0 1.8 %collective-permute-done.6 = f32[56,128]{1,0:T(8,128)S(1)} collective-permute-done((f32[56,128]{1,0:T(8,128)S(1)}, f32[56,128]{1,0:T(8,128)S(1)}, u32[]{:S(2)}, u32[]{:S(2)}) %collective-permute-start.6) | collective-permute-done | bytes 28704 | tf_op jit(solution)/shard_map/ppermute | solution.py:519
  25.8 2.7 %shard_map.70 = (f32[6,64]{1,0:T(8,128)}, f32[6,96]{1,0:T(8,128)}) custom-call(f32[56,128]{1,0:T(8,128)S(1)} %add.15.gram_ref, f32[128,128]{1,0:T(8,128)S(1)} %get-tuple-element.7.z_ref), custom_call_target="tpu_custom_call" | custom-call | tf_op jit(solution)/shard_map/pallas_call | solution.py:537
  (8 shorter events, 0.0 us)
Async XLA Ops:
  2.5 1.3 %collective-permute-start = (f32[120,128]{1,0:T(8,128)S(1)}, f32[120,128]{1,0:T(8,128)S(1)}, u32[]{:S(2)}, u32[]{:S(2)}) collective-permute-start(f32[120,128]{1,0:T(8,128)S(1)} %shard_map.68), channel_id=1, source_target_pairs={{0,1},{1,0},{2,3},{3,2},{4,5},{5,4},{6,7},{7,6},{8,9},{9,8},{10,11... | collective-permute-start | bytes 184328 | tf_op jit(solution)/shard_map/ppermute | solution.py:570
  3.8 6.1 %collective-permute-start.1 = (f32[24,128]{1,0:T(8,128)S(1)}, f32[24,128]{1,0:T(8,128)S(1)}, u32[]{:S(2)}, u32[]{:S(2)}) collective-permute-start(f32[24,128]{1,0:T(8,128)S(1)} %get-tuple-element.10), channel_id=1, source_target_pairs={{0,9},{1,8},{8,17},{9,16},{16,25},{17,24},{24,1},{25,0},{2,11},{3,... | collective-permute-start | bytes 36872 | tf_op jit(solution)/shard_map/ppermute | solution.py:519
  6.6 3.4 %collective-permute-start.2 = (f32[24,128]{1,0:T(8,128)S(1)}, f32[24,128]{1,0:T(8,128)S(1)}, u32[]{:S(2)}, u32[]{:S(2)}) collective-permute-start(f32[24,128]{1,0:T(8,128)S(1)} %get-tuple-element.11), channel_id=1, source_target_pairs={{0,25},{1,24},{8,1},{9,0},{16,9},{17,8},{24,17},{25,16},{2,27},{3,... | collective-permute-start | bytes 36872 | tf_op jit(solution)/shard_map/ppermute | solution.py:519
  10.1 3.4 %collective-permute-start.3 = (f32[72,128]{1,0:T(8,128)S(1)}, f32[72,128]{1,0:T(8,128)S(1)}, u32[]{:S(2)}, u32[]{:S(2)}) collective-permute-start(f32[72,128]{1,0:T(8,128)S(1)} %slice_add_fusion), channel_id=1, source_target_pairs={{0,3},{1,2},{2,1},{3,0},{4,7},{5,6},{6,5},{7,4},{8,11},{9,10},{10,... | collective-permute-start | bytes 110600 | tf_op jit(solution)/shard_map/ppermute | solution.py:519
  13.5 4.1 %collective-permute-start.4 = (f32[2,72,128]{2,1,0:T(8,128)S(1)}, f32[2,72,128]{2,1,0:T(8,128)S(1)}, u32[]{:S(2)}, u32[]{:S(2)}) collective-permute-start(f32[2,72,128]{2,1,0:T(8,128)S(1)} %pad_maximum_fusion.near_ref), channel_id=1, source_target_pairs={{0,5},{1,4},{2,7},{3,6},{4,1},{5,0},{6,3},{7,2},{8,13},{9,12},{10,... | collective-permute-start | bytes 221192 | tf_op jit(solution)/shard_map/ppermute | solution.py:519
  18.2 3.4 %collective-permute-start.5 = (f32[56,128]{1,0:T(8,128)S(1)}, f32[56,128]{1,0:T(8,128)S(1)}, u32[]{:S(2)}, u32[]{:S(2)}) collective-permute-start(f32[56,128]{1,0:T(8,128)S(1)} %get-tuple-element.6), channel_id=1, source_target_pairs={{0,9},{1,8},{8,1},{9,0},{16,25},{17,24},{24,17},{25,16},{2,11},{3,... | collective-permute-start | bytes 86024 | tf_op jit(solution)/shard_map/ppermute | solution.py:519
  21.6 4.2 %collective-permute-start.6 = (f32[56,128]{1,0:T(8,128)S(1)}, f32[56,128]{1,0:T(8,128)S(1)}, u32[]{:S(2)}, u32[]{:S(2)}) collective-permute-start(f32[56,128]{1,0:T(8,128)S(1)} %add.14), channel_id=1, source_target_pairs={{0,17},{1,16},{8,25},{9,24},{16,1},{17,0},{24,9},{25,8},{2,19},{3,... | collective-permute-start | bytes 86024 | tf_op jit(solution)/shard_map/ppermute | solution.py:519

commit v5 on v4

--- a/solution.py
+++ b/solution.py
@@ -346,11 +346,10 @@
         out_ref[pl.ds(base + 15, 6), :] = gathered(broad[384 + 32 * part : 416 + 32 * part], ())[:6]
 
 
-def features_kernel(near_ref, far_ref, z_out, gram_ref, b_ref, a_ref, z_ref):
+def features_kernel(own_ref, one_ref, swap_ref, both_ref, z_out, gram_ref, b_ref, a_ref, z_ref):
     mine = lax.axis_index("gy")
     chips = b_ref.shape[0]
-    for slot in range(chips):
-        b_ref[jnp.bitwise_xor(mine, slot)] = near_ref[slot] if slot < 2 else far_ref[slot - 2]
+    in_order(b_ref, mine, (own_ref, one_ref, swap_ref, both_ref))
     lane = lax.broadcasted_iota(jnp.int32, (FACE, 128), 1)
     upper = (lane // 32) % 2 == 1
     z_ref[:, 96:, :] = jnp.zeros((chips, 32, 128), jnp.float32)
@@ -425,8 +424,14 @@
         )
 
 
-def solve_kernel(total, gram_ref, z_ref, res_ref, coef_ref):
+def solve_kernel(total, own_ref, one_ref, swap_ref, both_ref, z_ref, res_ref, coef_ref, g_ref):
     core = lax.axis_index("gz")
+    in_order(g_ref, lax.axis_index("gx"), (own_ref, one_ref, swap_ref, both_ref))
+    packed = [
+        (g_ref[0, pl.ds(8 * i, 8), :] + g_ref[1, pl.ds(8 * i, 8), :])
+        + (g_ref[2, pl.ds(8 * i, 8), :] + g_ref[3, pl.ds(8 * i, 8), :])
+        for i in range(7)
+    ]
     one = jnp.where(core >= 0, 1.0, 2.0)
     count, group = 12, 2
     rows = lax.broadcasted_iota(jnp.int32, (8, 128), 0)
@@ -434,10 +439,10 @@
     half = []
     for i in range(count + 1):
         if i < 7:
-            value = gram_ref[pl.ds(8 * i, 8), :]
+            value = packed[i]
             half.append(jnp.where(lane >= rows + 8 * i, value, 0.0))
         else:
-            value = pltpu.roll(gram_ref[pl.ds(8 * i - 48, 8), :], 56, 1)
+            value = pltpu.roll(packed[i - 6], 56, 1)
             half.append(jnp.where((lane >= 56) & (lane <= rows + 8 * i), value, 0.0))
     blank = [jnp.zeros((8, 128), jnp.float32)]
     other = jnp.transpose(jnp.concatenate(half + blank * (15 - count), axis=0))
@@ -524,12 +529,22 @@
     return crosswise(value, axis, lambda chip: (chip + step) % size)
 
 
-def added_up(value, axis):
-    bit = 1
-    while bit < lax.axis_size(axis):
-        value = value + crosswise(value, axis, lambda chip: chip ^ bit)
-        bit *= 2
-    return value
+def gathered_over(value, axis):
+    pairs = []
+    for chip in range(lax.axis_size(axis)):
+        pairs += [(2 * chip, 2 * (chip ^ 1) + 1), (2 * chip + 1, 2 * (chip ^ 2))]
+    both = crosswise(value, axis, lambda chip: chip ^ 3)
+    one = lax.ppermute(value, (axis, "gz"), pairs)
+    return value, one, lax.ppermute(one, "gz", [(0, 1), (1, 0)]), both
+
+
+def in_order(target_ref, mine, refs):
+    core = lax.axis_index("gz")
+    own_ref, one_ref, swap_ref, both_ref = refs
+    target_ref[mine] = own_ref[...]
+    target_ref[jnp.bitwise_xor(mine, 2 - core)] = one_ref[...]
+    target_ref[jnp.bitwise_xor(mine, 1 + core)] = swap_ref[...]
+    target_ref[jnp.bitwise_xor(mine, 3)] = both_ref[...]
 
 
 def call(kernel, outs, scratch, place=pltpu.VMEM):
@@ -577,8 +592,7 @@
         [jnp.where(left, high, low), middle, jnp.where(left, low, high)], axis=0
     )
 
-    near = jnp.stack([own, crosswise(own, "gy", lambda chip: chip ^ 1)])
-    far = crosswise(near, "gy", lambda chip: chip ^ 2)
+    sums = gathered_over(own, "gy")
     stacked, gram = call(
         features_kernel,
         [(128, 128), (56, 128)],
@@ -587,22 +601,21 @@
             pltpu.VMEM((27 * chips, 128), wide_type),
             pltpu.VMEM((chips, 128, 128), wide_type),
         ],
-    )(near, far)
-    gram = added_up(gram, "gx")
+    )(*sums)
+    grams = gathered_over(gram, "gx")
     samples = (bx // 8) * (by // 8) * (length // 8)
     total = float(samples * lax.axis_size("gx") * chips)
     residual, coefficients = call(
-        functools.partial(solve_kernel, total), [(6, 64), (6, 96)], []
-    )(gram, stacked)
+        functools.partial(solve_kernel, total), [(6, 64), (6, 96)], [pltpu.VMEM((4, 56, 128), wide_type)]
+    )(*grams, stacked)
     return (residual, coefficients.T)
 
 
 def chip_form(mesh, velocity):
     shape = mesh.shape
     brick = (velocity.shape[1] // shape["gx"], velocity.shape[2] // shape["gy"])
-    even = shape["gx"] & (shape["gx"] - 1) == 0
     return (
-        even and shape["gy"] == 4 and shape["gz"] == 2
+        shape["gx"] == shape["gy"] == 4 and shape["gz"] == 2
         and brick == (16, 16) and velocity.shape[3] == 256
     )
 

time: 28.9 us -> 26.6 us (0.920)
  waiting for transfers between devices: 11.2 us -> 8.16 us
  starting transfers between devices: 11.3 us -> 12.2 us
    ppermute x0 -> x4, starting transfers between devices: none -> 4.58 us  [the longest x2 3.61 us: gathered_over(): one = lax.ppermute(value, (axis, 'gz'), pairs)]
    ppermute x6 -> x4, waiting for transfers between devices: 9.92 us -> 6.21 us  [crosswise(): return lax.ppermute(value, (axis, 'gz'), pairs)]
    ppermute x6 -> x4, starting transfers between devices: 11.2 us -> 7.53 us  [crosswise(): return lax.ppermute(value, (axis, 'gz'), pairs)]
    ppermute x0 -> x4, waiting for transfers between devices: none -> 0.71 us  [the longest x2 0.71 us: gathered_over(): one = lax.ppermute(value, (axis, 'gz'), pairs)]
  transfers between devices with their start and end apart: 7 -> 9, of which waited for: 6 -> 5; matrix products, arithmetic and copies ran while one was open for 0% -> 0% of each run, Pallas kernels for 0% -> 0%
where the time goes in v5:
time: 26.6 us; the launch traced here: 26.5 us
  starting transfers between devices  12.2 us (46%)
  waiting for transfers between devices  8.16 us (31%)
  Pallas kernels  5.26 us (20%)
  between operations  0.66 us (2%)
    ppermute x4, starting transfers between devices, crosswise(): return lax.ppermute(value, (axis, 'gz'), pairs)  7.53 us
    ppermute x4, waiting for transfers between devices, crosswise(): return lax.ppermute(value, (axis, 'gz'), pairs)  6.21 us
    pallas_call x3, Pallas kernels, run(): pl.pallas_call(kernel, out_shape=[jax.ShapeDtypeStruct(shape, jnp.float32...  5.26 us
    ppermute x2, starting transfers between devices, gathered_over(): one = lax.ppermute(value, (axis, 'gz'), pairs)  3.61 us
    ppermute x1, waiting for transfers between devices, chip_shards(): part = part + lax.ppermute(part, 'gz', [(0, 1), (1, 0)])  1.23 us
    ppermute x2, starting transfers between devices, gathered_over(): return (value, one, lax.ppermute(one, 'gz', [(0, 1), (1, 0)]), both)  0.97 us
    ppermute x2, waiting for transfers between devices, gathered_over(): one = lax.ppermute(value, (axis, 'gz'), pairs)  0.71 us
  transfers between devices with their start and end apart: 9, of which 5 were waited for; matrix products, arithmetic and copies ran while one was open for 0% of the time, Pallas kernels for 0%

profile of v5, /device:TPU:1, one launch (start us, length us, event | category | flops | bytes accessed | tf_op | source)
XLA Modules:
  0.0 26.5 jit_solution(12554254914696926316)
XLA Ops:
  0.6 1.9 %shard_map.68 = f32[120,128]{1,0:T(8,128)S(1)} custom-call(f32[3,16,16,128]{3,2,1,0:T(8,128)} %x_hbm.1, bf16[160,256]{1,0:T(8,128)(2,1)} %constant.12.clone.wv_hbm, bf16[32,256]{1,0:T(8,128)(2,1)} %constant.13.clone.wp_hbm, bf16[256,128]{1,0:T(8,128)(2,1)} %constant.14.clone.la_hbm, bf16[256,128]{1,0:T(8,128)(2,1)} %constant.15.clone.lb_hbm), custom_call_target="tpu_custom_call" | custom-call | tf_op jit(solution)/shard_map/pallas_call | solution.py:552
  2.5 0.1 collective-permute-start
  2.6 1.2 %collective-permute-done = f32[120,128]{1,0:T(8,128)S(1)} collective-permute-done((f32[120,128]{1,0:T(8,128)S(1)}, f32[120,128]{1,0:T(8,128)S(1)}, u32[]{:S(2)}, u32[]{:S(2)}) %collective-permute-start) | collective-permute-done | bytes 61472 | tf_op jit(solution)/shard_map/ppermute | solution.py:585
  3.8 2.7 %collective-permute-start.1 = (f32[24,128]{1,0:T(8,128)S(1)}, f32[24,128]{1,0:T(8,128)S(1)}, u32[]{:S(2)}, u32[]{:S(2)}) collective-permute-start(f32[24,128]{1,0:T(8,128)S(1)} %get-tuple-element.10), channel_id=1, source_target_pairs={{0,9},{1,8},{8,17},{9,16},{16,25},{17,24},{24,1},{25,0},{2,11},{3,... | collective-permute-start | bytes 36872 | tf_op jit(solution)/shard_map/ppermute | solution.py:524
  6.6 2.1 %collective-permute-start.2 = (f32[24,128]{1,0:T(8,128)S(1)}, f32[24,128]{1,0:T(8,128)S(1)}, u32[]{:S(2)}, u32[]{:S(2)}) collective-permute-start(f32[24,128]{1,0:T(8,128)S(1)} %get-tuple-element.11), channel_id=1, source_target_pairs={{0,25},{1,24},{8,1},{9,0},{16,9},{17,8},{24,17},{25,16},{2,27},{3,... | collective-permute-start | bytes 36872 | tf_op jit(solution)/shard_map/ppermute | solution.py:524
  8.7 0.1 pad.1.clone
  8.7 1.2 %collective-permute-done.1 = f32[24,128]{1,0:T(8,128)S(1)} collective-permute-done((f32[24,128]{1,0:T(8,128)S(1)}, f32[24,128]{1,0:T(8,128)S(1)}, u32[]{:S(2)}, u32[]{:S(2)}) %collective-permute-start.1) | collective-permute-done | bytes 12320 | tf_op jit(solution)/shard_map/ppermute | solution.py:524
  10.0 0.0 collective-permute-done.2
  10.0 0.1 slice_add_fusion.own_ref
  10.1 1.5 %collective-permute-start.3 = (f32[72,128]{1,0:T(8,128)S(1)}, f32[72,128]{1,0:T(8,128)S(1)}, u32[]{:S(2)}, u32[]{:S(2)}) collective-permute-start(f32[72,128]{1,0:T(8,128)S(1)} %slice_add_fusion.own_ref), channel_id=1, source_target_pairs={{0,3},{1,4},{2,1},{3,6},{4,7},{5,0},{6,5},{7,2},{8,11},{9,12},{10,... | collective-permute-start | bytes 110600 | tf_op jit(solution)/shard_map/ppermute | solution.py:537
  11.6 1.2 %collective-permute-start.5 = (f32[72,128]{1,0:T(8,128)S(1)}, f32[72,128]{1,0:T(8,128)S(1)}, u32[]{:S(2)}, u32[]{:S(2)}) collective-permute-start(f32[72,128]{1,0:T(8,128)S(1)} %slice_add_fusion.own_ref), channel_id=1, source_target_pairs={{0,7},{1,6},{2,5},{3,4},{4,3},{5,2},{6,1},{7,0},{8,15},{9,14},{10,... | collective-permute-start | bytes 110600 | tf_op jit(solution)/shard_map/ppermute | solution.py:524
  12.8 0.7 %collective-permute-done.3.one_ref = f32[72,128]{1,0:T(8,128)S(1)} collective-permute-done((f32[72,128]{1,0:T(8,128)S(1)}, f32[72,128]{1,0:T(8,128)S(1)}, u32[]{:S(2)}, u32[]{:S(2)}) %collective-permute-start.3) | collective-permute-done | bytes 36896 | tf_op jit(solution)/shard_map/ppermute | solution.py:537
  13.5 0.2 collective-permute-start.4
  13.7 2.1 %collective-permute-done.5.both_ref = f32[72,128]{1,0:T(8,128)S(1)} collective-permute-done((f32[72,128]{1,0:T(8,128)S(1)}, f32[72,128]{1,0:T(8,128)S(1)}, u32[]{:S(2)}, u32[]{:S(2)}) %collective-permute-start.5) | collective-permute-done | bytes 36896 | tf_op jit(solution)/shard_map/ppermute | solution.py:524
  15.8 0.0 collective-permute-done.4.swap_ref
  15.8 0.6 %shard_map.69 = (f32[128,128]{1,0:T(8,128)S(1)}, f32[56,128]{1,0:T(8,128)S(1)}) custom-call(f32[72,128]{1,0:T(8,128)S(1)} %slice_add_fusion.own_ref, f32[72,128]{1,0:T(8,128)S(1)} %collective-permute-done.3.one_ref, f32[72,128]{1,0:T(8,128)S(1)} %collective-permute-done.4.swap_ref, f32[72,128]{1,0:T(8,128)S(1)} %collective-permute-done.5.both_ref), custom_call_target="tpu_custom_call" | custom-call | tf_op jit(solution)/shard_map/pallas_call | solution.py:552
  16.5 2.1 %collective-permute-start.6 = (f32[56,128]{1,0:T(8,128)S(1)}, f32[56,128]{1,0:T(8,128)S(1)}, u32[]{:S(2)}, u32[]{:S(2)}) collective-permute-start(f32[56,128]{1,0:T(8,128)S(1)} %get-tuple-element.6.own_ref), channel_id=1, source_target_pairs={{0,9},{1,16},{8,1},{9,24},{16,25},{17,0},{24,17},{25,8},{2,11},{3,... | collective-permute-start | bytes 86024 | tf_op jit(solution)/shard_map/ppermute | solution.py:537
  18.6 1.5 %collective-permute-start.8 = (f32[56,128]{1,0:T(8,128)S(1)}, f32[56,128]{1,0:T(8,128)S(1)}, u32[]{:S(2)}, u32[]{:S(2)}) collective-permute-start(f32[56,128]{1,0:T(8,128)S(1)} %get-tuple-element.6.own_ref), channel_id=1, source_target_pairs={{0,25},{1,24},{8,17},{9,16},{16,9},{17,8},{24,1},{25,0},{2,27},{3,... | collective-permute-start | bytes 86024 | tf_op jit(solution)/shard_map/ppermute | solution.py:524
  20.1 0.0 collective-permute-done.6.one_ref
  20.1 0.7 %collective-permute-start.7 = (f32[56,128]{1,0:T(8,128)S(1)}, f32[56,128]{1,0:T(8,128)S(1)}, u32[]{:S(2)}, u32[]{:S(2)}) collective-permute-start(f32[56,128]{1,0:T(8,128)S(1)} %collective-permute-done.6.one_ref), channel_id=1, source_target_pairs={{0,1},{1,0},{2,3},{3,2},{4,5},{5,4},{6,7},{7,6},{8,9},{9,8},{10,11... | collective-permute-start | bytes 86024 | tf_op jit(solution)/shard_map/ppermute | solution.py:538
  20.9 2.8 %collective-permute-done.8.both_ref = f32[56,128]{1,0:T(8,128)S(1)} collective-permute-done((f32[56,128]{1,0:T(8,128)S(1)}, f32[56,128]{1,0:T(8,128)S(1)}, u32[]{:S(2)}, u32[]{:S(2)}) %collective-permute-start.8) | collective-permute-done | bytes 28704 | tf_op jit(solution)/shard_map/ppermute | solution.py:524
  23.7 0.0 collective-permute-done.7.swap_ref
  23.7 2.7 %shard_map.70 = (f32[6,64]{1,0:T(8,128)}, f32[6,96]{1,0:T(8,128)}) custom-call(f32[56,128]{1,0:T(8,128)S(1)} %get-tuple-element.6.own_ref, f32[56,128]{1,0:T(8,128)S(1)} %collective-permute-done.6.one_ref, f32[56,128]{1,0:T(8,128)S(1)} %collective-permute-done.7.swap_ref, f32[56,128]{1,0:T(8,128)S(1)} %collective-permute-done.8.both_ref, ...), custom_call_target="tpu_custom_call" | custom-call | tf_op jit(solution)/shard_map/pallas_call | solution.py:552
  (5 shorter events, 0.0 us)
Async XLA Ops:
  2.5 1.3 %collective-permute-start = (f32[120,128]{1,0:T(8,128)S(1)}, f32[120,128]{1,0:T(8,128)S(1)}, u32[]{:S(2)}, u32[]{:S(2)}) collective-permute-start(f32[120,128]{1,0:T(8,128)S(1)} %shard_map.68), channel_id=1, source_target_pairs={{0,1},{1,0},{2,3},{3,2},{4,5},{5,4},{6,7},{7,6},{8,9},{9,8},{10,11... | collective-permute-start | bytes 184328 | tf_op jit(solution)/shard_map/ppermute | solution.py:585
  3.8 6.1 %collective-permute-start.1 = (f32[24,128]{1,0:T(8,128)S(1)}, f32[24,128]{1,0:T(8,128)S(1)}, u32[]{:S(2)}, u32[]{:S(2)}) collective-permute-start(f32[24,128]{1,0:T(8,128)S(1)} %get-tuple-element.10), channel_id=1, source_target_pairs={{0,9},{1,8},{8,17},{9,16},{16,25},{17,24},{24,1},{25,0},{2,11},{3,... | collective-permute-start | bytes 36872 | tf_op jit(solution)/shard_map/ppermute | solution.py:524
  6.6 3.4 %collective-permute-start.2 = (f32[24,128]{1,0:T(8,128)S(1)}, f32[24,128]{1,0:T(8,128)S(1)}, u32[]{:S(2)}, u32[]{:S(2)}) collective-permute-start(f32[24,128]{1,0:T(8,128)S(1)} %get-tuple-element.11), channel_id=1, source_target_pairs={{0,25},{1,24},{8,1},{9,0},{16,9},{17,8},{24,17},{25,16},{2,27},{3,... | collective-permute-start | bytes 36872 | tf_op jit(solution)/shard_map/ppermute | solution.py:524
  10.1 3.4 %collective-permute-start.3 = (f32[72,128]{1,0:T(8,128)S(1)}, f32[72,128]{1,0:T(8,128)S(1)}, u32[]{:S(2)}, u32[]{:S(2)}) collective-permute-start(f32[72,128]{1,0:T(8,128)S(1)} %slice_add_fusion.own_ref), channel_id=1, source_target_pairs={{0,3},{1,4},{2,1},{3,6},{4,7},{5,0},{6,5},{7,2},{8,11},{9,12},{10,... | collective-permute-start | bytes 110600 | tf_op jit(solution)/shard_map/ppermute | solution.py:537
  11.6 4.3 %collective-permute-start.5 = (f32[72,128]{1,0:T(8,128)S(1)}, f32[72,128]{1,0:T(8,128)S(1)}, u32[]{:S(2)}, u32[]{:S(2)}) collective-permute-start(f32[72,128]{1,0:T(8,128)S(1)} %slice_add_fusion.own_ref), channel_id=1, source_target_pairs={{0,7},{1,6},{2,5},{3,4},{4,3},{5,2},{6,1},{7,0},{8,15},{9,14},{10,... | collective-permute-start | bytes 110600 | tf_op jit(solution)/shard_map/ppermute | solution.py:524
  13.5 2.4 %collective-permute-start.4 = (f32[72,128]{1,0:T(8,128)S(1)}, f32[72,128]{1,0:T(8,128)S(1)}, u32[]{:S(2)}, u32[]{:S(2)}) collective-permute-start(f32[72,128]{1,0:T(8,128)S(1)} %collective-permute-done.3.one_ref), channel_id=1, source_target_pairs={{0,1},{1,0},{2,3},{3,2},{4,5},{5,4},{6,7},{7,6},{8,9},{9,8},{10,11... | collective-permute-start | bytes 110600 | tf_op jit(solution)/shard_map/ppermute | solution.py:538
  16.5 3.6 %collective-permute-start.6 = (f32[56,128]{1,0:T(8,128)S(1)}, f32[56,128]{1,0:T(8,128)S(1)}, u32[]{:S(2)}, u32[]{:S(2)}) collective-permute-start(f32[56,128]{1,0:T(8,128)S(1)} %get-tuple-element.6.own_ref), channel_id=1, source_target_pairs={{0,9},{1,16},{8,1},{9,24},{16,25},{17,0},{24,17},{25,8},{2,11},{3,... | collective-permute-start | bytes 86024 | tf_op jit(solution)/shard_map/ppermute | solution.py:537
  18.6 5.1 %collective-permute-start.8 = (f32[56,128]{1,0:T(8,128)S(1)}, f32[56,128]{1,0:T(8,128)S(1)}, u32[]{:S(2)}, u32[]{:S(2)}) collective-permute-start(f32[56,128]{1,0:T(8,128)S(1)} %get-tuple-element.6.own_ref), channel_id=1, source_target_pairs={{0,25},{1,24},{8,17},{9,16},{16,9},{17,8},{24,1},{25,0},{2,27},{3,... | collective-permute-start | bytes 86024 | tf_op jit(solution)/shard_map/ppermute | solution.py:524
  20.1 3.6 %collective-permute-start.7 = (f32[56,128]{1,0:T(8,128)S(1)}, f32[56,128]{1,0:T(8,128)S(1)}, u32[]{:S(2)}, u32[]{:S(2)}) collective-permute-start(f32[56,128]{1,0:T(8,128)S(1)} %collective-permute-done.6.one_ref), channel_id=1, source_target_pairs={{0,1},{1,0},{2,3},{3,2},{4,5},{5,4},{6,7},{7,6},{8,9},{9,8},{10,11... | collective-permute-start | bytes 86024 | tf_op jit(solution)/shard_map/ppermute | solution.py:538

commit v6 on v5

--- a/solution.py
+++ b/solution.py
@@ -281,14 +281,14 @@
     def gathered(groups, blocks):
         total = jnp.zeros((8, 128), jnp.float32)
         for place in range(4):
-            base = merged = groups[8 * place : 8 * place + 8]
+            base = groups[8 * place : 8 * place + 8]
+            merged = pltpu.roll(base, 32 * place, 1) if place else base
             for block, chosen in blocks:
                 hit = rows == chosen[0]
                 for row in chosen[1:]:
                     hit = hit | (rows == row)
-                merged = jnp.where(hit, pltpu.roll(base, 128 - 32 * block, 1), merged)
-            if place:
-                merged = pltpu.roll(merged, 32 * place, 1)
+                turn = 32 * (place - block) % 128
+                merged = jnp.where(hit, pltpu.roll(base, turn, 1) if turn else base, merged)
             total = jnp.where(lanes == place, merged, total)
         return total
 
@@ -349,7 +349,7 @@
 def features_kernel(own_ref, one_ref, swap_ref, both_ref, z_out, gram_ref, b_ref, a_ref, z_ref):
     mine = lax.axis_index("gy")
     chips = b_ref.shape[0]
-    in_order(b_ref, mine, (own_ref, one_ref, swap_ref, both_ref))
+    in_order(b_ref, mine, (own_ref, one_ref, swap_ref, both_ref), False)
     lane = lax.broadcasted_iota(jnp.int32, (FACE, 128), 1)
     upper = (lane // 32) % 2 == 1
     z_ref[:, 96:, :] = jnp.zeros((chips, 32, 128), jnp.float32)
@@ -426,7 +426,7 @@
 
 def solve_kernel(total, own_ref, one_ref, swap_ref, both_ref, z_ref, res_ref, coef_ref, g_ref):
     core = lax.axis_index("gz")
-    in_order(g_ref, lax.axis_index("gx"), (own_ref, one_ref, swap_ref, both_ref))
+    in_order(g_ref, lax.axis_index("gx"), (own_ref, one_ref, swap_ref, both_ref), True)
     packed = [
         (g_ref[0, pl.ds(8 * i, 8), :] + g_ref[1, pl.ds(8 * i, 8), :])
         + (g_ref[2, pl.ds(8 * i, 8), :] + g_ref[3, pl.ds(8 * i, 8), :])
@@ -529,21 +529,25 @@
     return crosswise(value, axis, lambda chip: (chip + step) % size)
 
 
-def gathered_over(value, axis):
+def gathered_over(value, axis, straight):
     pairs = []
     for chip in range(lax.axis_size(axis)):
-        pairs += [(2 * chip, 2 * (chip ^ 1) + 1), (2 * chip + 1, 2 * (chip ^ 2))]
+        if straight:
+            pairs += [(2 * chip, 2 * (chip ^ 1)), (2 * chip + 1, 2 * (chip ^ 2) + 1)]
+        else:
+            pairs += [(2 * chip, 2 * (chip ^ 1) + 1), (2 * chip + 1, 2 * (chip ^ 2))]
     both = crosswise(value, axis, lambda chip: chip ^ 3)
     one = lax.ppermute(value, (axis, "gz"), pairs)
     return value, one, lax.ppermute(one, "gz", [(0, 1), (1, 0)]), both
 
 
-def in_order(target_ref, mine, refs):
+def in_order(target_ref, mine, refs, straight):
     core = lax.axis_index("gz")
+    first = 1 + core if straight else 2 - core
     own_ref, one_ref, swap_ref, both_ref = refs
     target_ref[mine] = own_ref[...]
-    target_ref[jnp.bitwise_xor(mine, 2 - core)] = one_ref[...]
-    target_ref[jnp.bitwise_xor(mine, 1 + core)] = swap_ref[...]
+    target_ref[jnp.bitwise_xor(mine, first)] = one_ref[...]
+    target_ref[jnp.bitwise_xor(mine, 3 - first)] = swap_ref[...]
     target_ref[jnp.bitwise_xor(mine, 3)] = both_ref[...]
 
 
@@ -592,7 +596,7 @@
         [jnp.where(left, high, low), middle, jnp.where(left, low, high)], axis=0
     )
 
-    sums = gathered_over(own, "gy")
+    sums = gathered_over(own, "gy", False)
     stacked, gram = call(
         features_kernel,
         [(128, 128), (56, 128)],
@@ -602,7 +606,7 @@
             pltpu.VMEM((chips, 128, 128), wide_type),
         ],
     )(*sums)
-    grams = gathered_over(gram, "gx")
+    grams = gathered_over(gram, "gx", True)
     samples = (bx // 8) * (by // 8) * (length // 8)
     total = float(samples * lax.axis_size("gx") * chips)
     residual, coefficients = call(

time: 26.6 us -> 26.4 us (level)
  starting transfers between devices: 12.2 us -> 11.9 us
    ppermute x2, starting transfers between devices: 0.97 us -> 0.62 us  [gathered_over(): return (value, one, lax.ppermute(one, 'gz', [(0, 1), (1, 0)]), both)]
  transfers between devices with their start and end apart: 9 -> 9, of which waited for: 5 -> 6; matrix products, arithmetic and copies ran while one was open for 0% -> 0% of each run, Pallas kernels for 0% -> 0%
where the time goes in v6:
time: 26.4 us; the launch traced here: 26.2 us
  starting transfers between devices  11.9 us (45%)
  waiting for transfers between devices  8.31 us (31%)
  Pallas kernels  5.2 us (20%)
  between operations  0.66 us (2%)
    ppermute x4, starting transfers between devices, crosswise(): return lax.ppermute(value, (axis, 'gz'), pairs)  7.75 us
    ppermute x4, waiting for transfers between devices, crosswise(): return lax.ppermute(value, (axis, 'gz'), pairs)  6.33 us
    pallas_call x3, Pallas kernels, run(): pl.pallas_call(kernel, out_shape=[jax.ShapeDtypeStruct(shape, jnp.float32...  5.2 us
    ppermute x2, starting transfers between devices, gathered_over(): one = lax.ppermute(value, (axis, 'gz'), pairs)  3.4 us
    ppermute x1, waiting for transfers between devices, chip_shards(): part = part + lax.ppermute(part, 'gz', [(0, 1), (1, 0)])  1.23 us
    ppermute x2, waiting for transfers between devices, gathered_over(): one = lax.ppermute(value, (axis, 'gz'), pairs)  0.74 us
    ppermute x2, starting transfers between devices, gathered_over(): return (value, one, lax.ppermute(one, 'gz', [(0, 1), (1, 0)]), both)  0.62 us
  transfers between devices with their start and end apart: 9, of which 6 were waited for; matrix products, arithmetic and copies ran while one was open for 0% of the time, Pallas kernels for 0%

profile of v6, /device:TPU:1, one launch (start us, length us, event | category | flops | bytes accessed | tf_op | source)
XLA Modules:
  0.0 26.2 jit_solution(5148093132537907428)
XLA Ops:
  0.6 1.8 %shard_map.68 = f32[120,128]{1,0:T(8,128)S(1)} custom-call(f32[3,16,16,128]{3,2,1,0:T(8,128)} %x_hbm.1, bf16[160,256]{1,0:T(8,128)(2,1)} %constant.12.clone.wv_hbm, bf16[32,256]{1,0:T(8,128)(2,1)} %constant.13.clone.wp_hbm, bf16[256,128]{1,0:T(8,128)(2,1)} %constant.14.clone.la_hbm, bf16[256,128]{1,0:T(8,128)(2,1)} %constant.15.clone.lb_hbm), custom_call_target="tpu_custom_call" | custom-call | tf_op jit(solution)/shard_map/pallas_call | solution.py:556
  2.4 0.1 collective-permute-start
  2.5 1.2 %collective-permute-done = f32[120,128]{1,0:T(8,128)S(1)} collective-permute-done((f32[120,128]{1,0:T(8,128)S(1)}, f32[120,128]{1,0:T(8,128)S(1)}, u32[]{:S(2)}, u32[]{:S(2)}) %collective-permute-start) | collective-permute-done | bytes 61472 | tf_op jit(solution)/shard_map/ppermute | solution.py:589
  3.8 2.7 %collective-permute-start.1 = (f32[24,128]{1,0:T(8,128)S(1)}, f32[24,128]{1,0:T(8,128)S(1)}, u32[]{:S(2)}, u32[]{:S(2)}) collective-permute-start(f32[24,128]{1,0:T(8,128)S(1)} %get-tuple-element.10), channel_id=1, source_target_pairs={{0,9},{1,8},{8,17},{9,16},{16,25},{17,24},{24,1},{25,0},{2,11},{3,... | collective-permute-start | bytes 36872 | tf_op jit(solution)/shard_map/ppermute | solution.py:524
  6.5 2.1 %collective-permute-start.2 = (f32[24,128]{1,0:T(8,128)S(1)}, f32[24,128]{1,0:T(8,128)S(1)}, u32[]{:S(2)}, u32[]{:S(2)}) collective-permute-start(f32[24,128]{1,0:T(8,128)S(1)} %get-tuple-element.11), channel_id=1, source_target_pairs={{0,25},{1,24},{8,1},{9,0},{16,9},{17,8},{24,17},{25,16},{2,27},{3,... | collective-permute-start | bytes 36872 | tf_op jit(solution)/shard_map/ppermute | solution.py:524
  8.6 0.1 pad.1.clone
  8.7 1.2 %collective-permute-done.1 = f32[24,128]{1,0:T(8,128)S(1)} collective-permute-done((f32[24,128]{1,0:T(8,128)S(1)}, f32[24,128]{1,0:T(8,128)S(1)}, u32[]{:S(2)}, u32[]{:S(2)}) %collective-permute-start.1) | collective-permute-done | bytes 12320 | tf_op jit(solution)/shard_map/ppermute | solution.py:524
  9.9 0.0 collective-permute-done.2
  9.9 0.1 slice_add_fusion.own_ref
  10.0 1.5 %collective-permute-start.3 = (f32[72,128]{1,0:T(8,128)S(1)}, f32[72,128]{1,0:T(8,128)S(1)}, u32[]{:S(2)}, u32[]{:S(2)}) collective-permute-start(f32[72,128]{1,0:T(8,128)S(1)} %slice_add_fusion.own_ref), channel_id=1, source_target_pairs={{0,3},{1,4},{2,1},{3,6},{4,7},{5,0},{6,5},{7,2},{8,11},{9,12},{10,... | collective-permute-start | bytes 110600 | tf_op jit(solution)/shard_map/ppermute | solution.py:540
  11.5 1.2 %collective-permute-start.5 = (f32[72,128]{1,0:T(8,128)S(1)}, f32[72,128]{1,0:T(8,128)S(1)}, u32[]{:S(2)}, u32[]{:S(2)}) collective-permute-start(f32[72,128]{1,0:T(8,128)S(1)} %slice_add_fusion.own_ref), channel_id=1, source_target_pairs={{0,7},{1,6},{2,5},{3,4},{4,3},{5,2},{6,1},{7,0},{8,15},{9,14},{10,... | collective-permute-start | bytes 110600 | tf_op jit(solution)/shard_map/ppermute | solution.py:524
  12.7 0.7 %collective-permute-done.3.one_ref = f32[72,128]{1,0:T(8,128)S(1)} collective-permute-done((f32[72,128]{1,0:T(8,128)S(1)}, f32[72,128]{1,0:T(8,128)S(1)}, u32[]{:S(2)}, u32[]{:S(2)}) %collective-permute-start.3) | collective-permute-done | bytes 36896 | tf_op jit(solution)/shard_map/ppermute | solution.py:540
  13.4 0.2 collective-permute-start.4
  13.6 2.1 %collective-permute-done.5.both_ref = f32[72,128]{1,0:T(8,128)S(1)} collective-permute-done((f32[72,128]{1,0:T(8,128)S(1)}, f32[72,128]{1,0:T(8,128)S(1)}, u32[]{:S(2)}, u32[]{:S(2)}) %collective-permute-start.5) | collective-permute-done | bytes 36896 | tf_op jit(solution)/shard_map/ppermute | solution.py:524
  15.8 0.0 collective-permute-done.4.swap_ref
  15.8 0.6 %shard_map.69 = (f32[128,128]{1,0:T(8,128)S(1)}, f32[56,128]{1,0:T(8,128)S(1)}) custom-call(f32[72,128]{1,0:T(8,128)S(1)} %slice_add_fusion.own_ref, f32[72,128]{1,0:T(8,128)S(1)} %collective-permute-done.3.one_ref, f32[72,128]{1,0:T(8,128)S(1)} %collective-permute-done.4.swap_ref, f32[72,128]{1,0:T(8,128)S(1)} %collective-permute-done.5.both_ref), custom_call_target="tpu_custom_call" | custom-call | tf_op jit(solution)/shard_map/pallas_call | solution.py:556
  16.4 1.9 %collective-permute-start.6 = (f32[56,128]{1,0:T(8,128)S(1)}, f32[56,128]{1,0:T(8,128)S(1)}, u32[]{:S(2)}, u32[]{:S(2)}) collective-permute-start(f32[56,128]{1,0:T(8,128)S(1)} %get-tuple-element.6.own_ref), channel_id=1, source_target_pairs={{0,8},{1,17},{8,0},{9,25},{16,24},{17,1},{24,16},{25,9},{2,10},{3,... | collective-permute-start | bytes 86024 | tf_op jit(solution)/shard_map/ppermute | solution.py:540
  18.3 1.7 %collective-permute-start.8 = (f32[56,128]{1,0:T(8,128)S(1)}, f32[56,128]{1,0:T(8,128)S(1)}, u32[]{:S(2)}, u32[]{:S(2)}) collective-permute-start(f32[56,128]{1,0:T(8,128)S(1)} %get-tuple-element.6.own_ref), channel_id=1, source_target_pairs={{0,25},{1,24},{8,17},{9,16},{16,9},{17,8},{24,1},{25,0},{2,27},{3,... | collective-permute-start | bytes 86024 | tf_op jit(solution)/shard_map/ppermute | solution.py:524
  20.0 0.1 collective-permute-done.6.one_ref
  20.1 0.4 %collective-permute-start.7 = (f32[56,128]{1,0:T(8,128)S(1)}, f32[56,128]{1,0:T(8,128)S(1)}, u32[]{:S(2)}, u32[]{:S(2)}) collective-permute-start(f32[56,128]{1,0:T(8,128)S(1)} %collective-permute-done.6.one_ref), channel_id=1, source_target_pairs={{0,1},{1,0},{2,3},{3,2},{4,5},{5,4},{6,7},{7,6},{8,9},{9,8},{10,11... | collective-permute-start | bytes 86024 | tf_op jit(solution)/shard_map/ppermute | solution.py:541
  20.5 3.0 %collective-permute-done.8.both_ref = f32[56,128]{1,0:T(8,128)S(1)} collective-permute-done((f32[56,128]{1,0:T(8,128)S(1)}, f32[56,128]{1,0:T(8,128)S(1)}, u32[]{:S(2)}, u32[]{:S(2)}) %collective-permute-start.8) | collective-permute-done | bytes 28704 | tf_op jit(solution)/shard_map/ppermute | solution.py:524
  23.5 0.0 collective-permute-done.7.swap_ref
  23.5 2.7 %shard_map.70 = (f32[6,64]{1,0:T(8,128)}, f32[6,96]{1,0:T(8,128)}) custom-call(f32[56,128]{1,0:T(8,128)S(1)} %get-tuple-element.6.own_ref, f32[56,128]{1,0:T(8,128)S(1)} %collective-permute-done.6.one_ref, f32[56,128]{1,0:T(8,128)S(1)} %collective-permute-done.7.swap_ref, f32[56,128]{1,0:T(8,128)S(1)} %collective-permute-done.8.both_ref, ...), custom_call_target="tpu_custom_call" | custom-call | tf_op jit(solution)/shard_map/pallas_call | solution.py:556
  (5 shorter events, 0.0 us)
Async XLA Ops:
  2.4 1.3 %collective-permute-start = (f32[120,128]{1,0:T(8,128)S(1)}, f32[120,128]{1,0:T(8,128)S(1)}, u32[]{:S(2)}, u32[]{:S(2)}) collective-permute-start(f32[120,128]{1,0:T(8,128)S(1)} %shard_map.68), channel_id=1, source_target_pairs={{0,1},{1,0},{2,3},{3,2},{4,5},{5,4},{6,7},{7,6},{8,9},{9,8},{10,11... | collective-permute-start | bytes 184328 | tf_op jit(solution)/shard_map/ppermute | solution.py:589
  3.8 6.1 %collective-permute-start.1 = (f32[24,128]{1,0:T(8,128)S(1)}, f32[24,128]{1,0:T(8,128)S(1)}, u32[]{:S(2)}, u32[]{:S(2)}) collective-permute-start(f32[24,128]{1,0:T(8,128)S(1)} %get-tuple-element.10), channel_id=1, source_target_pairs={{0,9},{1,8},{8,17},{9,16},{16,25},{17,24},{24,1},{25,0},{2,11},{3,... | collective-permute-start | bytes 36872 | tf_op jit(solution)/shard_map/ppermute | solution.py:524
  6.5 3.4 %collective-permute-start.2 = (f32[24,128]{1,0:T(8,128)S(1)}, f32[24,128]{1,0:T(8,128)S(1)}, u32[]{:S(2)}, u32[]{:S(2)}) collective-permute-start(f32[24,128]{1,0:T(8,128)S(1)} %get-tuple-element.11), channel_id=1, source_target_pairs={{0,25},{1,24},{8,1},{9,0},{16,9},{17,8},{24,17},{25,16},{2,27},{3,... | collective-permute-start | bytes 36872 | tf_op jit(solution)/shard_map/ppermute | solution.py:524
  10.0 3.4 %collective-permute-start.3 = (f32[72,128]{1,0:T(8,128)S(1)}, f32[72,128]{1,0:T(8,128)S(1)}, u32[]{:S(2)}, u32[]{:S(2)}) collective-permute-start(f32[72,128]{1,0:T(8,128)S(1)} %slice_add_fusion.own_ref), channel_id=1, source_target_pairs={{0,3},{1,4},{2,1},{3,6},{4,7},{5,0},{6,5},{7,2},{8,11},{9,12},{10,... | collective-permute-start | bytes 110600 | tf_op jit(solution)/shard_map/ppermute | solution.py:540
  11.5 4.3 %collective-permute-start.5 = (f32[72,128]{1,0:T(8,128)S(1)}, f32[72,128]{1,0:T(8,128)S(1)}, u32[]{:S(2)}, u32[]{:S(2)}) collective-permute-start(f32[72,128]{1,0:T(8,128)S(1)} %slice_add_fusion.own_ref), channel_id=1, source_target_pairs={{0,7},{1,6},{2,5},{3,4},{4,3},{5,2},{6,1},{7,0},{8,15},{9,14},{10,... | collective-permute-start | bytes 110600 | tf_op jit(solution)/shard_map/ppermute | solution.py:524
  13.4 2.4 %collective-permute-start.4 = (f32[72,128]{1,0:T(8,128)S(1)}, f32[72,128]{1,0:T(8,128)S(1)}, u32[]{:S(2)}, u32[]{:S(2)}) collective-permute-start(f32[72,128]{1,0:T(8,128)S(1)} %collective-permute-done.3.one_ref), channel_id=1, source_target_pairs={{0,1},{1,0},{2,3},{3,2},{4,5},{5,4},{6,7},{7,6},{8,9},{9,8},{10,11... | collective-permute-start | bytes 110600 | tf_op jit(solution)/shard_map/ppermute | solution.py:541
  16.4 3.7 %collective-permute-start.6 = (f32[56,128]{1,0:T(8,128)S(1)}, f32[56,128]{1,0:T(8,128)S(1)}, u32[]{:S(2)}, u32[]{:S(2)}) collective-permute-start(f32[56,128]{1,0:T(8,128)S(1)} %get-tuple-element.6.own_ref), channel_id=1, source_target_pairs={{0,8},{1,17},{8,0},{9,25},{16,24},{17,1},{24,16},{25,9},{2,10},{3,... | collective-permute-start | bytes 86024 | tf_op jit(solution)/shard_map/ppermute | solution.py:540
  18.3 5.1 %collective-permute-start.8 = (f32[56,128]{1,0:T(8,128)S(1)}, f32[56,128]{1,0:T(8,128)S(1)}, u32[]{:S(2)}, u32[]{:S(2)}) collective-permute-start(f32[56,128]{1,0:T(8,128)S(1)} %get-tuple-element.6.own_ref), channel_id=1, source_target_pairs={{0,25},{1,24},{8,17},{9,16},{16,9},{17,8},{24,1},{25,0},{2,27},{3,... | collective-permute-start | bytes 86024 | tf_op jit(solution)/shard_map/ppermute | solution.py:524
  20.1 3.3 %collective-permute-start.7 = (f32[56,128]{1,0:T(8,128)S(1)}, f32[56,128]{1,0:T(8,128)S(1)}, u32[]{:S(2)}, u32[]{:S(2)}) collective-permute-start(f32[56,128]{1,0:T(8,128)S(1)} %collective-permute-done.6.one_ref), channel_id=1, source_target_pairs={{0,1},{1,0},{2,3},{3,2},{4,5},{5,4},{6,7},{7,6},{8,9},{9,8},{10,11... | collective-permute-start | bytes 86024 | tf_op jit(solution)/shard_map/ppermute | solution.py:541

commit v7 on v6

--- a/solution.py
+++ b/solution.py
@@ -272,7 +272,7 @@
     copies += [pltpu.make_async_copy(wp_hbm, wp, sems.at[4])]
     copies += [pltpu.make_async_copy(la_hbm.at[pl.ds(begin, length)], la, sems.at[5])]
     copies += [pltpu.make_async_copy(lb_hbm.at[pl.ds(begin, length)], lb, sems.at[6])]
-    for copy in copies:
+    for copy in copies[1:4] + copies[:1] + copies[4:]:
         copy.start()
     rows = lax.broadcasted_iota(jnp.int32, (8, 128), 0)
     lanes = lax.broadcasted_iota(jnp.int32, (8, 128), 1) // 32

time: 26.4 us -> 26.4 us (level)
  no operation moved by 1% of the time
where the time goes in v7:
time: 26.4 us; the launch traced here: 26.2 us
  starting transfers between devices  11.8 us (45%)
  waiting for transfers between devices  8.31 us (31%)
  Pallas kernels  5.21 us (20%)
  between operations  0.66 us (2%)
    ppermute x4, starting transfers between devices, crosswise(): return lax.ppermute(value, (axis, 'gz'), pairs)  7.75 us
    ppermute x4, waiting for transfers between devices, crosswise(): return lax.ppermute(value, (axis, 'gz'), pairs)  6.34 us
    pallas_call x3, Pallas kernels, run(): pl.pallas_call(kernel, out_shape=[jax.ShapeDtypeStruct(shape, jnp.float32...  5.21 us
    ppermute x2, starting transfers between devices, gathered_over(): one = lax.ppermute(value, (axis, 'gz'), pairs)  3.41 us
    ppermute x1, waiting for transfers between devices, chip_shards(): part = part + lax.ppermute(part, 'gz', [(0, 1), (1, 0)])  1.23 us
    ppermute x2, waiting for transfers between devices, gathered_over(): one = lax.ppermute(value, (axis, 'gz'), pairs)  0.74 us
    ppermute x2, starting transfers between devices, gathered_over(): return (value, one, lax.ppermute(one, 'gz', [(0, 1), (1, 0)]), both)  0.61 us
  transfers between devices with their start and end apart: 9, of which 6 were waited for; matrix products, arithmetic and copies ran while one was open for 0% of the time, Pallas kernels for 0%

profile of v7, /device:TPU:1, one launch (start us, length us, event | category | flops | bytes accessed | tf_op | source)
XLA Modules:
  0.0 26.2 jit_solution(4114261426215103487)
XLA Ops:
  0.6 1.8 %shard_map.68 = f32[120,128]{1,0:T(8,128)S(1)} custom-call(f32[3,16,16,128]{3,2,1,0:T(8,128)} %x_hbm.1, bf16[160,256]{1,0:T(8,128)(2,1)} %constant.12.clone.wv_hbm, bf16[32,256]{1,0:T(8,128)(2,1)} %constant.13.clone.wp_hbm, bf16[256,128]{1,0:T(8,128)(2,1)} %constant.14.clone.la_hbm, bf16[256,128]{1,0:T(8,128)(2,1)} %constant.15.clone.lb_hbm), custom_call_target="tpu_custom_call" | custom-call | tf_op jit(solution)/shard_map/pallas_call | solution.py:556
  2.5 0.1 collective-permute-start
  2.5 1.2 %collective-permute-done = f32[120,128]{1,0:T(8,128)S(1)} collective-permute-done((f32[120,128]{1,0:T(8,128)S(1)}, f32[120,128]{1,0:T(8,128)S(1)}, u32[]{:S(2)}, u32[]{:S(2)}) %collective-permute-start) | collective-permute-done | bytes 61472 | tf_op jit(solution)/shard_map/ppermute | solution.py:589
  3.8 2.7 %collective-permute-start.1 = (f32[24,128]{1,0:T(8,128)S(1)}, f32[24,128]{1,0:T(8,128)S(1)}, u32[]{:S(2)}, u32[]{:S(2)}) collective-permute-start(f32[24,128]{1,0:T(8,128)S(1)} %get-tuple-element.10), channel_id=1, source_target_pairs={{0,9},{1,8},{8,17},{9,16},{16,25},{17,24},{24,1},{25,0},{2,11},{3,... | collective-permute-start | bytes 36872 | tf_op jit(solution)/shard_map/ppermute | solution.py:524
  6.5 2.1 %collective-permute-start.2 = (f32[24,128]{1,0:T(8,128)S(1)}, f32[24,128]{1,0:T(8,128)S(1)}, u32[]{:S(2)}, u32[]{:S(2)}) collective-permute-start(f32[24,128]{1,0:T(8,128)S(1)} %get-tuple-element.11), channel_id=1, source_target_pairs={{0,25},{1,24},{8,1},{9,0},{16,9},{17,8},{24,17},{25,16},{2,27},{3,... | collective-permute-start | bytes 36872 | tf_op jit(solution)/shard_map/ppermute | solution.py:524
  8.6 0.1 pad.1.clone
  8.7 1.2 %collective-permute-done.1 = f32[24,128]{1,0:T(8,128)S(1)} collective-permute-done((f32[24,128]{1,0:T(8,128)S(1)}, f32[24,128]{1,0:T(8,128)S(1)}, u32[]{:S(2)}, u32[]{:S(2)}) %collective-permute-start.1) | collective-permute-done | bytes 12320 | tf_op jit(solution)/shard_map/ppermute | solution.py:524
  9.9 0.0 collective-permute-done.2
  9.9 0.1 slice_add_fusion.own_ref
  10.0 1.5 %collective-permute-start.3 = (f32[72,128]{1,0:T(8,128)S(1)}, f32[72,128]{1,0:T(8,128)S(1)}, u32[]{:S(2)}, u32[]{:S(2)}) collective-permute-start(f32[72,128]{1,0:T(8,128)S(1)} %slice_add_fusion.own_ref), channel_id=1, source_target_pairs={{0,3},{1,4},{2,1},{3,6},{4,7},{5,0},{6,5},{7,2},{8,11},{9,12},{10,... | collective-permute-start | bytes 110600 | tf_op jit(solution)/shard_map/ppermute | solution.py:540
  11.5 1.2 %collective-permute-start.5 = (f32[72,128]{1,0:T(8,128)S(1)}, f32[72,128]{1,0:T(8,128)S(1)}, u32[]{:S(2)}, u32[]{:S(2)}) collective-permute-start(f32[72,128]{1,0:T(8,128)S(1)} %slice_add_fusion.own_ref), channel_id=1, source_target_pairs={{0,7},{1,6},{2,5},{3,4},{4,3},{5,2},{6,1},{7,0},{8,15},{9,14},{10,... | collective-permute-start | bytes 110600 | tf_op jit(solution)/shard_map/ppermute | solution.py:524
  12.7 0.7 %collective-permute-done.3.one_ref = f32[72,128]{1,0:T(8,128)S(1)} collective-permute-done((f32[72,128]{1,0:T(8,128)S(1)}, f32[72,128]{1,0:T(8,128)S(1)}, u32[]{:S(2)}, u32[]{:S(2)}) %collective-permute-start.3) | collective-permute-done | bytes 36896 | tf_op jit(solution)/shard_map/ppermute | solution.py:540
  13.4 0.2 collective-permute-start.4
  13.6 2.2 %collective-permute-done.5.both_ref = f32[72,128]{1,0:T(8,128)S(1)} collective-permute-done((f32[72,128]{1,0:T(8,128)S(1)}, f32[72,128]{1,0:T(8,128)S(1)}, u32[]{:S(2)}, u32[]{:S(2)}) %collective-permute-start.5) | collective-permute-done | bytes 36896 | tf_op jit(solution)/shard_map/ppermute | solution.py:524
  15.8 0.0 collective-permute-done.4.swap_ref
  15.8 0.6 %shard_map.69 = (f32[128,128]{1,0:T(8,128)S(1)}, f32[56,128]{1,0:T(8,128)S(1)}) custom-call(f32[72,128]{1,0:T(8,128)S(1)} %slice_add_fusion.own_ref, f32[72,128]{1,0:T(8,128)S(1)} %collective-permute-done.3.one_ref, f32[72,128]{1,0:T(8,128)S(1)} %collective-permute-done.4.swap_ref, f32[72,128]{1,0:T(8,128)S(1)} %collective-permute-done.5.both_ref), custom_call_target="tpu_custom_call" | custom-call | tf_op jit(solution)/shard_map/pallas_call | solution.py:556
  16.4 1.9 %collective-permute-start.6 = (f32[56,128]{1,0:T(8,128)S(1)}, f32[56,128]{1,0:T(8,128)S(1)}, u32[]{:S(2)}, u32[]{:S(2)}) collective-permute-start(f32[56,128]{1,0:T(8,128)S(1)} %get-tuple-element.6.own_ref), channel_id=1, source_target_pairs={{0,8},{1,17},{8,0},{9,25},{16,24},{17,1},{24,16},{25,9},{2,10},{3,... | collective-permute-start | bytes 86024 | tf_op jit(solution)/shard_map/ppermute | solution.py:540
  18.4 1.7 %collective-permute-start.8 = (f32[56,128]{1,0:T(8,128)S(1)}, f32[56,128]{1,0:T(8,128)S(1)}, u32[]{:S(2)}, u32[]{:S(2)}) collective-permute-start(f32[56,128]{1,0:T(8,128)S(1)} %get-tuple-element.6.own_ref), channel_id=1, source_target_pairs={{0,25},{1,24},{8,17},{9,16},{16,9},{17,8},{24,1},{25,0},{2,27},{3,... | collective-permute-start | bytes 86024 | tf_op jit(solution)/shard_map/ppermute | solution.py:524
  20.1 0.1 collective-permute-done.6.one_ref
  20.1 0.4 %collective-permute-start.7 = (f32[56,128]{1,0:T(8,128)S(1)}, f32[56,128]{1,0:T(8,128)S(1)}, u32[]{:S(2)}, u32[]{:S(2)}) collective-permute-start(f32[56,128]{1,0:T(8,128)S(1)} %collective-permute-done.6.one_ref), channel_id=1, source_target_pairs={{0,1},{1,0},{2,3},{3,2},{4,5},{5,4},{6,7},{7,6},{8,9},{9,8},{10,11... | collective-permute-start | bytes 86024 | tf_op jit(solution)/shard_map/ppermute | solution.py:541
  20.5 3.0 %collective-permute-done.8.both_ref = f32[56,128]{1,0:T(8,128)S(1)} collective-permute-done((f32[56,128]{1,0:T(8,128)S(1)}, f32[56,128]{1,0:T(8,128)S(1)}, u32[]{:S(2)}, u32[]{:S(2)}) %collective-permute-start.8) | collective-permute-done | bytes 28704 | tf_op jit(solution)/shard_map/ppermute | solution.py:524
  23.5 0.0 collective-permute-done.7.swap_ref
  23.5 2.7 %shard_map.70 = (f32[6,64]{1,0:T(8,128)}, f32[6,96]{1,0:T(8,128)}) custom-call(f32[56,128]{1,0:T(8,128)S(1)} %get-tuple-element.6.own_ref, f32[56,128]{1,0:T(8,128)S(1)} %collective-permute-done.6.one_ref, f32[56,128]{1,0:T(8,128)S(1)} %collective-permute-done.7.swap_ref, f32[56,128]{1,0:T(8,128)S(1)} %collective-permute-done.8.both_ref, ...), custom_call_target="tpu_custom_call" | custom-call | tf_op jit(solution)/shard_map/pallas_call | solution.py:556
  (5 shorter events, 0.0 us)
Async XLA Ops:
  2.5 1.3 %collective-permute-start = (f32[120,128]{1,0:T(8,128)S(1)}, f32[120,128]{1,0:T(8,128)S(1)}, u32[]{:S(2)}, u32[]{:S(2)}) collective-permute-start(f32[120,128]{1,0:T(8,128)S(1)} %shard_map.68), channel_id=1, source_target_pairs={{0,1},{1,0},{2,3},{3,2},{4,5},{5,4},{6,7},{7,6},{8,9},{9,8},{10,11... | collective-permute-start | bytes 184328 | tf_op jit(solution)/shard_map/ppermute | solution.py:589
  3.8 6.1 %collective-permute-start.1 = (f32[24,128]{1,0:T(8,128)S(1)}, f32[24,128]{1,0:T(8,128)S(1)}, u32[]{:S(2)}, u32[]{:S(2)}) collective-permute-start(f32[24,128]{1,0:T(8,128)S(1)} %get-tuple-element.10), channel_id=1, source_target_pairs={{0,9},{1,8},{8,17},{9,16},{16,25},{17,24},{24,1},{25,0},{2,11},{3,... | collective-permute-start | bytes 36872 | tf_op jit(solution)/shard_map/ppermute | solution.py:524
  6.5 3.4 %collective-permute-start.2 = (f32[24,128]{1,0:T(8,128)S(1)}, f32[24,128]{1,0:T(8,128)S(1)}, u32[]{:S(2)}, u32[]{:S(2)}) collective-permute-start(f32[24,128]{1,0:T(8,128)S(1)} %get-tuple-element.11), channel_id=1, source_target_pairs={{0,25},{1,24},{8,1},{9,0},{16,9},{17,8},{24,17},{25,16},{2,27},{3,... | collective-permute-start | bytes 36872 | tf_op jit(solution)/shard_map/ppermute | solution.py:524
  10.0 3.4 %collective-permute-start.3 = (f32[72,128]{1,0:T(8,128)S(1)}, f32[72,128]{1,0:T(8,128)S(1)}, u32[]{:S(2)}, u32[]{:S(2)}) collective-permute-start(f32[72,128]{1,0:T(8,128)S(1)} %slice_add_fusion.own_ref), channel_id=1, source_target_pairs={{0,3},{1,4},{2,1},{3,6},{4,7},{5,0},{6,5},{7,2},{8,11},{9,12},{10,... | collective-permute-start | bytes 110600 | tf_op jit(solution)/shard_map/ppermute | solution.py:540
  11.5 4.3 %collective-permute-start.5 = (f32[72,128]{1,0:T(8,128)S(1)}, f32[72,128]{1,0:T(8,128)S(1)}, u32[]{:S(2)}, u32[]{:S(2)}) collective-permute-start(f32[72,128]{1,0:T(8,128)S(1)} %slice_add_fusion.own_ref), channel_id=1, source_target_pairs={{0,7},{1,6},{2,5},{3,4},{4,3},{5,2},{6,1},{7,0},{8,15},{9,14},{10,... | collective-permute-start | bytes 110600 | tf_op jit(solution)/shard_map/ppermute | solution.py:524
  13.4 2.4 %collective-permute-start.4 = (f32[72,128]{1,0:T(8,128)S(1)}, f32[72,128]{1,0:T(8,128)S(1)}, u32[]{:S(2)}, u32[]{:S(2)}) collective-permute-start(f32[72,128]{1,0:T(8,128)S(1)} %collective-permute-done.3.one_ref), channel_id=1, source_target_pairs={{0,1},{1,0},{2,3},{3,2},{4,5},{5,4},{6,7},{7,6},{8,9},{9,8},{10,11... | collective-permute-start | bytes 110600 | tf_op jit(solution)/shard_map/ppermute | solution.py:541
  16.4 3.7 %collective-permute-start.6 = (f32[56,128]{1,0:T(8,128)S(1)}, f32[56,128]{1,0:T(8,128)S(1)}, u32[]{:S(2)}, u32[]{:S(2)}) collective-permute-start(f32[56,128]{1,0:T(8,128)S(1)} %get-tuple-element.6.own_ref), channel_id=1, source_target_pairs={{0,8},{1,17},{8,0},{9,25},{16,24},{17,1},{24,16},{25,9},{2,10},{3,... | collective-permute-start | bytes 86024 | tf_op jit(solution)/shard_map/ppermute | solution.py:540
  18.4 5.1 %collective-permute-start.8 = (f32[56,128]{1,0:T(8,128)S(1)}, f32[56,128]{1,0:T(8,128)S(1)}, u32[]{:S(2)}, u32[]{:S(2)}) collective-permute-start(f32[56,128]{1,0:T(8,128)S(1)} %get-tuple-element.6.own_ref), channel_id=1, source_target_pairs={{0,25},{1,24},{8,17},{9,16},{16,9},{17,8},{24,1},{25,0},{2,27},{3,... | collective-permute-start | bytes 86024 | tf_op jit(solution)/shard_map/ppermute | solution.py:524
  20.1 3.3 %collective-permute-start.7 = (f32[56,128]{1,0:T(8,128)S(1)}, f32[56,128]{1,0:T(8,128)S(1)}, u32[]{:S(2)}, u32[]{:S(2)}) collective-permute-start(f32[56,128]{1,0:T(8,128)S(1)} %collective-permute-done.6.one_ref), channel_id=1, source_target_pairs={{0,1},{1,0},{2,3},{3,2},{4,5},{5,4},{6,7},{7,6},{8,9},{9,8},{10,11... | collective-permute-start | bytes 86024 | tf_op jit(solution)/shard_map/ppermute | solution.py:541
